TPU v7x, 256 devices: a whole 4x4x8 slice. The times are simulated.
256 devices in a mesh: dp: 128 (over x, z_lo, y, core), tensor: 2 (over z_hi).
Axes of the slice: x: 4, y: 4, z: 8 (z_hi: 2, z_lo: 4; z = z_hi * 4 + z_lo), core: 2. Of those that a mesh axis runs over, the one named last changes fastest.
Arguments:
- tokens: bfloat16 [2, 256, 128, 1536], P(None, 'tensor', 'dp'), may hold values from -6 to 6
- cotangent: bfloat16 [2, 256, 128, 1536], P(None, 'tensor', 'dp'), may hold values from -6 to 6
- lengths: int32 [2, 256], replicated, may hold values from 1 to 128, 24576 in all within a row
- perm: int32 [2, 2, 128], replicated, may hold values from 0 to 127, each once within a row
- routes: int32 [2, 256, 128, 6], P(None, None, 'dp'), may hold values from 0 to 7, all different within a row
- gain_attn: float32 [1536], replicated, may hold values from 0.5 to 1.5
- gain_ffn: float32 [1536], replicated, may hold values from 0.5 to 1.5
- query_matrix: bfloat16 [1536, 1536], P('dp', 'tensor'), may hold values from -0.15625 to 0.15625
- key_matrix: bfloat16 [1536, 512], P('dp', 'tensor'), may hold values from -0.15625 to 0.15625
- value_matrix: bfloat16 [1536, 512], P('dp', 'tensor'), may hold values from -0.15625 to 0.15625
- w_out: bfloat16 [1536, 1536], P('tensor', 'dp'), may hold values from -0.875 to 0.875
- w_router: bfloat16 [1536, 8], replicated, may hold values from -0.078125 to 0.078125
- w_gate: bfloat16 [8, 1536, 512], P(None, 'dp', 'tensor'), may hold values from -0.15625 to 0.15625
- w_up: bfloat16 [8, 1536, 512], P(None, 'dp', 'tensor'), may hold values from -0.15625 to 0.15625
- w_down: bfloat16 [8, 512, 1536], P(None, 'tensor', 'dp'), may hold values from -0.75 to 0.75
- s_gate: bfloat16 [1536, 1024], P('dp', 'tensor'), may hold values from -0.15625 to 0.15625
- s_up: bfloat16 [1536, 1024], P('dp', 'tensor'), may hold values from -0.15625 to 0.15625
- s_down: bfloat16 [1024, 1536], P('tensor', 'dp'), may hold values from -0.25 to 0.25
Outputs:
- out_tokens: bfloat16 [2, 256, 128, 1536], P(None, 'tensor', 'dp')
- grad_tokens: bfloat16 [2, 256, 128, 1536], P(None, 'tensor', 'dp')
- grad_gain_attn: float32 [1536], replicated
- grad_gain_ffn: float32 [1536], replicated
- grad_query: float32 [1536, 1536], P('dp', 'tensor')
- grad_key: float32 [1536, 512], P('dp', 'tensor')
- grad_value: float32 [1536, 512], P('dp', 'tensor')
- grad_out: float32 [1536, 1536], P('tensor', 'dp')
- grad_router: float32 [1536, 8], replicated
- grad_gate: float32 [8, 1536, 512], P(None, 'dp', 'tensor')
- grad_up: float32 [8, 1536, 512], P(None, 'dp', 'tensor')
- grad_down: float32 [8, 512, 1536], P(None, 'tensor', 'dp')
- grad_sgate: float32 [1536, 1024], P('dp', 'tensor')
- grad_sup: float32 [1536, 1024], P('dp', 'tensor')
- grad_sdown: float32 [1024, 1536], P('tensor', 'dp')
Inputs may be any that keep to these rules, and one draw needn't show every extreme that they name: For each micro-batch m and half t, perm[m, t, :] names each of 0 .. 127 once. A token's 6 routes name different experts. The lengths of one micro-batch add up to 24576, and the longest equals 128.
All inputs are finite; a program needn't handle non-finite values.
Results may differ from a plain program's by a relative error of at most 0.02.
Values may be sent and summed in bfloat16 or wider, within the bound.
No kernel may reach another device: no remote copies, remote signals or barrier semaphores. Data moves between devices by JAX's collectives and lax.ppermute only.
A program may use at most 320 MiB of HBM per device.

v0:
```python
import math

import jax
import jax.numpy as jnp
from jax import lax
from jax.sharding import PartitionSpec as P

QUERY_HEAD_COUNT = 12
KEY_VALUE_HEADS = 4
HEAD_SIZE = 128
EXPERTS = 8
CAP = 128


EPS = 1e-06
HIGH = lax.Precision.HIGHEST


def joined_along(pieces, dim):
    pieces = jnp.moveaxis(pieces, 0, dim)
    lengths = pieces.shape
    return pieces.reshape(*lengths[:dim], lengths[dim] * lengths[dim + 1], *lengths[dim + 2 :])


def copy_for_each(shard, axis):
    devices = lax.axis_size(axis)
    return lax.all_to_all(
        jnp.broadcast_to(shard[None], (devices, *shard.shape)), axis, 0, 0, tiled=True
    )


def gather_directly(shard, axis, dim):
    return joined_along(copy_for_each(shard, axis), dim)


def rows_first(arrays, axis, dims):
    turned = [jnp.moveaxis(a, dim, 0) for a, dim in zip(arrays, dims)]
    widths = [t[0].size for t in turned]
    both = jnp.concatenate([t.reshape(-1, w) for t, w in zip(turned, widths)], axis=1)
    result = lax.all_gather(both, axis, axis=0, tiled=True)
    pieces = jnp.split(result, [sum(widths[:k]) for k in range(1, len(widths))], axis=1)
    return tuple(
        (
            jnp.moveaxis(b.reshape(-1, *t.shape[1:]), 0, dim)
            for b, t, dim in zip(pieces, turned, dims)
        )
    )


def in_blocks(shard, dim, devices):
    lengths = shard.shape
    pieces = shard.reshape(*lengths[:dim], devices, lengths[dim] // devices, *lengths[dim + 1 :])
    return jnp.moveaxis(pieces, dim, 0)


def one_scatter(arrays, axis, dims):
    devices = lax.axis_size(axis)
    pieces = [in_blocks(a, dim, devices) for a, dim in zip(arrays, dims)]
    lines = jnp.concatenate([b.reshape(devices, -1) for b in pieces], axis=1)
    extent = max(16, -(-lines.shape[1] // 1024) * 8)
    lines = jnp.pad(lines, ((0, 0), (0, extent * 128 - lines.shape[1]))).reshape(-1, 128)
    flat, at, finished = (lax.psum_scatter(lines, axis, tiled=True).reshape(-1), 0, [])
    for b in pieces:
        part = b[0]
        finished.append(flat[at : at + part.size].reshape(part.shape))
        at += part.size
    return tuple(finished)


def whole_rows(value_rows):
    return gather_directly(value_rows, "tensor", 0)


def rows_back(value_rows):
    return lax.psum_scatter(
        value_rows.astype(jnp.bfloat16), "tensor", scatter_dimension=0, tiled=True
    ).astype(jnp.float32)


def fetch_attention(query_matrix, key_matrix, value_matrix, w_out):
    return rows_first((query_matrix, key_matrix, value_matrix, w_out), "dp", (0, 0, 0, 1))


def fetch_ffn(w_gate, w_up, w_down, s_gate, s_up, s_down):
    return rows_first((w_gate, w_up, w_down, s_gate, s_up, s_down), "dp", (1, 1, 2, 0, 0, 1))


def reduce_grads(
    grad_query,
    grad_key,
    grad_value,
    grad_out,
    grad_gate,
    grad_up,
    grad_down,
    grad_sgate,
    grad_sup,
    grad_sdown,
):
    first = one_scatter(
        (grad_query, grad_key, grad_value, grad_sgate, grad_sup), "dp", (0, 0, 0, 0, 0)
    )
    second = one_scatter((grad_out, grad_gate, grad_up, grad_sdown), "dp", (1, 1, 1, 1))
    third = lax.psum_scatter(grad_down, "dp", scatter_dimension=2, tiled=True)
    return (
        first[0],
        first[1],
        first[2],
        second[0],
        second[1],
        second[2],
        third,
        first[3],
        first[4],
        second[3],
    )


def select_rows(block, index):
    return jnp.take(block, index, axis=0)


def silu_slope(value_rows):
    sigma = jax.nn.sigmoid(value_rows)
    return sigma * (1.0 + value_rows * (1.0 - sigma))


def attention_scores(query_rows, key, seq_len):
    scaled = jnp.einsum(
        "slkgd,smkd->skglm", query_rows, key, preferred_element_type=jnp.float32
    ) * (1.0 / math.sqrt(HEAD_SIZE))
    place = jnp.arange(seq_len, dtype=jnp.int32)
    return jnp.where(place[None, :] <= place[:, None], scaled, -1e30)


def slot_plan(route_rows, valid):
    experts_iota = jnp.arange(EXPERTS, dtype=jnp.int32)
    named = jnp.sum(
        (route_rows[:, :, None] == experts_iota[None, None, :]).astype(jnp.int32), axis=1
    )
    hits = named * valid[:, None].astype(jnp.int32)
    before = jnp.cumsum(hits, axis=0) - hits
    ranked = jnp.take_along_axis(before, route_rows, axis=1)
    kept = jnp.logical_and(valid[:, None], ranked < CAP)
    target = jnp.where(kept, route_rows * CAP + ranked, -1)
    return (kept, target)


def on_device(
    tokens,
    cotangent,
    lengths,
    perm,
    routes,
    gain_attn,
    gain_ffn,
    query_matrix,
    key_matrix,
    value_matrix,
    w_out,
    w_router,
    w_gate,
    w_up,
    w_down,
    s_gate,
    s_up,
    s_down,
):
    dp_count = lax.axis_size("dp")
    half_index = lax.axis_index("tensor")
    dp_index = lax.axis_index("dp")
    batches = tokens.shape[0]
    halves = perm.shape[1]
    seq_len = tokens.shape[2] * dp_count
    head_group = QUERY_HEAD_COUNT // KEY_VALUE_HEADS
    slot_count = EXPERTS * CAP
    order = lax.dynamic_index_in_dim(perm, half_index, 1, False)
    sent_tokens = jax.vmap(select_rows)(tokens, order)
    sent_cotangent = jax.vmap(select_rows)(cotangent, order)
    got_tokens, got_cotangent = (
        lax.all_to_all(sent_tokens, "dp", split_axis=1, concat_axis=2, tiled=True),
        lax.all_to_all(sent_cotangent, "dp", split_axis=1, concat_axis=2, tiled=True),
    )
    offsets = jnp.arange(halves, dtype=jnp.int32)[None, :, None] * dp_count
    pairs = jnp.transpose(perm + offsets, (0, 2, 1))
    route_pick = jax.vmap(select_rows)(routes, pairs.reshape(batches, -1))
    route_pick = route_pick.reshape(batches, dp_count, halves, routes.shape[2], routes.shape[3])
    got_routes = lax.all_to_all(route_pick, "dp", split_axis=1, concat_axis=3, tiled=True)
    own_pairs = lax.dynamic_index_in_dim(pairs, dp_index, 1, False)
    pair_lengths = jax.vmap(select_rows)(lengths, own_pairs)
    out_list = []
    grad_list = []
    total_big = None
    small_attn = jnp.zeros(gain_attn.shape, jnp.float32)
    small_ffn = jnp.zeros(gain_ffn.shape, jnp.float32)
    small_router = jnp.zeros(w_router.shape, jnp.float32)
    for batch in range(batches):
        x_rows = got_tokens[batch, 0].astype(jnp.float32)
        grad_rows = got_cotangent[batch, 0].astype(jnp.float32)
        route_rows = got_routes[batch, 0].reshape(-1, routes.shape[3])
        block_lengths = pair_lengths[batch]
        place = jnp.arange(seq_len, dtype=jnp.int32)
        valid = (place[None, :] < block_lengths[:, None]).reshape(-1)
        own_length = lax.dynamic_index_in_dim(block_lengths, half_index, 0, False)
        own_mask = (place < own_length).astype(jnp.float32)[:, None]
        query_w, key_w, value_w, out_w = fetch_attention(
            query_matrix, key_matrix, value_matrix, w_out
        )
        scale_attn = lax.rsqrt(jnp.mean(x_rows * x_rows, axis=-1, keepdims=True) + EPS)
        unit_attn = x_rows * scale_attn
        normed_input = whole_rows((unit_attn * gain_attn).astype(jnp.bfloat16))
        rows = normed_input.shape[0]
        query_rows = jnp.dot(normed_input, query_w, preferred_element_type=jnp.float32).astype(
            jnp.bfloat16
        )
        key = jnp.dot(normed_input, key_w, preferred_element_type=jnp.float32).astype(jnp.bfloat16)
        value_rows = jnp.dot(normed_input, value_w, preferred_element_type=jnp.float32).astype(
            jnp.bfloat16
        )
        heads_kv = key.shape[1] // HEAD_SIZE
        query_heads = query_rows.reshape(halves, seq_len, heads_kv, head_group, HEAD_SIZE)
        key_heads = key.reshape(halves, seq_len, heads_kv, HEAD_SIZE)
        value_heads = value_rows.reshape(halves, seq_len, heads_kv, HEAD_SIZE)
        scores = attention_scores(query_heads, key_heads, seq_len)
        log_total = jax.nn.logsumexp(scores, axis=-1, keepdims=True)
        probs_low = jnp.exp(scores - log_total).astype(jnp.bfloat16)
        mixed = jnp.einsum(
            "skglm,smkd->slkgd", probs_low, value_heads, preferred_element_type=jnp.float32
        )
        mixed = mixed.astype(jnp.bfloat16).reshape(rows, -1)
        hidden = x_rows + rows_back(jnp.dot(mixed, out_w, preferred_element_type=jnp.float32))
        scale_ffn = lax.rsqrt(jnp.mean(hidden * hidden, axis=-1, keepdims=True) + EPS)
        unit_ffn = hidden * scale_ffn
        normed_ffn = whole_rows((unit_ffn * gain_ffn).astype(jnp.bfloat16))
        gate_w, up_w, down_w, sgate_w, sup_w, sdown_w = fetch_ffn(
            w_gate, w_up, w_down, s_gate, s_up, s_down
        )
        logits = jnp.dot(normed_ffn, w_router, preferred_element_type=jnp.float32)
        gates = jax.nn.softmax(jnp.take_along_axis(logits, route_rows, axis=1), axis=-1)
        kept, target = slot_plan(route_rows, valid)
        slot_iota = jnp.arange(slot_count, dtype=jnp.int32)
        table = jnp.sum(
            (slot_iota[:, None, None] == target[None, :, :]).astype(jnp.bfloat16), axis=2
        )
        expert_in = jnp.dot(table, normed_ffn, preferred_element_type=jnp.float32).astype(
            jnp.bfloat16
        )
        expert_in = expert_in.reshape(EXPERTS, CAP, -1)
        gate_act = jnp.einsum("ecd,edf->ecf", expert_in, gate_w, preferred_element_type=jnp.float32)
        up_act = jnp.einsum("ecd,edf->ecf", expert_in, up_w, preferred_element_type=jnp.float32)
        inner = (jax.nn.silu(gate_act) * up_act).astype(jnp.bfloat16)
        expert_out = jnp.einsum(
            "ecf,efd->ecd", inner, down_w, preferred_element_type=jnp.float32
        ).reshape(slot_count, -1)
        safe_target = jnp.maximum(target, 0)
        kept_gates = jnp.where(kept, gates, 0.0)
        picked_out = jnp.take(expert_out, safe_target, axis=0)
        routed = jnp.sum(kept_gates[:, :, None] * picked_out, axis=1)
        shared_gate = jnp.dot(normed_ffn, sgate_w, preferred_element_type=jnp.float32)
        shared_up = jnp.dot(normed_ffn, sup_w, preferred_element_type=jnp.float32)
        shared_inner = (jax.nn.silu(shared_gate) * shared_up).astype(jnp.bfloat16)
        shared_out = jnp.dot(shared_inner, sdown_w, preferred_element_type=jnp.float32)
        branch = rows_back(routed + shared_out)
        out_list.append((own_mask * (hidden + branch)).astype(jnp.bfloat16))
        grad_own = own_mask * grad_rows
        grad_low = whole_rows(grad_own.astype(jnp.bfloat16))
        grad_full = grad_low.astype(jnp.float32)
        shared_grad = jnp.dot(grad_low, sdown_w.T, preferred_element_type=jnp.float32)
        grad_sgate_act = (shared_grad * shared_up * silu_slope(shared_gate)).astype(jnp.bfloat16)
        grad_sup_act = (shared_grad * jax.nn.silu(shared_gate)).astype(jnp.bfloat16)
        grad_normed = jnp.dot(grad_sgate_act, sgate_w.T, preferred_element_type=jnp.float32)
        grad_normed = grad_normed + jnp.dot(
            grad_sup_act, sup_w.T, preferred_element_type=jnp.float32
        )
        big_sdown = jnp.dot(shared_inner.T, grad_low, preferred_element_type=jnp.float32)
        big_sgate = jnp.dot(normed_ffn.T, grad_sgate_act, preferred_element_type=jnp.float32)
        big_sup = jnp.dot(normed_ffn.T, grad_sup_act, preferred_element_type=jnp.float32)
        row_iota = jnp.arange(rows, dtype=jnp.int32)
        drop_target = jnp.where(kept, target, slot_count)
        slot_row = (
            jnp.zeros((slot_count,), jnp.int32)
            .at[drop_target]
            .set(jnp.broadcast_to(row_iota[:, None], target.shape), mode="drop")
        )
        slot_gate = jnp.zeros((slot_count,), jnp.float32).at[drop_target].set(gates, mode="drop")
        grad_expert = (slot_gate[:, None] * jnp.take(grad_full, slot_row, axis=0)).astype(
            jnp.bfloat16
        )
        grad_expert = grad_expert.reshape(EXPERTS, CAP, -1)
        grad_inner = jnp.einsum(
            "ecd,efd->ecf", grad_expert, down_w, preferred_element_type=jnp.float32
        )
        big_down = jnp.einsum(
            "ecf,ecd->efd", inner, grad_expert, preferred_element_type=jnp.float32
        )
        grad_gate_act = (grad_inner * up_act * silu_slope(gate_act)).astype(jnp.bfloat16)
        grad_up_act = (grad_inner * jax.nn.silu(gate_act)).astype(jnp.bfloat16)
        grad_in = jnp.einsum(
            "ecf,edf->ecd", grad_gate_act, gate_w, preferred_element_type=jnp.float32
        )
        grad_in = grad_in + jnp.einsum(
            "ecf,edf->ecd", grad_up_act, up_w, preferred_element_type=jnp.float32
        )
        grad_in = grad_in.reshape(slot_count, -1)
        big_gate = jnp.einsum(
            "ecd,ecf->edf", expert_in, grad_gate_act, preferred_element_type=jnp.float32
        )
        big_up = jnp.einsum(
            "ecd,ecf->edf", expert_in, grad_up_act, preferred_element_type=jnp.float32
        )
        grad_normed = grad_normed + jnp.sum(
            kept.astype(jnp.float32)[:, :, None] * jnp.take(grad_in, safe_target, axis=0), axis=1
        )
        grad_gates = jnp.where(kept, jnp.sum(grad_full[:, None, :] * picked_out, axis=-1), 0.0)
        grad_chosen = gates * (grad_gates - jnp.sum(gates * grad_gates, axis=-1, keepdims=True))
        experts_iota = jnp.arange(EXPERTS, dtype=jnp.int32)
        grad_logits = jnp.sum(
            (route_rows[:, :, None] == experts_iota[None, None, :]).astype(jnp.float32)
            * grad_chosen[:, :, None],
            axis=1,
        )
        small_router = small_router + jnp.dot(
            normed_ffn.astype(jnp.float32).T, grad_logits, precision=HIGH
        )
        grad_normed = grad_normed + jnp.dot(
            grad_logits, w_router.astype(jnp.float32).T, precision=HIGH
        )
        grad_ffn_own = rows_back(grad_normed)
        small_ffn = small_ffn + jnp.sum(grad_ffn_own * unit_ffn, axis=0)
        scaled_ffn = grad_ffn_own * gain_ffn
        grad_hidden = grad_own + scale_ffn * (
            scaled_ffn - unit_ffn * jnp.mean(scaled_ffn * unit_ffn, axis=-1, keepdims=True)
        )
        grad_attn = whole_rows(grad_hidden.astype(jnp.bfloat16))
        grad_mixed = jnp.dot(grad_attn, out_w.T, preferred_element_type=jnp.float32).astype(
            jnp.bfloat16
        )
        big_out = jnp.dot(mixed.T, grad_attn, preferred_element_type=jnp.float32)
        grad_mixed_heads = grad_mixed.reshape(halves, seq_len, heads_kv, head_group, HEAD_SIZE)
        probs = jnp.exp(attention_scores(query_heads, key_heads, seq_len) - log_total)
        probs_again = probs.astype(jnp.bfloat16)
        grad_probs = jnp.einsum(
            "slkgd,smkd->skglm", grad_mixed_heads, value_heads, preferred_element_type=jnp.float32
        )
        grad_scores = (
            probs * (grad_probs - jnp.sum(probs * grad_probs, axis=-1, keepdims=True))
        ).astype(jnp.bfloat16)
        inverse_root = 1.0 / math.sqrt(HEAD_SIZE)
        grad_query = (
            (
                jnp.einsum(
                    "skglm,smkd->slkgd", grad_scores, key_heads, preferred_element_type=jnp.float32
                )
                * inverse_root
            )
            .astype(jnp.bfloat16)
            .reshape(rows, -1)
        )
        grad_key = (
            (
                jnp.einsum(
                    "skglm,slkgd->smkd",
                    grad_scores,
                    query_heads,
                    preferred_element_type=jnp.float32,
                )
                * inverse_root
            )
            .astype(jnp.bfloat16)
            .reshape(rows, -1)
        )
        grad_value = (
            jnp.einsum(
                "skglm,slkgd->smkd",
                probs_again,
                grad_mixed_heads,
                preferred_element_type=jnp.float32,
            )
            .astype(jnp.bfloat16)
            .reshape(rows, -1)
        )
        grad_normed_attn = jnp.dot(grad_query, query_w.T, preferred_element_type=jnp.float32)
        grad_normed_attn = grad_normed_attn + jnp.dot(
            grad_key, key_w.T, preferred_element_type=jnp.float32
        )
        grad_normed_attn = grad_normed_attn + jnp.dot(
            grad_value, value_w.T, preferred_element_type=jnp.float32
        )
        big_query = jnp.dot(normed_input.T, grad_query, preferred_element_type=jnp.float32)
        big_key = jnp.dot(normed_input.T, grad_key, preferred_element_type=jnp.float32)
        big_value = jnp.dot(normed_input.T, grad_value, preferred_element_type=jnp.float32)
        grad_attn_own = rows_back(grad_normed_attn)
        small_attn = small_attn + jnp.sum(grad_attn_own * unit_attn, axis=0)
        scaled_attn = grad_attn_own * gain_attn
        grad_x = grad_hidden + scale_attn * (
            scaled_attn - unit_attn * jnp.mean(scaled_attn * unit_attn, axis=-1, keepdims=True)
        )
        grad_list.append(grad_x.astype(jnp.bfloat16))
        big = (
            big_query,
            big_key,
            big_value,
            big_out,
            big_gate,
            big_up,
            big_down,
            big_sgate,
            big_sup,
            big_sdown,
        )
        total_big = (
            big if total_big is None else tuple((old + new for old, new in zip(total_big, big)))
        )
    total_big = reduce_grads(*total_big)
    final_attn, final_ffn, final_router = lax.psum(
        (small_attn, small_ffn, small_router), ("dp", "tensor")
    )
    out_stack = jnp.stack(out_list)[:, None]
    grad_stack = jnp.stack(grad_list)[:, None]
    back_out, back_grad = (
        lax.all_to_all(out_stack, "dp", split_axis=2, concat_axis=1, tiled=True),
        lax.all_to_all(grad_stack, "dp", split_axis=2, concat_axis=1, tiled=True),
    )
    inverse = jnp.argsort(order, axis=1)
    out_tokens = jax.vmap(select_rows)(back_out, inverse)
    grad_tokens = jax.vmap(select_rows)(back_grad, inverse)
    return (
        out_tokens,
        grad_tokens,
        final_attn,
        final_ffn,
        total_big[0],
        total_big[1],
        total_big[2],
        total_big[3],
        final_router,
        total_big[4],
        total_big[5],
        total_big[6],
        total_big[7],
        total_big[8],
        total_big[9],
    )


def solution(mesh):
    return jax.shard_map(
        on_device,
        mesh=mesh,
        in_specs=(
            P(None, "tensor", "dp", None),
            P(None, "tensor", "dp", None),
            P(),
            P(),
            P(None, None, "dp", None),
            P(),
            P(),
            P("dp", "tensor"),
            P("dp", "tensor"),
            P("dp", "tensor"),
            P("tensor", "dp"),
            P(),
            P(None, "dp", "tensor"),
            P(None, "dp", "tensor"),
            P(None, "tensor", "dp"),
            P("dp", "tensor"),
            P("dp", "tensor"),
            P("tensor", "dp"),
        ),
        out_specs=(
            P(None, "tensor", "dp", None),
            P(None, "tensor", "dp", None),
            P(),
            P(),
            P("dp", "tensor"),
            P("dp", "tensor"),
            P("dp", "tensor"),
            P("tensor", "dp"),
            P(),
            P(None, "dp", "tensor"),
            P(None, "dp", "tensor"),
            P(None, "tensor", "dp"),
            P("dp", "tensor"),
            P("dp", "tensor"),
            P("tensor", "dp"),
        ),
        check_vma=False,
    )
```

profile of v0, /device:TPU:1, one launch (start us, length us, event | category | flops | bytes accessed | tf_op | source)
XLA Modules:
  0.0 2964.3 jit_solution(14631701834171605317)
XLA Ops:
  24.2 38.1 %all_to_all.97 = bf16[2,128,1,1536]{3,0,2,1:T(2,128)(2,1)S(1)} all-to-all(bf16[2,128,1,1536]{3,0,2,1:T(2,128)(2,1)S(1)} %get-tuple-element.234), channel_id=1, replica_groups=mesh['dp'=128,'tensor'=2] {'dp'}, dimensions={1} | all-to-all | bytes 1572864 | tf_op jit(solution)/shard_map/all_to_all | solution.py:181
  71.4 169.4 %all-gather.5.cloned.1.call-done = bf16[128,12,2048]{2,1,0:T(8,128)(2,1)} async-done(((bf16[1,12,2048]{2,1,0:T(8,128)(2,1)}), bf16[128,12,2048]{2,1,0:T(8,128)(2,1)}) %all-gather.5.cloned.1.call-update) | async-done | bytes 6291472 | tf_op jit(solution)/shard_map/all_gather | solution.py:40
  240.8 10.7 reshape.962
  270.2 8.3 all-to-all-start.2
  281.6 23.8 all-to-all-done.2
  305.4 7.4 all-to-all-start.7
  314.9 9.5 gather_fusion.3
  324.7 16.5 all-to-all-done.7
  353.1 27.7 all-to-all-done.8
  402.0 13.1 all-to-all-done.3
  415.5 9.6 gather_fusion.4
  440.0 126.2 %all-gather.7.cloned.1.call-done = bf16[128,12,7680]{2,1,0:T(8,128)(2,1)} async-done(((bf16[1,12,7680]{2,1,0:T(8,128)(2,1)}), bf16[128,12,7680]{2,1,0:T(8,128)(2,1)}) %all-gather.7.cloned.1.call-update) | async-done | bytes 23592976 | tf_op jit(solution)/shard_map/all_gather | solution.py:40
  566.2 32.0 %reshape.964 = bf16[1536,7680]{1,0:T(8,128)(2,1)} reshape(bf16[128,12,7680]{2,1,0:T(8,128)(2,1)} %all-gather.7.cloned.1.call-done) | data formatting | bytes 47185920
  598.2 13.9 fusion.240
  617.6 8.7 copy.811
  626.3 8.6 copy.809
  634.9 8.7 copy.810
  643.6 8.7 copy.807
  652.3 8.6 copy.808
  676.3 13.1 gather_fusion.5
  689.4 11.4 reshape.984
  705.8 7.6 fusion.22
  713.4 13.3 gather_fusion.12
  726.8 11.6 reshape.1016
  744.8 17.2 multiply_reduce_fusion.1
  767.1 34.1 %reduce-scatter.18.cloned.1.call-done = bf16[128,1536]{1,0:T(8,128)(2,1)} async-done(((bf16[256,1536]{1,0:T(8,128)(2,1)}), bf16[128,1536]{1,0:T(8,128)(2,1)}) %reduce-scatter.18.cloned.1.call-update) | async-done | bytes 393232 | tf_op jit(solution)/shard_map/reduce_scatter | solution.py:75
  811.5 16.3 all-to-all-done.9
  843.0 9.5 gather_fusion.6
  853.0 24.0 reduce-scatter.20.cloned.1.call-done
  883.6 18.4 all-to-all-done.4
  923.7 6.5 scatter_custom_fusion.3
  953.2 8.6 fusion.256
  964.3 32.8 %reduce-scatter.12.cloned.1.call-done = bf16[128,1536]{1,0:T(8,128)(2,1)} async-done(((bf16[256,1536]{1,0:T(8,128)(2,1)}), bf16[128,1536]{1,0:T(8,128)(2,1)}) %reduce-scatter.12.cloned.1.call-update) | async-done | bytes 393232 | tf_op jit(solution)/shard_map/reduce_scatter | solution.py:75
  1004.6 8.3 fusion.255
  1014.6 8.5 all-to-all-done.5
  1028.9 9.5 gather_fusion.7
  1066.0 13.2 gather_fusion.8
  1079.1 11.5 reshape.998
  1095.7 7.6 fusion.25
  1103.3 13.1 gather_fusion.14
  1116.4 11.9 reshape.1022
  1134.9 17.2 multiply_reduce_fusion
  1183.8 10.1 reduce-scatter.22.cloned.1.call-done
  1201.9 12.0 convolution_add_fusion.1
  1213.8 6.5 all-to-all-done.11
  1260.2 14.5 copy.882
  1274.8 12.9 copy.883
  1287.6 7.4 convolution_add_fusion.2
  1295.0 17.6 copy.878
  1312.6 12.9 copy.879
  1365.0 6.4 reshape.726
  1371.4 6.7 copy.875
  1378.1 6.6 reshape.727
  1387.4 29.5 pad_maximum_fusion
  1422.1 12.9 reshape.722
  1435.0 33.3 %copy.886 = f32[128,64512]{1,0:T(8,128)} copy(f32[128,64512]{0,1:T(8,128)} %pad_maximum_fusion) | data formatting | bytes 66060288 | tf_op jit(solution)/shard_map/concatenate | solution.py:59
  1468.3 27.9 reshape.734
  1497.2 8.4 fusion.259
  1505.7 6.7 convolution_add_fusion
  1512.4 17.4 copy.889
  1538.8 12.7 all-to-all-start.12
  1554.5 32.3 %all-to-all-done.12 = bf16[2,1,128,1536]{3,0,1,2:T(2,128)(2,1)S(1)} async-done(((bf16[2,1,128,1536]{3,0,1,2:T(2,128)(2,1)}), bf16[2,1,128,1536]{3,0,1,2:T(2,128)(2,1)S(1)}, u32[]{:S(2)}, u32[]{:S(2)}) %all-to-all-start.12) | async-done | bytes 786464 | tf_op jit(solution)/shard_map/all_to_all | solution.py:422
  1598.0 82.6 %all-reduce.2 = (f32[1536]{0:T(1024)}, f32[1536]{0:T(1024)}, f32[1536,8]{0,1:T(8,128)}) all-reduce(f32[1536]{0:T(1024)S(1)} %add.359, f32[1536]{0:T(1024)S(1)} %add.360, f32[1536,8]{0,1:T(8,128)S(1)} %convolution_add_fusion.20), channel_id=1, replica_groups=mesh['dp'=128,'tensor'=2] {'dp','tensor'}, use_global_device_ids=true, to_apply=%region_51.57 | all-reduce | flops 15360 | bytes 122880 | tf_op jit(solution)/shard_map/psum | solution.py:415
  1689.3 1255.4 %all-reduce.6.cloned.1.call-done = (f32[27648,128]{1,0:T(8,128)}, f32[64512,128]{1,0:T(8,128)}) async-done(((f32[27648,128]{1,0:T(8,128)}, f32[64512,128]{1,0:T(8,128)}), (f32[27648,128]{1,0:T(8,128)}, f32[64512,128]{1,0:T(8,128)})) %all-reduce.6.cloned.1.call-update) | async-done | bytes 47185936
  (732 shorter events, 436.4 us)
Async XLA Ops:
  10.0 230.8 %all-gather.5.cloned.1.call-start = ((), (), s32[]{:S(2)}) async-start(), calls=%async_computation.31 | async-start | bytes 8454144 | tf_op jit(solution)/shard_map/all_gather | solution.py:40
  19.3 45.1 %copy-start.112 = (f32[1536]{0:T(1024)S(1)}, f32[1536]{0:T(1024)}, u32[]{:S(2)}) copy-start(f32[1536]{0:T(1024)} %param.33) | copy-start | bytes 18436
  64.4 287.5 %copy-start.21 = (bf16[128,1536]{1,0:T(8,128)(2,1)}, bf16[128,1536]{1,0:T(8,128)(2,1)S(1)}, u32[]{:S(2)}) copy-start(bf16[128,1536]{1,0:T(8,128)(2,1)S(1)} %get-tuple-element.186) | copy-start | bytes 1179652
  65.6 185.9 %all-to-all-start.1 = ((bf16[2,128,1536]{2,1,0:T(8,128)(2,1)}), bf16[2,128,1536]{2,1,0:T(8,128)(2,1)S(1)}, u32[]{:S(2)}, u32[]{:S(2)}) async-start(bf16[2,128,1536]{2,1,0:T(8,128)(2,1)} %broadcast_in_dim.105), calls=%async_computation.1 | async-start | bytes 1572864 | tf_op jit(solution)/shard_map/all_to_all | solution.py:27
  71.1 279.6 %reduce-scatter.10.cloned.1.call-start = ((), (), s32[]{:S(2)}) async-start(), calls=%async_computation.22 | async-start | bytes 1179648 | tf_op jit(solution)/shard_map/reduce_scatter | solution.py:75
  71.4 186.7 %copy-start.121 = (pred[128,128]{0,1:T(8,128)(4,1)}, pred[128,128]{0,1:T(8,128)(4,1)S(1)}, u32[]{:S(2)}) copy-start(pred[128,128]{0,1:T(8,128)(4,1)S(1)} %iota_compare_fusion.2) | copy-start | bytes 49156
  263.6 302.6 %all-gather.7.cloned.1.call-start = ((), (), s32[]{:S(2)}) async-start(), calls=%async_computation.32 | async-start | bytes 31703040 | tf_op jit(solution)/shard_map/all_gather | solution.py:40
  270.2 35.2 %all-to-all-start.2 = ((s32[2,128,2,1,6]{4,2,3,0,1:T(2,128)}), s32[2,128,2,1,6]{4,2,3,0,1:T(2,128)S(1)}, u32[]{:S(2)}, u32[]{:S(2)}) async-start(s32[2,128,2,1,6]{4,2,3,0,1:T(2,128)} %copy_select_fusion), calls=%async_computation.3 | async-start | bytes 524288 | tf_op jit(solution)/shard_map/all_to_all | solution.py:188
  281.4 61.8 %copy-start.162 = (f32[128]{0:T(128)}, f32[128]{0:T(128)S(1)}, u32[]{:S(2)}) copy-start(f32[128]{0:T(128)S(1)} %compare_convert_fusion.1) | copy-start | bytes 1540
  281.5 106.1 %copy-start.155 = (s32[1536]{0:T(1024)}, s32[1536]{0:T(1024)S(1)}, u32[]{:S(2)}) copy-start(s32[1536]{0:T(1024)S(1)} %reshape.877) | copy-start | bytes 18436
  305.4 35.8 %all-to-all-start.7 = ((bf16[2,128,1,1536]{3,0,2,1:T(2,128)(2,1)}), bf16[2,128,1,1536]{3,0,2,1:T(2,128)(2,1)S(1)}, u32[]{:S(2)}, u32[]{:S(2)}) async-start(bf16[2,128,1,1536]{3,0,2,1:T(2,128)(2,1)} %get-tuple-element.233), calls=%async_computation.11 | async-start | bytes 1572864 | tf_op jit(solution)/shard_map/all_to_all | solution.py:182
  324.7 100.7 %copy-start.134 = (pred[256,6]{0,1:T(8,128)(4,1)}, pred[256,6]{0,1:T(8,128)(4,1)S(1)}, u32[]{:S(2)}) copy-start(pred[256,6]{0,1:T(8,128)(4,1)S(1)} %get-tuple-element.179) | copy-start | bytes 4612
  345.2 35.7 %all-to-all-start.8 = ((bf16[2,128,1536]{2,1,0:T(8,128)(2,1)}), bf16[2,128,1536]{2,1,0:T(8,128)(2,1)S(1)}, u32[]{:S(2)}, u32[]{:S(2)}) async-start(bf16[2,128,1536]{2,1,0:T(8,128)(2,1)} %broadcast_in_dim.116), calls=%async_computation.12 | async-start | bytes 1572864 | tf_op jit(solution)/shard_map/all_to_all | solution.py:27
  352.0 50.1 %copy-start.149 = (f32[128]{0:T(128)}, f32[128]{0:T(128)S(1)}, u32[]{:S(2)}) copy-start(f32[128]{0:T(128)S(1)} %add_rsqrt_fusion.2) | copy-start | bytes 1540
  381.9 33.3 %all-to-all-start.3 = ((bf16[2,128,1536]{2,1,0:T(8,128)(2,1)}), bf16[2,128,1536]{2,1,0:T(8,128)(2,1)S(1)}, u32[]{:S(2)}, u32[]{:S(2)}) async-start(bf16[2,128,1536]{2,1,0:T(8,128)(2,1)} %broadcast_in_dim.110), calls=%async_computation.4 | async-start | bytes 1572864 | tf_op jit(solution)/shard_map/all_to_all | solution.py:27
  385.4 415.8 %reduce-scatter.18.cloned.1.call-start = ((), (), s32[]{:S(2)}) async-start(), calls=%async_computation.26 | async-start | bytes 1179648 | tf_op jit(solution)/shard_map/reduce_scatter | solution.py:75
  415.2 199.7 %copy-start.10 = (bf16[2,128,1536]{2,1,0:T(8,128)(2,1)}, bf16[2,128,1536]{2,1,0:T(8,128)(2,1)S(1)}, u32[]{:S(2)}) copy-start(bf16[2,128,1536]{2,1,0:T(8,128)(2,1)S(1)} %all-to-all-done.3) | copy-start | bytes 2359300
  672.3 33.4 %copy-start.73 = (bf16[8,128,256]{2,1,0:T(8,128)(2,1)}, bf16[8,128,256]{2,1,0:T(8,128)(2,1)S(1)}, u32[]{:S(2)}) copy-start(bf16[8,128,256]{2,1,0:T(8,128)(2,1)S(1)} %get-tuple-element.211) | copy-start | bytes 1572868
  762.0 39.2 %copy-start.22 = (bf16[128,1536]{1,0:T(8,128)(2,1)S(1)}, bf16[128,1536]{1,0:T(8,128)(2,1)}, u32[]{:S(2)}) copy-start(bf16[128,1536]{1,0:T(8,128)(2,1)} %copy-done.21) | copy-start | bytes 1179652
  762.0 39.2 %copy-start.42 = (bf16[128,1536]{1,0:T(8,128)(2,1)S(1)}, bf16[128,1536]{1,0:T(8,128)(2,1)}, u32[]{:S(2)}) copy-start(bf16[128,1536]{1,0:T(8,128)(2,1)} %reduce-scatter.10.cloned.1.call-done) | copy-start | bytes 1179652
  762.0 39.2 %copy-start.104 = (f32[1536]{0:T(1024)S(1)}, f32[1536]{0:T(1024)}, u32[]{:S(2)}) copy-start(f32[1536]{0:T(1024)} %param.34) | copy-start | bytes 18436
  762.0 39.2 %copy-start.150 = (f32[128]{0:T(128)S(1)}, f32[128]{0:T(128)}, u32[]{:S(2)}) copy-start(f32[128]{0:T(128)} %copy-done.149) | copy-start | bytes 1540
  762.0 41.2 %copy-start.36 = (bf16[1,128,1,1536]{3,0,2,1:T(2,128)(2,1)S(1)}, bf16[1,128,1,1536]{3,0,2,1:T(2,128)(2,1)}, u32[]{:S(2)}) copy-start(bf16[1,128,1,1536]{3,0,2,1:T(2,128)(2,1)} %copy-done.35) | copy-start | bytes 1179652
  762.0 41.2 %copy-start.163 = (f32[128]{0:T(128)S(1)}, f32[128]{0:T(128)}, u32[]{:S(2)}) copy-start(f32[128]{0:T(128)} %copy-done.162) | copy-start | bytes 1540
  762.2 41.0 %copy-start.127 = (f32[256,8]{0,1:T(8,128)}, f32[256,8]{0,1:T(8,128)S(1)}, u32[]{:S(2)}) copy-start(f32[256,8]{0,1:T(8,128)S(1)} %select_reduce_fusion.1) | copy-start | bytes 24580
  765.3 45.4 %copy-start.102 = (s32[1,1,2,128,1,6]{5,2,0,3,4,1:T(2,128)S(1)}, s32[1,1,2,128,1,6]{5,2,0,3,4,1:T(2,128)}, u32[]{:S(2)}) copy-start(s32[1,1,2,128,1,6]{5,2,0,3,4,1:T(2,128)} %get-tuple-element.232) | copy-start | bytes 18436
  805.6 22.1 all-to-all-start.9
  809.1 67.9 %reduce-scatter.20.cloned.1.call-start = ((), (), s32[]{:S(2)}) async-start(), calls=%async_computation.27 | async-start | bytes 1179648 | tf_op jit(solution)/shard_map/reduce_scatter | solution.py:75
  842.9 34.1 %copy-start.113 = (f32[1536]{0:T(1024)S(1)}, f32[1536]{0:T(1024)}, u32[]{:S(2)}) copy-start(f32[1536]{0:T(1024)} %param.33) | copy-start | bytes 18436
  842.9 34.1 %copy-start.159 = (f32[128]{0:T(128)S(1)}, f32[128]{0:T(128)}, u32[]{:S(2)}) copy-start(f32[128]{0:T(128)} %copy-done.158) | copy-start | bytes 1540
  842.9 40.5 %copy-start.160 = (f32[128]{0:T(128)S(1)}, f32[128]{0:T(128)}, u32[]{:S(2)}) copy-start(f32[128]{0:T(128)} %compare_convert_fusion) | copy-start | bytes 1540
  852.8 186.0 %copy-start.133 = (pred[256,6]{0,1:T(8,128)(4,1)}, pred[256,6]{0,1:T(8,128)(4,1)S(1)}, u32[]{:S(2)}) copy-start(pred[256,6]{0,1:T(8,128)(4,1)S(1)} %get-tuple-element.190) | copy-start | bytes 4612
  853.0 144.1 %copy-start.23 = (bf16[128,1536]{1,0:T(8,128)(2,1)}, bf16[128,1536]{1,0:T(8,128)(2,1)S(1)}, u32[]{:S(2)}) copy-start(bf16[128,1536]{1,0:T(8,128)(2,1)S(1)} %get-tuple-element.197) | copy-start | bytes 1179652
  853.0 53.8 %copy-start.156 = (f32[128]{0:T(128)}, f32[128]{0:T(128)S(1)}, u32[]{:S(2)}) copy-start(f32[128]{0:T(128)S(1)} %add_rsqrt_fusion.1) | copy-start | bytes 1540
  879.9 22.1 all-to-all-start.4
  903.0 30.7 %all-to-all-start.10 = ((bf16[2,128,1536]{2,1,0:T(8,128)(2,1)}), bf16[2,128,1536]{2,1,0:T(8,128)(2,1)S(1)}, u32[]{:S(2)}, u32[]{:S(2)}) async-start(bf16[2,128,1536]{2,1,0:T(8,128)(2,1)} %broadcast_in_dim.121), calls=%async_computation.16 | async-start | bytes 1572864 | tf_op jit(solution)/shard_map/all_to_all | solution.py:27
  906.7 56.3 %reduce-scatter.14.cloned.1.call-start = ((), (), s32[]{:S(2)}) async-start(), calls=%async_computation.24 | async-start | bytes 1179648 | tf_op jit(solution)/shard_map/reduce_scatter | solution.py:75
  923.3 73.7 %reduce-scatter.12.cloned.1.call-start = ((), (), s32[]{:S(2)}) async-start(), calls=%async_computation.23 | async-start | bytes 1179648 | tf_op jit(solution)/shard_map/reduce_scatter | solution.py:75
  953.2 43.9 %copy-start.37 = (bf16[1,128,1,1536]{3,0,2,1:T(2,128)(2,1)S(1)}, bf16[1,128,1,1536]{3,0,2,1:T(2,128)(2,1)}, u32[]{:S(2)}) copy-start(bf16[1,128,1,1536]{3,0,2,1:T(2,128)(2,1)} %copy-done.35) | copy-start | bytes 1179652
  953.2 43.9 %copy-start.43 = (bf16[128,1536]{1,0:T(8,128)(2,1)S(1)}, bf16[128,1536]{1,0:T(8,128)(2,1)}, u32[]{:S(2)}) copy-start(bf16[128,1536]{1,0:T(8,128)(2,1)} %reduce-scatter.10.cloned.1.call-done) | copy-start | bytes 1179652
  953.2 43.9 %copy-start.53 = (bf16[128,1536]{1,0:T(8,128)(2,1)S(1)}, bf16[128,1536]{1,0:T(8,128)(2,1)}, u32[]{:S(2)}) copy-start(bf16[128,1536]{1,0:T(8,128)(2,1)} %reduce-scatter.18.cloned.1.call-done) | copy-start | bytes 1179652
  953.2 43.9 %copy-start.151 = (f32[128]{0:T(128)S(1)}, f32[128]{0:T(128)}, u32[]{:S(2)}) copy-start(f32[128]{0:T(128)} %copy-done.149) | copy-start | bytes 1540
  953.2 43.9 %copy-start.164 = (f32[128]{0:T(128)S(1)}, f32[128]{0:T(128)}, u32[]{:S(2)}) copy-start(f32[128]{0:T(128)} %copy-done.162) | copy-start | bytes 1540
  953.2 43.9 %copy-start.167 = (f32[128]{0:T(128)S(1)}, f32[128]{0:T(128)}, u32[]{:S(2)}) copy-start(f32[128]{0:T(128)} %copy-done.166) | copy-start | bytes 1540
  961.8 42.8 %copy-start.74 = (bf16[8,128,256]{2,1,0:T(8,128)(2,1)S(1)}, bf16[8,128,256]{2,1,0:T(8,128)(2,1)}, u32[]{:S(2)}) copy-start(bf16[8,128,256]{2,1,0:T(8,128)(2,1)} %copy-done.73) | copy-start | bytes 1572868
  964.3 48.7 %copy-start.152 = (f32[128]{0:T(128)}, f32[128]{0:T(128)S(1)}, u32[]{:S(2)}) copy-start(f32[128]{0:T(128)S(1)} %add_rsqrt_fusion) | copy-start | bytes 1540
  1001.0 22.1 all-to-all-start.5
  1004.5 189.4 %reduce-scatter.22.cloned.1.call-start = ((), (), s32[]{:S(2)}) async-start(), calls=%async_computation.28 | async-start | bytes 1179648 | tf_op jit(solution)/shard_map/reduce_scatter | solution.py:75
  1023.1 151.4 %copy-start.13 = (bf16[2,128,1536]{2,1,0:T(8,128)(2,1)}, bf16[2,128,1536]{2,1,0:T(8,128)(2,1)S(1)}, u32[]{:S(2)}) copy-start(bf16[2,128,1536]{2,1,0:T(8,128)(2,1)S(1)} %all-to-all-done.5) | copy-start | bytes 2359300
  1061.8 33.9 %copy-start.69 = (bf16[8,128,256]{2,1,0:T(8,128)(2,1)}, bf16[8,128,256]{2,1,0:T(8,128)(2,1)S(1)}, u32[]{:S(2)}) copy-start(bf16[8,128,256]{2,1,0:T(8,128)(2,1)S(1)} %get-tuple-element.214) | copy-start | bytes 1572868
  1198.2 22.1 all-to-all-start.11
  1201.8 328.1 %reduce-scatter.24.cloned.1.call-start = ((), (), s32[]{:S(2)}) async-start(), calls=%async_computation.29 | async-start | bytes 1179648 | tf_op jit(solution)/shard_map/reduce_scatter | solution.py:75
  1237.2 296.0 %reduce-scatter.16.cloned.1.call-start = ((), (), s32[]{:S(2)}) async-start(), calls=%async_computation.25 | async-start | bytes 1179648 | tf_op jit(solution)/shard_map/reduce_scatter | solution.py:75
  1328.5 1616.1 %all-reduce.6.cloned.1.call-start = ((), (), s32[]{:S(2)}) async-start(), calls=%async_computation.33 | async-start | bytes 94371840
  1496.2 1460.1 %reduce-scatter.26.cloned.1.call-start = ((), (), s32[]{:S(2)}) async-start(), calls=%async_computation.30 | async-start | bytes 12681216 | tf_op jit(solution)/shard_map/reduce_scatter | solution.py:104
  1533.2 62.5 %copy-start.12 = (bf16[2,128,1536]{2,1,0:T(8,128)(2,1)S(1)}, bf16[2,128,1536]{2,1,0:T(8,128)(2,1)}, u32[]{:S(2)}) copy-start(bf16[2,128,1536]{2,1,0:T(8,128)(2,1)} %copy-done.10) | copy-start | bytes 2359300
  1533.2 63.6 %copy-start.14 = (bf16[2,128,1536]{2,1,0:T(8,128)(2,1)S(1)}, bf16[2,128,1536]{2,1,0:T(8,128)(2,1)}, u32[]{:S(2)}) copy-start(bf16[2,128,1536]{2,1,0:T(8,128)(2,1)} %copy-done.13) | copy-start | bytes 2359300
  1536.0 61.9 %copy-start.139 = (f32[1536]{0:T(1024)S(1)}, f32[1536]{0:T(1024)}, u32[]{:S(2)}) copy-start(f32[1536]{0:T(1024)} %get-tuple-element.163) | copy-start | bytes 18436
  1536.0 61.9 %copy-start.141 = (f32[1536]{0:T(1024)S(1)}, f32[1536]{0:T(1024)}, u32[]{:S(2)}) copy-start(f32[1536]{0:T(1024)} %get-tuple-element.161) | copy-start | bytes 18436
  1536.0 61.9 %copy-start.140 = (f32[1536]{0:T(1024)S(1)}, f32[1536]{0:T(1024)}, u32[]{:S(2)}) copy-start(f32[1536]{0:T(1024)} %get-tuple-element.167) | copy-start | bytes 18436
  1536.0 62.0 %copy-start.142 = (f32[1536]{0:T(1024)S(1)}, f32[1536]{0:T(1024)}, u32[]{:S(2)}) copy-start(f32[1536]{0:T(1024)} %get-tuple-element.165) | copy-start | bytes 18436
  1538.8 48.0 %all-to-all-start.12 = ((bf16[2,1,128,1536]{3,0,1,2:T(2,128)(2,1)}), bf16[2,1,128,1536]{3,0,1,2:T(2,128)(2,1)S(1)}, u32[]{:S(2)}, u32[]{:S(2)}) async-start(bf16[2,1,128,1536]{3,0,1,2:T(2,128)(2,1)} %copy.871), calls=%async_computation.20 | async-start | bytes 1572864 | tf_op jit(solution)/shard_map/all_to_all | solution.py:422
  1586.8 97.5 %all-to-all-start.6 = ((bf16[2,1,128,1536]{3,0,1,2:T(2,128)(2,1)}), bf16[2,1,128,1536]{3,0,1,2:T(2,128)(2,1)S(1)}, u32[]{:S(2)}, u32[]{:S(2)}) async-start(bf16[2,1,128,1536]{3,0,1,2:T(2,128)(2,1)} %copy.828), calls=%async_computation.10 | async-start | bytes 1572864 | tf_op jit(solution)/shard_map/all_to_all | solution.py:421
  1684.4 1272.0 %copy-start.1 = (bf16[2,128,1,1536]{3,1,2,0:T(8,128)(2,1)S(1)}, bf16[2,128,1,1536]{3,1,2,0:T(8,128)(2,1)}, u32[]{:S(2)}) copy-start(bf16[2,128,1,1536]{3,1,2,0:T(8,128)(2,1)} %param.29) | copy-start | bytes 2359300
  (144 other events, 1450.5 us)
Sparse Core Ops, SparseCore 0:
  11.7 2.2 sort.21.cloned.1.call-done
  263.7 38.8 reduce-scatter.9
  767.2 33.8 reduce-scatter.17
  841.8 35.1 reduce-scatter.19
  923.4 39.5 reduce-scatter.13
  965.4 31.6 reduce-scatter.11
  1158.6 35.2 reduce-scatter.21
  1237.3 35.1 reduce-scatter.23
  1328.6 35.2 reduce-scatter.15
  1529.9 756.2 reduce-scatter.25
  (1 shorter events, 0.0 us)
Sparse Core Ops, SparseCore 1:
  13.0 227.8 all-gather.4
  266.1 300.0 all-gather.6
  1496.3 1448.3 all-reduce.5
where the time goes:
time: 2990 us; the launch traced here: 2960 us
  waiting for transfers between devices  1820 us (61%)
  local copies, waits for them, and re-layouts  583 us (19%)
  matrix products  240 us (8%)
  blocking collectives  121 us (4%)
  other arithmetic  116 us (4%)
  starting transfers between devices  67.8 us (2%)
    unnamed x13, waiting for transfers between devices  1260 us
    all_gather x2, waiting for transfers between devices, rows_first(): result = lax.all_gather(both, axis, axis=0, tiled=True)  296 us
    reduce_scatter x8, waiting for transfers between devices, rows_back(): lax.psum_scatter(value_rows.astype(jnp.bfloat16), 'tensor', scatter_dimen...  102 us
    all_to_all x8, waiting for transfers between devices, copy_for_each(): lax.all_to_all(jnp.broadcast_to(shard[None], (devices, *shard.shape)), ax...  90.6 us
    psum x1, blocking collectives, on_device(): lax.psum((small_attn, small_ffn, small_router), ('dp', 'tensor'))  82.6 us
    unnamed x393, local copies, waits for them, and re-layouts  69 us
  transfers between devices with their start and end apart: 24, of which 17 were waited for; matrix products, arithmetic and copies ran while one was open for 18% of the time, Pallas kernels for 0%

commit v1 on v0

v1 whole, which is shorter than its diff:
```python
import math

import jax
import jax.numpy as jnp
import numpy as np
from jax import lax
from jax.sharding import Mesh
from jax.sharding import PartitionSpec as P

QUERY_HEAD_COUNT = 12
KEY_VALUE_HEADS = 4
HEAD_SIZE = 128
GROUP = QUERY_HEAD_COUNT // KEY_VALUE_HEADS
CAP = 128
EPS = 1e-06
DP = ("x", "zl", "y", "c")
EVERY = ("x", "zl", "y", "c", "zh")
SWAP = ((0, 1), (1, 0))
F32 = jnp.float32
BF16 = jnp.bfloat16


def dot(left, right, contract, out=F32):
    result = lax.dot_general(
        left, right, (((contract[0],), (contract[1],)), ((), ())), preferred_element_type=F32
    )
    return result.astype(out)


def swapped(value, axis):
    return lax.ppermute(value, axis, SWAP)


def whole_rows(own):
    pair = jnp.concatenate([own, swapped(own, "zh")], axis=0)
    return jnp.concatenate([pair, swapped(pair, "c")], axis=0)


def rows_back(part):
    half = part.shape[0] // 2
    both = part[:half].astype(F32) + swapped(part[half:], "c").astype(F32)
    quarter = half // 2
    sent = swapped(both[quarter:].astype(BF16), "zh")
    return both[:quarter] + sent.astype(F32)


def gathered(shard):
    near = lax.all_gather(shard, "zl", axis=0, tiled=True)
    return lax.all_gather(near, ("x", "y"), axis=0, tiled=True)


def scattered(total):
    near = lax.psum_scatter(total, ("x", "y"), scatter_dimension=0, tiled=True)
    return lax.psum_scatter(near, "zl", scatter_dimension=0, tiled=True)


def silu_slope(value):
    sigma = jax.nn.sigmoid(value)
    return sigma * (1.0 + value * (1.0 - sigma))


def attention_scores(query, key):
    scaled = jnp.einsum("slgd,smd->sglm", query, key, preferred_element_type=F32) * (
        1.0 / math.sqrt(HEAD_SIZE)
    )
    place = jnp.arange(query.shape[1], dtype=jnp.int32)
    return jnp.where(place[None, :] <= place[:, None], scaled, -1e30)


def on_device(
    tokens,
    cotangent,
    lengths,
    perm,
    routes,
    gain_attn,
    gain_ffn,
    query_matrix,
    key_matrix,
    value_matrix,
    w_out,
    w_router,
    w_gate,
    w_up,
    w_down,
    s_gate,
    s_up,
    s_down,
):
    t = lax.axis_index("zh")
    place_here = lax.axis_index(DP)
    side_x, side_zl, side_y = (lax.axis_size(a) for a in ("x", "zl", "y"))
    batches, seqs = tokens.shape[0], tokens.shape[1]
    seq_len = lax.axis_size(DP)
    width = tokens.shape[3]
    experts = w_gate.shape[0]
    rows_here = query_matrix.shape[0]

    def halves(value):
        return jnp.moveaxis(value.reshape(*value.shape[:-1], 2, value.shape[-1] // 2), -2, 0)

    def expert_halves(value):
        both = value.reshape(experts, rows_here, 2, value.shape[-1] // 2)
        return jnp.transpose(both, (2, 1, 0, 3)).reshape(2, rows_here, -1)

    attn_shard = jnp.concatenate(
        [halves(query_matrix), halves(key_matrix), halves(value_matrix), halves(w_out.T)], axis=2
    )
    ffn_shard = jnp.concatenate(
        [
            expert_halves(w_gate),
            halves(s_gate),
            expert_halves(w_up),
            halves(s_up),
            expert_halves(jnp.swapaxes(w_down, 1, 2)),
            halves(s_down.T),
        ],
        axis=2,
    )
    attn_cols = attn_shard.shape[2]
    both_shards = jnp.concatenate([attn_shard, ffn_shard], axis=2)
    chip_rows = lax.all_to_all(both_shards, "c", 0, 0, tiled=True)
    chip_rows = chip_rows.reshape(2 * rows_here, -1)
    attn_w = gathered(chip_rows[:, :attn_cols])
    ffn_w = gathered(chip_rows[:, attn_cols:])
    q_cols = query_matrix.shape[1] // 2
    k_cols = key_matrix.shape[1] // 2
    qkv_cols = q_cols + 2 * k_cols
    qkv_w, out_w = attn_w[:, :qkv_cols], attn_w[:, qkv_cols:]
    hidden_e = w_gate.shape[2] // 2
    hidden = experts * hidden_e + s_gate.shape[1] // 2
    up_w, down_w = ffn_w[:, : 2 * hidden], ffn_w[:, 2 * hidden :]

    def reorder(value):
        parts = value.reshape(side_x, side_zl, side_y, -1, *value.shape[1:])
        return jnp.swapaxes(parts, 1, 2).reshape(value.shape)

    unit = width // (side_x * side_zl * side_y)
    iota = jnp.arange(width, dtype=jnp.int32)
    mate = (
        (iota // (unit * side_y * side_zl)) * (unit * side_y * side_zl)
        + ((iota // unit) % side_zl) * (unit * side_y)
        + ((iota // (unit * side_zl)) % side_y) * unit
        + iota % unit
    )
    features = (iota[:, None] == mate[None, :]).astype(BF16)
    order = lax.dynamic_index_in_dim(perm, t, 1, False)
    deal = (order[:, :, None] == jnp.arange(seqs, dtype=jnp.int32)[None, None, :]).astype(BF16)
    own_routes = lax.dynamic_slice_in_dim(routes[:, :, 0], t * seqs, seqs, 1)
    own_lengths = lax.dynamic_slice_in_dim(lengths, t * seqs, seqs, 1)
    own_valid = place_here < own_lengths
    named = jnp.any(
        own_routes[:, :, :, None] == jnp.arange(experts, dtype=jnp.int32), axis=2
    )
    marks = jnp.concatenate(
        [jnp.logical_and(named, own_valid[:, :, None]), own_valid[:, :, None]], axis=2
    ).astype(BF16)
    marks = jnp.pad(marks, ((0, 0), (0, 0), (0, 128 - marks.shape[2])))

    def dealt(value):
        sent = jnp.einsum("mjs,msd->jmd", deal, value, preferred_element_type=F32)
        sent = sent.astype(BF16).reshape(seqs, -1, 128)
        got = lax.all_to_all(sent, DP, 0, 0, tiled=True)
        got = jnp.swapaxes(got.reshape(seq_len, batches, -1), 0, 1)
        return got.reshape(batches * seq_len, -1)

    own_in = dealt(jnp.concatenate([tokens[:, :, 0], marks], axis=2))
    own_marks = own_in[:, width:]
    x_own = dot(own_in[:, :width], features, (1, 0))
    own_cot = dealt(cotangent[:, :, 0])
    own_keep = own_marks[:, experts : experts + 1].astype(F32)
    gy_own = own_keep * dot(own_cot, features, (1, 0))

    gain_a, gain_f = reorder(gain_attn), reorder(gain_ffn)
    router = reorder(w_router)
    scale_attn = lax.rsqrt(jnp.mean(x_own * x_own, axis=-1, keepdims=True) + EPS)
    unit_attn = x_own * scale_attn
    both = whole_rows(
        jnp.concatenate([(unit_attn * gain_a).astype(BF16), own_marks], axis=1)
    )
    n1, marks_all = both[:, :width], both[:, width:]
    gy = whole_rows(gy_own.astype(BF16))
    rows = n1.shape[0]
    count = rows // seq_len
    qkv = dot(n1, qkv_w, (1, 0), BF16)
    query = qkv[:, :q_cols].reshape(count, seq_len, GROUP, HEAD_SIZE)
    key = qkv[:, q_cols : q_cols + k_cols].reshape(count, seq_len, HEAD_SIZE)
    value = qkv[:, q_cols + k_cols :].reshape(count, seq_len, HEAD_SIZE)
    scores = attention_scores(query, key)
    log_total = jax.nn.logsumexp(scores, axis=-1, keepdims=True)
    probs = jnp.exp(scores - log_total)
    probs_low = probs.astype(BF16)
    mixed = jnp.einsum("sglm,smd->slgd", probs_low, value, preferred_element_type=F32)
    mixed = mixed.astype(BF16).reshape(rows, q_cols)
    h_own = x_own + rows_back(dot(mixed, out_w, (1, 1), BF16))

    scale_ffn = lax.rsqrt(jnp.mean(h_own * h_own, axis=-1, keepdims=True) + EPS)
    unit_ffn = h_own * scale_ffn
    n2 = whole_rows((unit_ffn * gain_f).astype(BF16))
    logits = dot(n2, router, (1, 0))
    hits = marks_all[:, :experts]
    per_seq = hits.reshape(2, 2, batches, seq_len, experts)
    place = jnp.arange(seq_len, dtype=jnp.int32)
    earlier = (place[None, :] < place[:, None]).astype(BF16)
    before = jnp.einsum("pq,ctmqe->ctmpe", earlier, per_seq, preferred_element_type=F32)
    totals = jnp.sum(per_seq.astype(F32), axis=3, keepdims=True)
    is_later = jnp.stack([t == 1, t == 0]).astype(F32)[None, :, None, None, None]
    rank = before + is_later * totals[:, ::-1]
    named_all = hits > 0
    kept = jnp.logical_and(named_all, rank.reshape(rows, experts) < CAP)
    top = jnp.max(jnp.where(named_all, logits, -1e30), axis=1, keepdims=True)
    powers = jnp.where(named_all, jnp.exp(jnp.where(named_all, logits - top, 0.0)), 0.0)
    gates = powers / jnp.maximum(jnp.sum(powers, axis=1, keepdims=True), 1e-30)
    kept_gates = jnp.where(kept, gates, 0.0)

    def spread(per_expert):
        wide = jnp.broadcast_to(per_expert[:, :, None], (rows, experts, hidden_e))
        return jnp.concatenate(
            [wide.reshape(rows, -1), jnp.ones((rows, hidden - experts * hidden_e), F32)], axis=1
        )

    weight = spread(kept_gates)
    ab = dot(n2, up_w, (1, 0))
    a, b = ab[:, :hidden], ab[:, hidden:]
    silu_a = jax.nn.silu(a)
    inner = (silu_a * b).astype(BF16)
    weighted = (weight * inner.astype(F32)).astype(BF16)
    branch = rows_back(dot(weighted, down_w, (1, 1), BF16))
    out_own = (own_keep * (h_own + branch)).astype(BF16)

    dhid = dot(gy, down_w, (1, 0))
    dgates = jnp.sum(
        (inner.astype(F32) * dhid)[:, : experts * hidden_e].reshape(rows, experts, hidden_e), axis=2
    )
    dgates = jnp.where(kept, dgates, 0.0)
    dlogits = gates * (dgates - jnp.sum(gates * dgates, axis=1, keepdims=True))
    dinner = weight * dhid
    dab = jnp.concatenate(
        [(dinner * b * silu_slope(a)).astype(BF16), (dinner * silu_a).astype(BF16)], axis=1
    )
    dn2_part = dot(dab, up_w, (1, 1)) + dot(dlogits.astype(BF16), router, (1, 1))
    dn2 = rows_back(dn2_part.astype(BF16))
    big_ffn = jnp.concatenate(
        [dot(n2, dab, (0, 0), BF16), dot(gy, weighted, (0, 0), BF16)], axis=1
    )
    dn2, big_ffn = lax.optimization_barrier((dn2, big_ffn))
    grad_ffn_w = scattered(big_ffn)
    small_router = dot(n2, dlogits.astype(BF16), (0, 0))
    small_ffn = jnp.sum(dn2 * unit_ffn, axis=0)
    scaled = dn2 * gain_f
    dh = gy_own + scale_ffn * (
        scaled - unit_ffn * jnp.mean(scaled * unit_ffn, axis=-1, keepdims=True)
    )

    dattn = whole_rows(dh.astype(BF16))
    dmixed = dot(dattn, out_w, (1, 0), BF16)
    big_out = dot(dattn, mixed, (0, 0), BF16)
    dheads = dmixed.reshape(count, seq_len, GROUP, HEAD_SIZE)
    dprobs = jnp.einsum("slgd,smd->sglm", dheads, value, preferred_element_type=F32)
    dscores = (probs * (dprobs - jnp.sum(probs * dprobs, axis=-1, keepdims=True))).astype(BF16)
    root = 1.0 / math.sqrt(HEAD_SIZE)
    dq = jnp.einsum("sglm,smd->slgd", dscores, key, preferred_element_type=F32) * root
    dk = jnp.einsum("sglm,slgd->smd", dscores, query, preferred_element_type=F32) * root
    dv = jnp.einsum("sglm,slgd->smd", probs_low, dheads, preferred_element_type=F32)
    dqkv = jnp.concatenate(
        [
            dq.astype(BF16).reshape(rows, -1),
            dk.astype(BF16).reshape(rows, -1),
            dv.astype(BF16).reshape(rows, -1),
        ],
        axis=1,
    )
    dn1 = rows_back(dot(dqkv, qkv_w, (1, 1), BF16))
    big_attn = jnp.concatenate([dot(n1, dqkv, (0, 0), BF16), big_out], axis=1)
    grad_attn_w = scattered(big_attn)
    small_attn = jnp.sum(dn1 * unit_attn, axis=0)
    scaled = dn1 * gain_a
    dx_own = dh + scale_attn * (
        scaled - unit_attn * jnp.mean(scaled * unit_attn, axis=-1, keepdims=True)
    )
    dx_own = dx_own.astype(BF16)

    def returned(own):
        natural = dot(own, features, (1, 0), BF16).reshape(batches, seq_len, -1)
        sent = jnp.swapaxes(natural, 0, 1).reshape(seq_len, -1, 128)
        got = lax.all_to_all(sent, DP, 0, 0, tiled=True).reshape(seqs, batches, -1)
        back = jnp.einsum("mjs,jmd->msd", deal, got, preferred_element_type=F32)
        return back.astype(BF16)[:, :, None]

    out_tokens = returned(out_own)
    grad_tokens = returned(dx_own)

    small = jnp.concatenate([small_attn[None], small_ffn[None], small_router.T], axis=0)
    small = lax.psum(small, EVERY)
    final = reorder(small.T)

    mine = jnp.concatenate([grad_attn_w, grad_ffn_w], axis=1).reshape(2, rows_here, -1)
    mine = lax.all_to_all(mine, "c", 0, 0, tiled=True).astype(F32)

    def join(start, cols):
        part = mine[:, :, start : start + cols]
        return jnp.swapaxes(part, 0, 1).reshape(rows_here, 2 * cols)

    def join_experts(start):
        part = mine[:, :, start : start + experts * hidden_e]
        part = part.reshape(2, rows_here, experts, hidden_e)
        return jnp.transpose(part, (2, 1, 0, 3)).reshape(experts, rows_here, 2 * hidden_e)

    shared_cols = s_gate.shape[1] // 2
    ffn_at = attn_cols
    each = experts * hidden_e
    return (
        out_tokens,
        grad_tokens,
        final[:, 0],
        final[:, 1],
        join(0, q_cols),
        join(q_cols, k_cols),
        join(q_cols + k_cols, k_cols),
        join(qkv_cols, q_cols).T,
        final[:, 2:],
        join_experts(ffn_at),
        join_experts(ffn_at + hidden),
        jnp.swapaxes(join_experts(ffn_at + 2 * hidden), 1, 2),
        join(ffn_at + each, shared_cols),
        join(ffn_at + hidden + each, shared_cols),
        join(ffn_at + 2 * hidden + each, shared_cols).T,
    )


def solution(mesh):
    devices = np.asarray(mesh.devices)
    side = round((devices.shape[0] // 2) ** (1 / 3))
    fine = Mesh(devices.reshape(side, side, side, 2, 2), EVERY)
    rows, cols = P(DP, "zh"), P("zh", DP)
    seqs = P(None, "zh", DP, None)
    return jax.shard_map(
        on_device,
        mesh=fine,
        in_specs=(
            seqs,
            seqs,
            P(),
            P(),
            P(None, None, DP, None),
            P(),
            P(),
            rows,
            rows,
            rows,
            cols,
            P(),
            P(None, DP, "zh"),
            P(None, DP, "zh"),
            P(None, "zh", DP),
            rows,
            rows,
            cols,
        ),
        out_specs=(
            seqs,
            seqs,
            P(),
            P(),
            rows,
            rows,
            rows,
            cols,
            P(),
            P(None, DP, "zh"),
            P(None, DP, "zh"),
            P(None, "zh", DP),
            rows,
            rows,
            cols,
        ),
        check_vma=False,
    )
```

time: 2990 us -> 805 us (0.27)
  waiting for transfers between devices: 1820 us -> 343 us
  local copies, waits for them, and re-layouts: 583 us -> 62.4 us
  matrix products: 240 us -> 119 us
  other arithmetic: 116 us -> 43.6 us
  starting transfers between devices: 67.8 us -> 103 us
    unnamed x13 -> x6, waiting for transfers between devices: 1260 us -> 0.4 us
    all_gather x2, waiting for transfers between devices: 296 us -> 0.01 us  [gathered(): return lax.all_gather(near, ('x', 'y'), axis=0, tiled=True)]
    ppermute x0 -> x16, waiting for transfers between devices: none -> 203 us  [swapped(): return lax.ppermute(value, axis, SWAP)]
    gather x34 -> x0, local copies, waits for them, and re-layouts: 169 us -> none  [the longest x4 49.9 us: on_device(): jnp.take(grad_in, safe_target, axis=0)]
    dot_general x80 -> x30, matrix products: 240 us -> 119 us  [the longest x19 109 us: dot(): lax.dot_general(left, right, (((contract[0],), (contract[1],)), ((), ()))...]
    all_to_all x12 -> x4, waiting for transfers between devices: 163 us -> 68.6 us  [the longest x2 55.2 us: dealt(): got = lax.all_to_all(sent, DP, 0, 0, tiled=True)]
    reshape x32 -> x33, local copies, waits for them, and re-layouts: 91.4 us -> 23 us  [the longest x7 5.24 us: halves(): value.reshape(*value.shape[:-1], 2, value.shape[-1] // 2)]
    add x5 -> x0, local copies, waits for them, and re-layouts: 59.4 us -> none  [on_device(): old + new]
  transfers between devices with their start and end apart: 24 -> 26, of which waited for: 17 -> 14; matrix products, arithmetic and copies ran while one was open for 18% -> 16% of each run, Pallas kernels for 0% -> 0%
where the time goes in v1:
time: 805 us; the launch traced here: 802 us
  waiting for transfers between devices  343 us (43%)
  matrix products  119 us (15%)
  blocking collectives  114 us (14%)
  starting transfers between devices  103 us (13%)
  local copies, waits for them, and re-layouts  62.4 us (8%)
  other arithmetic  43.6 us (5%)
  between operations  16.1 us (2%)
    ppermute x16, waiting for transfers between devices, swapped(): return lax.ppermute(value, axis, SWAP)  203 us
    dot_general x19, matrix products, dot(): lax.dot_general(left, right, (((contract[0],), (contract[1],)), ((), ()))...  109 us
    psum x1, blocking collectives, on_device(): small = lax.psum(small, EVERY)  76.8 us
    reduce_scatter x2, waiting for transfers between devices, scattered(): near = lax.psum_scatter(total, ('x', 'y'), scatter_dimension=0, tiled=True)  70.9 us
    all_to_all x2, waiting for transfers between devices, dealt(): got = lax.all_to_all(sent, DP, 0, 0, tiled=True)  55.2 us
    all_to_all x2, starting transfers between devices, returned(): got = lax.all_to_all(sent, DP, 0, 0, tiled=True).reshape(seqs, batches, -1)  37.8 us
    ppermute x16, starting transfers between devices, swapped(): return lax.ppermute(value, axis, SWAP)  34.6 us
    all_to_all x2, starting transfers between devices, dealt(): got = lax.all_to_all(sent, DP, 0, 0, tiled=True)  30.2 us
  transfers between devices with their start and end apart: 26, of which 14 were waited for; matrix products, arithmetic and copies ran while one was open for 16% of the time, Pallas kernels for 0%

profile of v1, /device:TPU:1, one launch (start us, length us, event | category | flops | bytes accessed | tf_op | source)
XLA Modules:
  0.0 801.6 jit_solution(6814157459256501051)
XLA Ops:
  15.3 6.8 all_to_all.30
  22.3 11.6 %all_gather.12 = bf16[96,1024]{1,0:T(8,128)(2,1)} all-gather(bf16[24,1024]{1,0:T(8,128)(2,1)S(1)} %slice.195), channel_id=1, replica_groups=mesh['x'=4,'zl'=4,'y'=4,'c'=2,'zh'=2] {'zl'}, dimensions={0}, use_global_device_ids=true | all-gather | bytes 245760 | tf_op jit(solution)/shard_map/all_gather | solution.py:48
  34.0 14.4 %all_gather.14 = bf16[96,3840]{1,0:T(8,128)(2,1)} all-gather(bf16[24,3840]{1,0:T(8,128)(2,1)S(1)} %slice.205), channel_id=1, replica_groups=mesh['x'=4,'zl'=4,'y'=4,'c'=2,'zh'=2] {'zl'}, dimensions={0}, use_global_device_ids=true | all-gather | bytes 921600 | tf_op jit(solution)/shard_map/all_gather | solution.py:48
  49.5 2.1 copy.287
  51.6 16.4 %all-to-all-start = ((bf16[128,26,128]{2,1,0:T(8,128)(2,1)}), bf16[128,26,128]{2,1,0:T(8,128)(2,1)S(1)}, u32[]{:S(2)}, u32[]{:S(2)}) async-start(bf16[128,26,128]{2,1,0:T(8,128)(2,1)} %copy.287), calls=%async_computation | async-start | bytes 2097152 | tf_op jit(solution)/shard_map/all_to_all | solution.py:163
  68.3 29.3 %all-to-all-done = bf16[128,26,128]{2,1,0:T(8,128)(2,1)S(1)} async-done(((bf16[128,26,128]{2,1,0:T(8,128)(2,1)}), bf16[128,26,128]{2,1,0:T(8,128)(2,1)S(1)}, u32[]{:S(2)}, u32[]{:S(2)}) %all-to-all-start) | async-done | bytes 852000 | tf_op jit(solution)/shard_map/all_to_all | solution.py:163
  99.4 2.1 multiply_reduce_fusion.5
  101.9 5.1 collective-permute-start
  107.0 27.6 %collective-permute-done = bf16[256,1664]{1,0:T(8,128)(2,1)S(1)} collective-permute-done((bf16[256,1664]{1,0:T(8,128)(2,1)S(1)}, bf16[256,1664]{1,0:T(8,128)(2,1)S(1)}, u32[]{:S(2)}, u32[]{:S(2)}) %collective-permute-start) | collective-permute-done | bytes 852000 | tf_op jit(solution)/shard_map/ppermute | solution.py:31
  134.8 2.7 collective-permute-start.1
  137.5 3.2 collective-permute-done.1
  141.9 6.2 pad_maximum_fusion.2
  148.1 5.1 fusion.32
  156.7 1.9 fusion.119
  159.9 3.4 convolution_convert_fusion.3
  164.0 3.0 collective-permute-done.2
  170.1 5.3 collective-permute-start.3
  179.5 13.8 %all-to-all-start.3 = ((bf16[128,24,128]{2,1,0:T(8,128)(2,1)}), bf16[128,24,128]{2,1,0:T(8,128)(2,1)S(1)}, u32[]{:S(2)}, u32[]{:S(2)}) async-start(bf16[128,24,128]{2,1,0:T(8,128)(2,1)} %copy.309), calls=%async_computation.3 | async-start | bytes 1572864 | tf_op jit(solution)/shard_map/all_to_all | solution.py:163
  193.6 2.5 multiply_reduce_fusion.4
  197.5 5.0 collective-permute-start.4
  202.5 39.9 %collective-permute-done.4 = bf16[256,1536]{1,0:T(8,128)(2,1)S(1)} collective-permute-done((bf16[256,1536]{1,0:T(8,128)(2,1)S(1)}, bf16[256,1536]{1,0:T(8,128)(2,1)S(1)}, u32[]{:S(2)}, u32[]{:S(2)}) %collective-permute-start.4) | collective-permute-done | bytes 786464 | tf_op jit(solution)/shard_map/ppermute | solution.py:31
  245.4 25.9 %all-to-all-done.3 = bf16[128,24,128]{2,1,0:T(8,128)(2,1)S(1)} async-done(((bf16[128,24,128]{2,1,0:T(8,128)(2,1)}), bf16[128,24,128]{2,1,0:T(8,128)(2,1)S(1)}, u32[]{:S(2)}, u32[]{:S(2)}) %all-to-all-start.3) | async-done | bytes 786464 | tf_op jit(solution)/shard_map/all_to_all | solution.py:163
  275.1 3.5 fusion.120
  279.2 36.7 %collective-permute-done.8 = bf16[256,1536]{1,0:T(8,128)(2,1)S(1)} collective-permute-done((bf16[256,1536]{1,0:T(8,128)(2,1)}, bf16[256,1536]{1,0:T(8,128)(2,1)S(1)}, u32[]{:S(2)}, u32[]{:S(2)}) %collective-permute-start.8) | collective-permute-done | bytes 786464 | tf_op jit(solution)/shard_map/ppermute | solution.py:31
  315.8 2.6 pad_maximum_fusion.11
  319.9 2.9 select_reduce_fusion
  325.3 3.1 copy.408
  328.4 13.9 %fusion.6 = f32[1024,2560]{1,0:T(8,128)} fusion(bf16[1536,3840]{1,0:T(8,128)(2,1)} %all-gather.5.cloned.1.call-done, bf16[512,1536]{1,0:T(8,128)(2,1)} %collective-permute-done.5, bf16[256,1536]{1,0:T(8,128)(2,1)} %copy-done.32, bf16[256,1536]{1,0:T(8,128)(2,1)S(1)} %copy-done.15), kind=kOutput, calls=%fused_computation.10 | convolution fusion | flops 8062500864 | bytes 21495808 | tf_op jit(solution)/shard_map/dot_general | solution.py:24
  342.3 15.2 %multiply_convert_fusion.1 = (bf16[1024,1280]{1,0:T(8,128)(2,1)}, bf16[1024,1280]{1,0:T(8,128)(2,1)}, bf16[1024,1280]{1,0:T(8,128)(2,1)}, f32[1024,1280]{1,0:T(8,128)}, f32[1024,1280]{1,0:T(8,128)}) fusion(f32[1024,2560]{1,0:T(8,128)} %fusion.6, f32[1024,1024]{1,0:T(8,128)} %bitcast.256, bf16[1536,3840]{1,0:T(8,128)(2,1)} %all-gather.5.cloned.1.call-done, ...), kind=kOutput, calls=%fused_computation.18 | convolution fusion | flops 4060872704 | bytes 40108032 | tf_op jit(solution)/shard_map/dot_general | solution.py:24
  357.5 4.4 fusion.16
  361.9 3.0 copy.372
  364.9 3.4 reduce_sum.113
  370.2 12.7 %add_convert_fusion = bf16[1024,1536]{1,0:T(8,128)(2,1)S(1)} fusion(f32[1024,1536]{1,0:T(8,128)S(1)} %fusion.121, bf16[1536,3840]{1,0:T(8,128)(2,1)} %all-gather.5.cloned.1.call-done, bf16[1024,1280]{1,0:T(8,128)(2,1)} %get-tuple-element.125, bf16[1024,1280]{1,0:T(8,128)(2,1)} %get-tuple-element.124), kind=kOutput, calls=%fused_computation.12 | convolution fusion | flops 8066695168 | bytes 22544384 | tf_op jit(solution)/shard_map/dot_general | solution.py:24
  384.0 6.9 convolution_convert_fusion.1
  390.9 11.4 %convolution_convert_fusion = bf16[1536,2560]{1,0:T(8,128)(2,1)S(1)} fusion(bf16[1024,1280]{1,0:T(8,128)(2,1)} %get-tuple-element.125, bf16[1024,1280]{1,0:T(8,128)(2,1)} %get-tuple-element.124, bf16[512,1536]{1,0:T(8,128)(2,1)} %collective-permute-done.5, bf16[256,1536]{1,0:T(8,128)(2,1)S(1)} %copy-done.33, bf16[256,1536]{1,0:T(8,128)(2,1)S(1)} %copy-done.16), kind=kOutput, calls=%fused_computation.1 | convolution fusion | flops 8076918784 | bytes 16252928 | tf_op jit(solution)/shard_map/dot_general | solution.py:24
  402.3 1.9 convert_add_fusion.1
  404.2 1.7 copy-done.9
  406.0 2.8 collective-permute-start.11
  408.8 5.1 pad_maximum_fusion
  413.8 27.7 %collective-permute-done.11 = bf16[256,1536]{1,0:T(8,128)(2,1)S(1)} collective-permute-done((bf16[256,1536]{1,0:T(8,128)(2,1)S(1)}, bf16[256,1536]{1,0:T(8,128)(2,1)S(1)}, u32[]{:S(2)}, u32[]{:S(2)}) %collective-permute-start.11) | collective-permute-done | bytes 786464 | tf_op jit(solution)/shard_map/ppermute | solution.py:31
  443.1 1.9 multiply_reduce_fusion
  446.8 5.1 collective-permute-start.12
  451.9 28.1 %collective-permute-done.12 = bf16[256,1536]{1,0:T(8,128)(2,1)S(1)} collective-permute-done((bf16[256,1536]{1,0:T(8,128)(2,1)S(1)}, bf16[256,1536]{1,0:T(8,128)(2,1)S(1)}, u32[]{:S(2)}, u32[]{:S(2)}) %collective-permute-start.12) | collective-permute-done | bytes 786464 | tf_op jit(solution)/shard_map/ppermute | solution.py:31
  480.7 3.0 collective-permute-done.13
  484.9 4.0 convolution_convert_fusion.11
  488.8 2.4 reshape.412
  496.3 4.7 convolution_convert_fusion.5
  501.1 1.8 convolution_convert_fusion.6
  502.9 2.2 pad_maximum_fusion.8
  505.7 7.2 convolution_convert_fusion.4
  514.8 2.9 convolution_convert_fusion.2
  519.3 2.1 collective-permute-done.14
  524.4 3.0 collective-permute-start.15
  527.4 31.9 %collective-permute-done.7 = bf16[256,1536]{1,0:T(8,128)(2,1)S(1)} collective-permute-done((bf16[256,1536]{1,0:T(8,128)(2,1)S(1)}, bf16[256,1536]{1,0:T(8,128)(2,1)S(1)}, u32[]{:S(2)}, u32[]{:S(2)}) %collective-permute-start.7) | collective-permute-done | bytes 786464 | tf_op jit(solution)/shard_map/ppermute | solution.py:31
  559.3 3.1 fusion.25
  565.4 31.4 %all-to-all-start.2 = ((bf16[128,24,128]{2,1,0:T(8,128)(2,1)}), bf16[128,24,128]{2,1,0:T(8,128)(2,1)S(1)}, u32[]{:S(2)}, u32[]{:S(2)}) async-start(bf16[128,24,128]{2,1,0:T(8,128)(2,1)} %copy.304), calls=%async_computation.2 | async-start | bytes 1572864 | tf_op jit(solution)/shard_map/all_to_all | solution.py:286
  597.1 2.0 multiply_reduce_fusion.1
  599.2 5.2 fusion.26
  607.3 13.4 %all-to-all-done.2 = bf16[128,24,128]{2,1,0:T(8,128)(2,1)S(1)} async-done(((bf16[128,24,128]{2,1,0:T(8,128)(2,1)}), bf16[128,24,128]{2,1,0:T(8,128)(2,1)S(1)}, u32[]{:S(2)}, u32[]{:S(2)}) %all-to-all-start.2) | async-done | bytes 786464 | tf_op jit(solution)/shard_map/all_to_all | solution.py:286
  620.7 6.3 all-to-all-start.4
  627.1 70.8 %reduce-scatter.9.cloned.1.call-done = bf16[96,3840]{1,0:T(8,128)(2,1)} async-done(((bf16[1536,3840]{1,0:T(8,128)(2,1)}), bf16[96,3840]{1,0:T(8,128)(2,1)}) %reduce-scatter.9.cloned.1.call-update) | async-done | bytes 737296 | tf_op jit(solution)/shard_map/reduce_scatter | solution.py:53
  698.1 2.0 fusion.112
  702.7 76.8 %psum.7 = f32[1536,10]{0,1:T(8,128)S(1)} all-reduce(f32[1536,10]{0,1:T(8,128)S(1)} %reshape.385), channel_id=1, replica_groups=mesh['x'=4,'zl'=4,'y'=4,'c'=2,'zh'=2] {'x','zl','y','c','zh'}, use_global_device_ids=true, to_apply=%region_15.16 | all-reduce | flops 15360 | bytes 122880 | tf_op jit(solution)/shard_map/psum | solution.py:294
  783.6 4.6 all_to_all.31
  (300 shorter events, 77.5 us)
Async XLA Ops:
  7.2 168.2 %copy-start = (bf16[2,128,1,1536]{3,1,2,0:T(8,128)(2,1)S(1)}, bf16[2,128,1,1536]{3,1,2,0:T(8,128)(2,1)}, u32[]{:S(2)}) copy-start(bf16[2,128,1,1536]{3,1,2,0:T(8,128)(2,1)} %param.19) | copy-start | bytes 2359300
  7.2 41.3 %copy-start.50 = (s32[2,256]{1,0:T(2,128)S(1)}, s32[2,256]{1,0:T(2,128)}, u32[]{:S(2)}) copy-start(s32[2,256]{1,0:T(2,128)} %param.20) | copy-start | bytes 6148
  7.2 41.3 %copy-start.49 = (s32[2,256,1,6]{1,2,3,0:T(1,128)S(1)}, s32[2,256,1,6]{1,2,3,0:T(1,128)}, u32[]{:S(2)}) copy-start(s32[2,256,1,6]{1,2,3,0:T(1,128)} %param.22) | copy-start | bytes 36868
  7.2 41.3 %copy-start.29 = (bf16[2,128,1,1536]{3,1,2,0:T(8,128)(2,1)S(1)}, bf16[2,128,1,1536]{3,1,2,0:T(8,128)(2,1)}, u32[]{:S(2)}) copy-start(bf16[2,128,1,1536]{3,1,2,0:T(8,128)(2,1)} %param.18) | copy-start | bytes 2359300
  7.2 140.9 %all-gather.3.cloned.1.call-start = ((), (), s32[]{:S(2)}) async-start(), calls=%async_computation.10 | async-start | bytes 3342336 | tf_op jit(solution)/shard_map/all_gather | solution.py:49
  15.1 34.0 %copy-start.51 = (s32[2,2,128]{2,1,0:T(2,128)S(1)}, s32[2,2,128]{2,1,0:T(2,128)}, u32[]{:S(2)}) copy-start(s32[2,2,128]{2,1,0:T(2,128)} %param.21) | copy-start | bytes 6148
  33.9 294.4 %all-gather.5.cloned.1.call-start = ((), (), s32[]{:S(2)}) async-start(), calls=%async_computation.11 | async-start | bytes 12533760 | tf_op jit(solution)/shard_map/all_gather | solution.py:49
  49.0 19.0 %copy-start.47 = (f32[1536]{0:T(1024)S(1)}, f32[1536]{0:T(1024)}, u32[]{:S(2)}) copy-start(f32[1536]{0:T(1024)} %param.23) | copy-start | bytes 18436
  49.1 126.3 %copy-start.43 = (s32[2,1,128]{2,1,0:T(1,128)}, s32[2,1,128]{2,1,0:T(1,128)S(1)}, u32[]{:S(2)}) copy-start(s32[2,1,128]{2,1,0:T(1,128)S(1)} %constant_dynamic-slice_fusion.1) | copy-start | bytes 3076
  51.6 45.9 %all-to-all-start = ((bf16[128,26,128]{2,1,0:T(8,128)(2,1)}), bf16[128,26,128]{2,1,0:T(8,128)(2,1)S(1)}, u32[]{:S(2)}, u32[]{:S(2)}) async-start(bf16[128,26,128]{2,1,0:T(8,128)(2,1)} %copy.287), calls=%async_computation | async-start | bytes 2097152 | tf_op jit(solution)/shard_map/all_to_all | solution.py:163
  68.2 33.4 %copy-start.40 = (f32[1536]{0:T(1024)}, f32[1536]{0:T(1024)S(1)}, u32[]{:S(2)}) copy-start(f32[1536]{0:T(1024)S(1)} %mul.258) | copy-start | bytes 18436
  101.6 33.2 %copy-start.5 = (f32[256,1536]{1,0:T(8,128)}, f32[256,1536]{1,0:T(8,128)S(1)}, u32[]{:S(2)}) copy-start(f32[256,1536]{1,0:T(8,128)S(1)} %get-tuple-element.141) | copy-start | bytes 4718596
  101.6 33.2 %copy-start.45 = (f32[256]{0:T(256)}, f32[256]{0:T(256)S(1)}, u32[]{:S(2)}) copy-start(f32[256]{0:T(256)S(1)} %add_rsqrt_fusion.1) | copy-start | bytes 3076
  101.9 32.8 %collective-permute-start = (bf16[256,1664]{1,0:T(8,128)(2,1)S(1)}, bf16[256,1664]{1,0:T(8,128)(2,1)S(1)}, u32[]{:S(2)}, u32[]{:S(2)}) collective-permute-start(bf16[256,1664]{1,0:T(8,128)(2,1)S(1)} %pad_maximum_fusion.18), channel_id=1, source_target_pairs={{0,1},{1,0},{2,3},{3,2},{4,5},{5,4},{6,7},{7,6},{8,9},{9,8},{10,11... | collective-permute-start | bytes 2555912 | tf_op jit(solution)/shard_map/ppermute | solution.py:31
  134.6 6.1 copy-start.10
  134.8 5.9 collective-permute-start.1
  156.7 2.7 copy-start.18
  159.9 3.4 copy-start.30
  163.5 3.5 collective-permute-start.2
  170.1 23.3 %copy-start.48 = (f32[1536]{0:T(1024)S(1)}, f32[1536]{0:T(1024)}, u32[]{:S(2)}) copy-start(f32[1536]{0:T(1024)} %param.24) | copy-start | bytes 18436
  170.1 23.5 %collective-permute-start.3 = (bf16[256,1536]{1,0:T(8,128)(2,1)}, bf16[256,1536]{1,0:T(8,128)(2,1)}, u32[]{:S(2)}, u32[]{:S(2)}) collective-permute-start(bf16[256,1536]{1,0:T(8,128)(2,1)} %slice.320), channel_id=1, source_target_pairs={{0,1},{1,0},{2,3},{3,2},{4,5},{5,4},{6,7},{7,6},{8,9},{9,8},{10,11... | collective-permute-start | bytes 2359304 | tf_op jit(solution)/shard_map/ppermute | solution.py:31
  179.5 91.8 %all-to-all-start.3 = ((bf16[128,24,128]{2,1,0:T(8,128)(2,1)}), bf16[128,24,128]{2,1,0:T(8,128)(2,1)S(1)}, u32[]{:S(2)}, u32[]{:S(2)}) async-start(bf16[128,24,128]{2,1,0:T(8,128)(2,1)} %copy.309), calls=%async_computation.3 | async-start | bytes 1572864 | tf_op jit(solution)/shard_map/all_to_all | solution.py:163
  193.3 405.8 %reduce-scatter.5.cloned.1.call-start = ((), (), s32[]{:S(2)}) async-start(), calls=%async_computation.12 | async-start | bytes 3342336 | tf_op jit(solution)/shard_map/reduce_scatter | solution.py:53
  197.4 46.3 %copy-start.14 = (bf16[256,1536]{1,0:T(8,128)(2,1)}, bf16[256,1536]{1,0:T(8,128)(2,1)S(1)}, u32[]{:S(2)}) copy-start(bf16[256,1536]{1,0:T(8,128)(2,1)S(1)} %multiply_convert_fusion.4) | copy-start | bytes 2359300
  197.5 44.9 %collective-permute-start.4 = (bf16[256,1536]{1,0:T(8,128)(2,1)S(1)}, bf16[256,1536]{1,0:T(8,128)(2,1)S(1)}, u32[]{:S(2)}, u32[]{:S(2)}) collective-permute-start(bf16[256,1536]{1,0:T(8,128)(2,1)S(1)} %multiply_convert_fusion.4), channel_id=1, source_target_pairs={{0,1},{1,0},{2,3},{3,2},{4,5},{5,4},{6,7},{7,6},{8,9},{9,8},{10,11... | collective-permute-start | bytes 2359304 | tf_op jit(solution)/shard_map/ppermute | solution.py:31
  243.7 76.1 %collective-permute-start.5 = (bf16[512,1536]{1,0:T(8,128)(2,1)}, bf16[512,1536]{1,0:T(8,128)(2,1)}, u32[]{:S(2)}, u32[]{:S(2)}) collective-permute-start(bf16[512,1536]{1,0:T(8,128)(2,1)} %pad_maximum_fusion.10), channel_id=1, source_target_pairs={{0,2},{2,0},{1,3},{3,1},{4,6},{6,4},{5,7},{7,5},{8,10},{10,8},{9,1... | collective-permute-start | bytes 4718600 | tf_op jit(solution)/shard_map/ppermute | solution.py:31
  275.1 3.5 copy-start.42
  278.6 37.2 %collective-permute-start.8 = (bf16[256,1536]{1,0:T(8,128)(2,1)}, bf16[256,1536]{1,0:T(8,128)(2,1)S(1)}, u32[]{:S(2)}, u32[]{:S(2)}) collective-permute-start(bf16[256,1536]{1,0:T(8,128)(2,1)} %get-tuple-element.144), channel_id=1, source_target_pairs={{0,1},{1,0},{2,3},{3,2},{4,5},{5,4},{6,7},{7,6},{8,9},{9,8},{10,11... | collective-permute-start | bytes 2359304 | tf_op jit(solution)/shard_map/ppermute | solution.py:31
  279.1 40.8 %copy-start.22 = (bf16[512,1664]{1,0:T(8,128)(2,1)S(1)}, bf16[512,1664]{1,0:T(8,128)(2,1)}, u32[]{:S(2)}) copy-start(bf16[512,1664]{1,0:T(8,128)(2,1)} %copy-done.21) | copy-start | bytes 5111812
  315.8 4.0 copy-start.35
  318.5 23.8 %collective-permute-start.9 = (bf16[512,1536]{1,0:T(8,128)(2,1)}, bf16[512,1536]{1,0:T(8,128)(2,1)}, u32[]{:S(2)}, u32[]{:S(2)}) collective-permute-start(bf16[512,1536]{1,0:T(8,128)(2,1)} %pad_maximum_fusion.11), channel_id=1, source_target_pairs={{0,2},{2,0},{1,3},{3,1},{4,6},{6,4},{5,7},{7,5},{8,10},{10,8},{9,1... | collective-permute-start | bytes 4718600 | tf_op jit(solution)/shard_map/ppermute | solution.py:31
  325.3 3.1 copy-start.15
  328.4 13.9 %copy-start.36 = (bf16[256,1536]{1,0:T(8,128)(2,1)S(1)}, bf16[256,1536]{1,0:T(8,128)(2,1)}, u32[]{:S(2)}) copy-start(bf16[256,1536]{1,0:T(8,128)(2,1)} %copy-done.35) | copy-start | bytes 2359300
  383.0 19.3 %collective-permute-start.10 = (bf16[512,1536]{1,0:T(8,128)(2,1)S(1)}, bf16[512,1536]{1,0:T(8,128)(2,1)}, u32[]{:S(2)}, u32[]{:S(2)}) collective-permute-start(bf16[512,1536]{1,0:T(8,128)(2,1)S(1)} %slice.217), channel_id=1, source_target_pairs={{0,2},{2,0},{1,3},{3,1},{4,6},{6,4},{5,7},{7,5},{8,10},{10,8},{9,1... | collective-permute-start | bytes 4718600 | tf_op jit(solution)/shard_map/ppermute | solution.py:31
  384.0 6.9 copy-start.16
  384.0 6.9 copy-start.33
  406.0 35.5 %collective-permute-start.11 = (bf16[256,1536]{1,0:T(8,128)(2,1)S(1)}, bf16[256,1536]{1,0:T(8,128)(2,1)S(1)}, u32[]{:S(2)}, u32[]{:S(2)}) collective-permute-start(bf16[256,1536]{1,0:T(8,128)(2,1)S(1)} %slice.318), channel_id=1, source_target_pairs={{0,1},{1,0},{2,3},{3,2},{4,5},{5,4},{6,7},{7,6},{8,9},{9,8},{10,11... | collective-permute-start | bytes 2359304 | tf_op jit(solution)/shard_map/ppermute | solution.py:31
  413.8 31.3 %copy-start.3 = (f32[256,1536]{1,0:T(8,128)S(1)}, f32[256,1536]{1,0:T(8,128)}, u32[]{:S(2)}) copy-start(f32[256,1536]{1,0:T(8,128)} %copy-done.2) | copy-start | bytes 4718596
  413.8 31.3 %copy-start.23 = (f32[256,1536]{1,0:T(8,128)S(1)}, f32[256,1536]{1,0:T(8,128)}, u32[]{:S(2)}) copy-start(f32[256,1536]{1,0:T(8,128)} %get-tuple-element.145) | copy-start | bytes 4718596
  446.8 42.1 %copy-start.12 = (bf16[256,1536]{1,0:T(8,128)(2,1)}, bf16[256,1536]{1,0:T(8,128)(2,1)S(1)}, u32[]{:S(2)}) copy-start(bf16[256,1536]{1,0:T(8,128)(2,1)S(1)} %get-tuple-element.115) | copy-start | bytes 2359300
  446.8 33.2 %collective-permute-start.12 = (bf16[256,1536]{1,0:T(8,128)(2,1)S(1)}, bf16[256,1536]{1,0:T(8,128)(2,1)S(1)}, u32[]{:S(2)}, u32[]{:S(2)}) collective-permute-start(bf16[256,1536]{1,0:T(8,128)(2,1)S(1)} %get-tuple-element.115), channel_id=1, source_target_pairs={{0,1},{1,0},{2,3},{3,2},{4,5},{5,4},{6,7},{7,6},{8,9},{9,8},{10,11... | collective-permute-start | bytes 2359304 | tf_op jit(solution)/shard_map/ppermute | solution.py:31
  480.0 3.7 copy-start.38
  480.1 3.6 collective-permute-start.13
  496.3 4.7 copy-start.13
  496.3 4.7 copy-start.31
  496.3 4.7 copy-start.39
  496.3 4.7 copy-start.54
  505.1 192.9 %reduce-scatter.9.cloned.1.call-start = ((), (), s32[]{:S(2)}) async-start(), calls=%async_computation.14 | async-start | bytes 12533760 | tf_op jit(solution)/shard_map/reduce_scatter | solution.py:53
  513.0 5.3 collective-permute-start.6
  517.8 3.5 collective-permute-start.14
  518.8 40.5 %copy-start.4 = (f32[256,1536]{1,0:T(8,128)S(1)}, f32[256,1536]{1,0:T(8,128)}, u32[]{:S(2)}) copy-start(f32[256,1536]{1,0:T(8,128)} %copy-done.2) | copy-start | bytes 4718596
  518.8 40.5 %collective-permute-start.7 = (bf16[256,1536]{1,0:T(8,128)(2,1)S(1)}, bf16[256,1536]{1,0:T(8,128)(2,1)S(1)}, u32[]{:S(2)}, u32[]{:S(2)}) collective-permute-start(bf16[256,1536]{1,0:T(8,128)(2,1)S(1)} %slice.319), channel_id=1, source_target_pairs={{0,1},{1,0},{2,3},{3,2},{4,5},{5,4},{6,7},{7,6},{8,9},{9,8},{10,11... | collective-permute-start | bytes 2359304 | tf_op jit(solution)/shard_map/ppermute | solution.py:31
  524.4 72.7 %collective-permute-start.15 = (bf16[256,1536]{1,0:T(8,128)(2,1)}, bf16[256,1536]{1,0:T(8,128)(2,1)S(1)}, u32[]{:S(2)}, u32[]{:S(2)}) collective-permute-start(bf16[256,1536]{1,0:T(8,128)(2,1)} %slice.317), channel_id=1, source_target_pairs={{0,1},{1,0},{2,3},{3,2},{4,5},{5,4},{6,7},{7,6},{8,9},{9,8},{10,11... | collective-permute-start | bytes 2359304 | tf_op jit(solution)/shard_map/ppermute | solution.py:31
  562.4 34.7 %copy-start.6 = (f32[256,1536]{1,0:T(8,128)S(1)}, f32[256,1536]{1,0:T(8,128)}, u32[]{:S(2)}) copy-start(f32[256,1536]{1,0:T(8,128)} %copy-done.5) | copy-start | bytes 4718596
  562.4 34.7 %copy-start.41 = (f32[1536]{0:T(1024)S(1)}, f32[1536]{0:T(1024)}, u32[]{:S(2)}) copy-start(f32[1536]{0:T(1024)} %copy-done.40) | copy-start | bytes 18436
  562.5 34.7 %copy-start.46 = (f32[256]{0:T(256)S(1)}, f32[256]{0:T(256)}, u32[]{:S(2)}) copy-start(f32[256]{0:T(256)} %copy-done.45) | copy-start | bytes 3076
  565.4 55.4 %all-to-all-start.2 = ((bf16[128,24,128]{2,1,0:T(8,128)(2,1)}), bf16[128,24,128]{2,1,0:T(8,128)(2,1)S(1)}, u32[]{:S(2)}, u32[]{:S(2)}) async-start(bf16[128,24,128]{2,1,0:T(8,128)(2,1)} %copy.304), calls=%async_computation.2 | async-start | bytes 1572864 | tf_op jit(solution)/shard_map/all_to_all | solution.py:286
  596.8 185.8 %reduce-scatter.7.cloned.1.call-start = ((), (), s32[]{:S(2)}) async-start(), calls=%async_computation.13 | async-start | bytes 245760 | tf_op jit(solution)/shard_map/reduce_scatter | solution.py:54
  604.3 93.7 %copy-start.17 = (bf16[256,1536]{1,0:T(8,128)(2,1)S(1)}, bf16[256,1536]{1,0:T(8,128)(2,1)}, u32[]{:S(2)}) copy-start(bf16[256,1536]{1,0:T(8,128)(2,1)} %copy-done.14) | copy-start | bytes 2359300
  604.3 93.7 %copy-start.28 = (bf16[1024,8]{1,0:T(8,128)(2,1)S(1)}, bf16[1024,8]{1,0:T(8,128)(2,1)}, u32[]{:S(2)}) copy-start(bf16[1024,8]{1,0:T(8,128)(2,1)} %copy-done.27) | copy-start | bytes 49156
  604.3 93.7 %copy-start.34 = (bf16[256,1536]{1,0:T(8,128)(2,1)S(1)}, bf16[256,1536]{1,0:T(8,128)(2,1)}, u32[]{:S(2)}) copy-start(bf16[256,1536]{1,0:T(8,128)(2,1)} %copy-done.32) | copy-start | bytes 2359300
  620.7 160.0 %all-to-all-start.4 = ((bf16[128,24,128]{2,1,0:T(8,128)(2,1)}), bf16[128,24,128]{2,1,0:T(8,128)(2,1)S(1)}, u32[]{:S(2)}, u32[]{:S(2)}) async-start(bf16[128,24,128]{2,1,0:T(8,128)(2,1)} %copy.323), calls=%async_computation.4 | async-start | bytes 1572864 | tf_op jit(solution)/shard_map/all_to_all | solution.py:286
  627.1 155.5 %reduce-scatter.11.cloned.1.call-start = ((), (), s32[]{:S(2)}) async-start(), calls=%async_computation.15 | async-start | bytes 921600 | tf_op jit(solution)/shard_map/reduce_scatter | solution.py:54
  781.3 13.0 %copy-start.1 = (bf16[2,128,1,1536]{3,1,2,0:T(8,128)(2,1)S(1)}, bf16[2,128,1,1536]{3,1,2,0:T(8,128)(2,1)}, u32[]{:S(2)}) copy-start(bf16[2,128,1,1536]{3,1,2,0:T(8,128)(2,1)} %param.19) | copy-start | bytes 2359300
  (17 other events, 26.2 us)
Sparse Core Ops, SparseCore 0:
  34.1 63.0 all-gather.2
  99.6 89.7 all-gather.4
  505.2 82.5 reduce-scatter.4
  591.5 106.4 reduce-scatter.8
  700.5 21.9 reduce-scatter.6
  724.9 28.1 reduce-scatter.10

commit v2 on v1

v2 whole, which is shorter than its diff:
```python
import math

import jax
import jax.numpy as jnp
import numpy as np
from jax import lax
from jax.sharding import Mesh
from jax.sharding import PartitionSpec as P

QUERY_HEAD_COUNT = 12
KEY_VALUE_HEADS = 4
HEAD_SIZE = 128
GROUP = QUERY_HEAD_COUNT // KEY_VALUE_HEADS
CAP = 128
EPS = 1e-06
DP = ("x", "z1", "z0", "y", "c")
EVERY = ("x", "z1", "z0", "y", "c", "zh")
F32 = jnp.float32
BF16 = jnp.bfloat16


def dot(left, right, contract, out=F32):
    result = lax.dot_general(
        left, right, (((contract[0],), (contract[1],)), ((), ())), preferred_element_type=F32
    )
    return result.astype(out)


def swapped(value, axis, bit=1):
    return lax.ppermute(value, axis, [(i, i ^ bit) for i in range(lax.axis_size(axis))])


def whole_rows(own):
    pair = jnp.concatenate([own, swapped(own, "z0")], axis=0)
    return jnp.concatenate([pair, swapped(pair, "c")], axis=0)


def rows_back(part):
    half = part.shape[0] // 2
    both = part[:half].astype(F32) + swapped(part[half:], "c").astype(F32)
    quarter = half // 2
    sent = swapped(both[quarter:].astype(BF16), "z0")
    return both[:quarter] + sent.astype(F32)


def z_routes():
    wide = lax.axis_size("z1")
    found = []
    for k1 in range(wide):
        for k2 in range(2):
            pairs = []
            for z1 in range(wide):
                for z0 in range(2):
                    for zh in range(2):
                        goal = ((z1 ^ k1) * 2 + zh) * 2 + (z0 ^ k2)
                        pairs.append(((z1 * 2 + z0) * 2 + zh, goal))
            found.append(pairs)
    return found


def z_gathered(shard):
    return jnp.concatenate(
        [lax.ppermute(shard, ("z1", "z0", "zh"), pairs) for pairs in z_routes()], axis=0
    )


def z_scattered(near):
    routes = z_routes()
    pieces = near.reshape(len(routes), -1, near.shape[1])
    total = 0.0
    for piece, pairs in zip(pieces, routes):
        back = [(goal, start) for start, goal in pairs]
        total = total + lax.ppermute(piece, ("z1", "z0", "zh"), back).astype(F32)
    return total.astype(BF16)


def xy_gathered(near):
    return lax.all_gather(near, ("x", "y"), axis=0, tiled=True)


def xy_scattered(total):
    return lax.psum_scatter(total, ("x", "y"), scatter_dimension=0, tiled=True)


def xy_scattered_apart(total):
    count = lax.axis_size(("x", "y"))
    pieces = total.reshape(count, -1, total.shape[1])
    got = lax.all_to_all(pieces, ("x", "y"), 0, 0, tiled=True)
    return jnp.sum(got.astype(F32), axis=0).astype(BF16)


def summed_everywhere(value):
    for axis in EVERY:
        bit = 1
        while bit < lax.axis_size(axis):
            value = value + swapped(value, axis, bit)
            bit *= 2
    return value


def silu_slope(value):
    sigma = jax.nn.sigmoid(value)
    return sigma * (1.0 + value * (1.0 - sigma))


def attention_scores(query, key):
    scaled = jnp.einsum("slgd,smd->sglm", query, key, preferred_element_type=F32) * (
        1.0 / math.sqrt(HEAD_SIZE)
    )
    place = jnp.arange(query.shape[1], dtype=jnp.int32)
    return jnp.where(place[None, :] <= place[:, None], scaled, -1e30)


def on_device(
    tokens,
    cotangent,
    lengths,
    perm,
    routes,
    gain_attn,
    gain_ffn,
    query_matrix,
    key_matrix,
    value_matrix,
    w_out,
    w_router,
    w_gate,
    w_up,
    w_down,
    s_gate,
    s_up,
    s_down,
):
    t = lax.axis_index("zh")
    place_here = lax.axis_index(DP)
    side_x, side_z1, side_z0, side_y = (lax.axis_size(a) for a in ("x", "z1", "z0", "y"))
    side_zl = side_z1 * side_z0
    flips = (lax.axis_index("z1"), t)
    batches, seqs = tokens.shape[0], tokens.shape[1]
    seq_len = lax.axis_size(DP)
    width = tokens.shape[3]
    experts = w_gate.shape[0]
    rows_here = query_matrix.shape[0]

    def halves(value):
        cols = value.shape[-1] // 2
        return value[..., :cols], value[..., cols:]

    def by_row(value):
        return jnp.concatenate([value[e] for e in range(experts)], axis=1)

    attn_parts = [halves(v) for v in (query_matrix, key_matrix, value_matrix, w_out.T)]
    ffn_parts = [
        tuple(by_row(v) for v in halves(w_gate)),
        halves(s_gate),
        tuple(by_row(v) for v in halves(w_up)),
        halves(s_up),
        tuple(by_row(v) for v in halves(jnp.swapaxes(w_down, 1, 2))),
        halves(s_down.T),
    ]
    attn_cols = sum(p[0].shape[1] for p in attn_parts)
    both_shards = jnp.stack(
        [jnp.concatenate([p[c] for p in attn_parts + ffn_parts], axis=1) for c in (0, 1)]
    )
    chip_rows = lax.all_to_all(both_shards, "c", 0, 0, tiled=True)
    chip_rows = chip_rows.reshape(2 * rows_here, -1)
    near = z_gathered(chip_rows)
    attn_w = xy_gathered(near[:, :attn_cols])
    ffn_w = xy_gathered(near[:, attn_cols:])
    q_cols = query_matrix.shape[1] // 2
    k_cols = key_matrix.shape[1] // 2
    qkv_cols = q_cols + 2 * k_cols
    qkv_w, out_w = attn_w[:, :qkv_cols], attn_w[:, qkv_cols:]
    hidden_e = w_gate.shape[2] // 2
    hidden = experts * hidden_e + s_gate.shape[1] // 2
    up_w, down_w = ffn_w[:, : 2 * hidden], ffn_w[:, 2 * hidden :]

    def flipped(value, axes):
        for axis, flip in zip(axes, flips):
            value = jnp.where(flip == 1, jnp.flip(value, axis), value)
        return value

    def to_local(value):
        parts = value.reshape(-1, side_x, side_z1, side_z0, side_y, width // (seq_len // 2))
        return flipped(jnp.transpose(parts, (0, 1, 4, 2, 3, 5)), (3, 4)).reshape(value.shape)

    def to_natural(value):
        parts = value.reshape(-1, side_x, side_y, side_z1, side_z0, width // (seq_len // 2))
        return jnp.transpose(flipped(parts, (3, 4)), (0, 1, 3, 4, 2, 5)).reshape(value.shape)

    unit = width // (seq_len // 2)
    iota = jnp.arange(width, dtype=jnp.int32)
    piece = iota // unit
    zl_of = (piece % side_zl) ^ (flips[0] * 2 + flips[1])
    mate = (
        ((piece // (side_zl * side_y)) * side_zl + zl_of) * side_y + (piece // side_zl) % side_y
    ) * unit + iota % unit
    features = (iota[:, None] == mate[None, :]).astype(BF16)

    order = lax.dynamic_index_in_dim(perm, t, 1, False)
    deal = (order[:, :, None] == jnp.arange(seqs, dtype=jnp.int32)[None, None, :]).astype(BF16)
    own_routes = lax.dynamic_slice_in_dim(routes[:, :, 0], t * seqs, seqs, 1)
    own_lengths = lax.dynamic_slice_in_dim(lengths, t * seqs, seqs, 1)
    own_valid = place_here < own_lengths
    named = jnp.any(
        own_routes[:, :, :, None] == jnp.arange(experts, dtype=jnp.int32), axis=2
    )
    marks = jnp.concatenate(
        [jnp.logical_and(named, own_valid[:, :, None]), own_valid[:, :, None]], axis=2
    ).astype(BF16)
    marks = jnp.pad(marks, ((0, 0), (0, 0), (0, 128 - marks.shape[2])))
    rows_in = jnp.concatenate([tokens[:, :, 0], marks, cotangent[:, :, 0]], axis=2)
    sent = jnp.einsum("mjs,msd->jmd", deal, rows_in, preferred_element_type=F32)
    sent = sent.astype(BF16).reshape(seqs, -1, 128)
    got = lax.all_to_all(sent, DP, 0, 0, tiled=True).reshape(seq_len, batches, -1)
    own_in = jnp.swapaxes(got, 0, 1)
    x_own = dot(own_in[:, :, :width].reshape(batches * seq_len, width), features, (1, 0))
    own_marks = own_in[:, :, width : width + 128]
    own_hits = own_marks[:, :, :experts]
    own_keep = own_marks[:, :, experts].reshape(-1, 1).astype(F32)
    gy_own = own_keep * dot(
        own_in[:, :, width + 128 :].reshape(batches * seq_len, width), features, (1, 0)
    )

    place = jnp.arange(seq_len, dtype=jnp.int32)
    earlier = (place[None, :] < place[:, None]).astype(BF16)
    before = jnp.einsum("pq,mqe->mpe", earlier, own_hits, preferred_element_type=F32)
    totals = jnp.sum(own_hits.astype(F32), axis=1)
    other_totals = swapped(totals, "zh")
    rank = before + jnp.where(t == 1, other_totals, 0.0)[:, None, :]
    own_kept = jnp.where(rank < CAP, own_hits, jnp.zeros_like(own_hits))
    flags = jnp.concatenate([own_hits, own_kept], axis=2).reshape(batches * seq_len, -1)
    flags = jnp.pad(flags, ((0, 0), (0, 128 - flags.shape[1])))

    small_in = to_local(
        jnp.concatenate([gain_attn[None], gain_ffn[None], w_router.T.astype(F32)], axis=0)
    )
    gain_a, gain_f, router = small_in[0:1], small_in[1:2], small_in[2:].astype(BF16)
    scale_attn = lax.rsqrt(jnp.mean(x_own * x_own, axis=-1, keepdims=True) + EPS)
    unit_attn = x_own * scale_attn
    n1 = whole_rows((unit_attn * gain_a).astype(BF16))
    gy_own_low = jnp.concatenate([gy_own.astype(BF16), flags], axis=1)
    n1, gy_own_low = lax.optimization_barrier((n1, gy_own_low))
    both = whole_rows(gy_own_low)
    gy, flags_all = both[:, :width], both[:, width:]
    rows = n1.shape[0]
    count = rows // seq_len
    qkv = dot(n1, qkv_w, (1, 0), BF16)
    query = qkv[:, :q_cols].reshape(count, seq_len, GROUP, HEAD_SIZE)
    key = qkv[:, q_cols : q_cols + k_cols].reshape(count, seq_len, HEAD_SIZE)
    value = qkv[:, q_cols + k_cols :].reshape(count, seq_len, HEAD_SIZE)
    scores = attention_scores(query, key)
    log_total = jax.nn.logsumexp(scores, axis=-1, keepdims=True)
    probs = jnp.exp(scores - log_total)
    probs_low = probs.astype(BF16)
    mixed = jnp.einsum("sglm,smd->slgd", probs_low, value, preferred_element_type=F32)
    mixed = mixed.astype(BF16).reshape(rows, q_cols)
    h_own = x_own + rows_back(dot(mixed, out_w, (1, 1), BF16))

    scale_ffn = lax.rsqrt(jnp.mean(h_own * h_own, axis=-1, keepdims=True) + EPS)
    unit_ffn = h_own * scale_ffn
    n2 = whole_rows((unit_ffn * gain_f).astype(BF16))
    logits = dot(n2, router, (1, 1))
    named_all = flags_all[:, :experts] > 0
    kept = flags_all[:, experts : 2 * experts] > 0
    top = jnp.max(jnp.where(named_all, logits, -1e30), axis=1, keepdims=True)
    powers = jnp.where(named_all, jnp.exp(jnp.where(named_all, logits - top, 0.0)), 0.0)
    gates = powers / jnp.maximum(jnp.sum(powers, axis=1, keepdims=True), 1e-30)
    kept_gates = jnp.where(kept, gates, 0.0)

    def spread(per_expert):
        wide = jnp.broadcast_to(per_expert[:, :, None], (rows, experts, hidden_e))
        return jnp.concatenate(
            [wide.reshape(rows, -1), jnp.ones((rows, hidden - experts * hidden_e), F32)], axis=1
        )

    weight = spread(kept_gates)
    ab = dot(n2, up_w, (1, 0))
    a, b = ab[:, :hidden], ab[:, hidden:]
    silu_a = jax.nn.silu(a)
    inner = (silu_a * b).astype(BF16)
    weighted = (weight * inner.astype(F32)).astype(BF16)
    dhid = dot(gy, down_w, (1, 0))
    dgates = jnp.sum(
        (inner.astype(F32) * dhid)[:, : experts * hidden_e].reshape(rows, experts, hidden_e), axis=2
    )
    dgates = jnp.where(kept, dgates, 0.0)
    dlogits = gates * (dgates - jnp.sum(gates * dgates, axis=1, keepdims=True))
    dlogits = dlogits.astype(BF16)
    dinner = weight * dhid
    dab = jnp.concatenate(
        [(dinner * b * silu_slope(a)).astype(BF16), (dinner * silu_a).astype(BF16)], axis=1
    )
    dn2_part = (dot(dab, up_w, (1, 1)) + dot(dlogits, router, (1, 0))).astype(BF16)
    big_ffn = jnp.concatenate(
        [dot(n2, dab, (0, 0), BF16), dot(gy, weighted, (0, 0), BF16)], axis=1
    )
    out_part = dot(weighted, down_w, (1, 1), BF16)
    small_router = dot(dlogits, n2, (0, 0))
    small_ffn = jnp.sum(dn2_part.astype(F32) * n2.astype(F32), axis=0, keepdims=True) / gain_f
    dn2 = rows_back(dn2_part)
    dn2, big_ffn, out_part = lax.optimization_barrier((dn2, big_ffn, out_part))
    near_ffn = xy_scattered(big_ffn)
    scaled = dn2 * gain_f
    dh = gy_own + scale_ffn * (
        scaled - unit_ffn * jnp.mean(scaled * unit_ffn, axis=-1, keepdims=True)
    )

    dattn = whole_rows(dh.astype(BF16))
    dmixed = dot(dattn, out_w, (1, 0), BF16)
    big_out = dot(dattn, mixed, (0, 0), BF16)
    dheads = dmixed.reshape(count, seq_len, GROUP, HEAD_SIZE)
    dprobs = jnp.einsum("slgd,smd->sglm", dheads, value, preferred_element_type=F32)
    dscores = (probs * (dprobs - jnp.sum(probs * dprobs, axis=-1, keepdims=True))).astype(BF16)
    root = 1.0 / math.sqrt(HEAD_SIZE)
    dq = jnp.einsum("sglm,smd->slgd", dscores, key, preferred_element_type=F32) * root
    dk = jnp.einsum("sglm,slgd->smd", dscores, query, preferred_element_type=F32) * root
    dv = jnp.einsum("sglm,slgd->smd", probs_low, dheads, preferred_element_type=F32)
    dqkv = jnp.concatenate(
        [
            dq.astype(BF16).reshape(rows, -1),
            dk.astype(BF16).reshape(rows, -1),
            dv.astype(BF16).reshape(rows, -1),
        ],
        axis=1,
    )
    dn1_part = dot(dqkv, qkv_w, (1, 1), BF16)
    big_attn = jnp.concatenate([dot(n1, dqkv, (0, 0), BF16), big_out], axis=1)
    near_attn = xy_scattered_apart(big_attn)
    small_attn = jnp.sum(dn1_part.astype(F32) * n1.astype(F32), axis=0, keepdims=True) / gain_a
    small = jnp.concatenate([small_attn, small_ffn, small_router], axis=0)
    final = summed_everywhere(to_natural(small))
    dn1 = rows_back(dn1_part)
    scaled = dn1 * gain_a
    dx_own = dh + scale_attn * (
        scaled - unit_attn * jnp.mean(scaled * unit_attn, axis=-1, keepdims=True)
    )
    dx_own = dx_own.astype(BF16)

    def returned(own):
        natural = dot(own, features, (1, 1), BF16).reshape(batches, seq_len, -1)
        sent = jnp.swapaxes(natural, 0, 1).reshape(seq_len, -1, 128)
        got = lax.all_to_all(sent, DP, 0, 0, tiled=True).reshape(seqs, batches, -1)
        back = jnp.einsum("mjs,jmd->msd", deal, got, preferred_element_type=F32)
        return back.astype(BF16)[:, :, None]

    branch = rows_back(out_part)
    out_own = (own_keep * (h_own + branch)).astype(BF16)
    out_tokens = returned(out_own)
    grad_tokens = returned(dx_own)

    def exchanged(near_grads):
        chip = z_scattered(near_grads).reshape(2, rows_here, -1)
        return lax.all_to_all(chip, "c", 0, 0, tiled=True).astype(F32)

    mine = jnp.concatenate([exchanged(near_attn), exchanged(near_ffn)], axis=2)

    def join(start, cols):
        part = mine[:, :, start : start + cols]
        return jnp.swapaxes(part, 0, 1).reshape(rows_here, 2 * cols)

    def join_experts(start):
        part = mine[:, :, start : start + experts * hidden_e]
        part = part.reshape(2, rows_here, experts, hidden_e)
        return jnp.transpose(part, (2, 1, 0, 3)).reshape(experts, rows_here, 2 * hidden_e)

    shared_cols = s_gate.shape[1] // 2
    ffn_at = attn_cols
    each = experts * hidden_e
    return (
        out_tokens,
        grad_tokens,
        final[0],
        final[1],
        join(0, q_cols),
        join(q_cols, k_cols),
        join(q_cols + k_cols, k_cols),
        join(qkv_cols, q_cols).T,
        final[2:].T,
        join_experts(ffn_at),
        join_experts(ffn_at + hidden),
        jnp.swapaxes(join_experts(ffn_at + 2 * hidden), 1, 2),
        join(ffn_at + each, shared_cols),
        join(ffn_at + hidden + each, shared_cols),
        join(ffn_at + 2 * hidden + each, shared_cols).T,
    )


def solution(mesh):
    devices = np.asarray(mesh.devices)
    side = round((devices.shape[0] // 2) ** (1 / 3))
    fine = Mesh(devices.reshape(side, side // 2, 2, side, 2, 2), EVERY)
    rows, cols = P(DP, "zh"), P("zh", DP)
    seqs = P(None, "zh", DP, None)
    return jax.shard_map(
        on_device,
        mesh=fine,
        in_specs=(
            seqs,
            seqs,
            P(),
            P(),
            P(None, None, DP, None),
            P(),
            P(),
            rows,
            rows,
            rows,
            cols,
            P(),
            P(None, DP, "zh"),
            P(None, DP, "zh"),
            P(None, "zh", DP),
            rows,
            rows,
            cols,
        ),
        out_specs=(
            seqs,
            seqs,
            P(),
            P(),
            rows,
            rows,
            rows,
            cols,
            P(),
            P(None, DP, "zh"),
            P(None, DP, "zh"),
            P(None, "zh", DP),
            rows,
            rows,
            cols,
        ),
        check_vma=False,
    )
```

time: 805 us -> 645 us (0.80)
  waiting for transfers between devices: 343 us -> 226 us
  blocking collectives: 114 us -> 16.6 us
  local copies, waits for them, and re-layouts: 62.4 us -> 86.2 us
  other arithmetic: 43.6 us -> 59.4 us
    psum x1 -> x0, blocking collectives: 76.8 us -> none  [on_device(): small = lax.psum(small, EVERY)]
    reduce_scatter x4 -> x1, waiting for transfers between devices: 70.9 us -> 0.02 us  [xy_scattered(): return lax.psum_scatter(total, ('x', 'y'), scatter_dimension=0, tiled=True)]
    ppermute x16 -> x37, waiting for transfers between devices: 203 us -> 167 us  [the longest x25 144 us: swapped(): lax.ppermute(value, axis, [(i, i ^ bit) for i in range(lax.axis_size(axis...]
    ppermute x16 -> x37, starting transfers between devices: 34.6 us -> 64.4 us  [the longest x25 37.5 us: swapped(): lax.ppermute(value, axis, [(i, i ^ bit) for i in range(lax.axis_size(axis...]
    all_gather x2 -> x0, blocking collectives: 26.1 us -> none  [gathered(): near = lax.all_gather(shard, 'zl', axis=0, tiled=True)]
    all_to_all x2, starting transfers between devices: 37.8 us -> 17.7 us  [returned(): got = lax.all_to_all(sent, DP, 0, 0, tiled=True).reshape(seqs, batches, -1)]
    all_to_all x2, waiting for transfers between devices: 55.2 us -> 42.8 us  [the longest x1 42.8 us: on_device(): lax.all_to_all(sent, DP, 0, 0, tiled=True).reshape(seq_len, batches, -1)]
    concatenate x2 -> x12, local copies, waits for them, and re-layouts: 0.05 us -> 9.15 us  [the longest x1 4.67 us: on_device(): big_attn = jnp.concatenate([dot(n1, dqkv, (0, 0), BF16), big_out], axis=1)]
  transfers between devices with their start and end apart: 26 -> 44, of which waited for: 14 -> 21; matrix products, arithmetic and copies ran while one was open for 16% -> 29% of each run, Pallas kernels for 0% -> 0%
where the time goes in v2:
time: 645 us; the launch traced here: 634 us
  waiting for transfers between devices  226 us (35%)
  matrix products  125 us (19%)
  starting transfers between devices  105 us (16%)
  local copies, waits for them, and re-layouts  86.2 us (13%)
  other arithmetic  59.4 us (9%)
  blocking collectives  16.6 us (3%)
  between operations  15.8 us (2%)
    ppermute x25, waiting for transfers between devices, swapped(): lax.ppermute(value, axis, [(i, i ^ bit) for i in range(lax.axis_size(axis...  144 us
    dot_general x19, matrix products, dot(): lax.dot_general(left, right, (((contract[0],), (contract[1],)), ((), ()))...  114 us
    all_to_all x1, waiting for transfers between devices, on_device(): lax.all_to_all(sent, DP, 0, 0, tiled=True).reshape(seq_len, batches, -1)  42.8 us
    ppermute x25, starting transfers between devices, swapped(): lax.ppermute(value, axis, [(i, i ^ bit) for i in range(lax.axis_size(axis...  37.5 us
    unnamed x198, local copies, waits for them, and re-layouts  27.1 us
    all_to_all x1, starting transfers between devices, on_device(): lax.all_to_all(sent, DP, 0, 0, tiled=True).reshape(seq_len, batches, -1)  18.2 us
    ppermute x4, waiting for transfers between devices, z_gathered(): lax.ppermute(shard, ('z1', 'z0', 'zh'), pairs)  18 us
    all_to_all x2, starting transfers between devices, returned(): got = lax.all_to_all(sent, DP, 0, 0, tiled=True).reshape(seqs, batches, -1)  17.7 us
  transfers between devices with their start and end apart: 44, of which 21 were waited for; matrix products, arithmetic and copies ran while one was open for 29% of the time, Pallas kernels for 0%

profile of v2, /device:TPU:1, one launch (start us, length us, event | category | flops | bytes accessed | tf_op | source)
XLA Modules:
  0.0 634.0 jit_solution(10063231581099115957)
XLA Ops:
  16.3 7.0 %all_to_all.35 = bf16[2,12,4864]{2,1,0:T(8,128)(2,1)S(1)} all-to-all(bf16[2,12,4864]{2,1,0:T(8,128)(2,1)S(1)} %pad_maximum_fusion.18), channel_id=1, replica_groups=mesh['x'=4,'z1'=2,'z0'=2,'y'=4,'c'=2,'zh'=2] {'c'}, dimensions={0} | all-to-all | bytes 466944 | tf_op jit(solution)/shard_map/all_to_all | solution.py:165
  24.2 6.3 collective-permute-start.6
  31.0 3.4 collective-permute-start.4
  34.4 18.0 %collective-permute-done.4 = bf16[24,4864]{1,0:T(8,128)(2,1)S(1)} collective-permute-done((bf16[24,4864]{1,0:T(8,128)(2,1)S(1)}, bf16[24,4864]{1,0:T(8,128)(2,1)S(1)}, u32[]{:S(2)}, u32[]{:S(2)}) %collective-permute-start.4) | collective-permute-done | bytes 233504 | tf_op jit(solution)/shard_map/ppermute | solution.py:63
  57.8 2.8 copy.303
  60.6 18.2 %all-to-all-start = ((bf16[128,50,128]{2,1,0:T(8,128)(2,1)}), bf16[128,50,128]{2,1,0:T(8,128)(2,1)S(1)}, u32[]{:S(2)}, u32[]{:S(2)}) async-start(bf16[128,50,128]{2,1,0:T(8,128)(2,1)} %copy.303), calls=%async_computation | async-start | bytes 3670016 | tf_op jit(solution)/shard_map/all_to_all | solution.py:215
  82.5 42.8 %all-to-all-done = bf16[128,50,128]{2,1,0:T(8,128)(2,1)S(1)} async-done(((bf16[128,50,128]{2,1,0:T(8,128)(2,1)}), bf16[128,50,128]{2,1,0:T(8,128)(2,1)S(1)}, u32[]{:S(2)}, u32[]{:S(2)}) %all-to-all-start) | async-done | bytes 1638432 | tf_op jit(solution)/shard_map/all_to_all | solution.py:215
  132.5 17.9 %collective-permute-done = bf16[256,1536]{1,0:T(8,128)(2,1)S(1)} collective-permute-done((bf16[256,1536]{1,0:T(8,128)(2,1)S(1)}, bf16[256,1536]{1,0:T(8,128)(2,1)S(1)}, u32[]{:S(2)}, u32[]{:S(2)}) %collective-permute-start) | collective-permute-done | bytes 786464 | tf_op jit(solution)/shard_map/ppermute | solution.py:30
  153.9 3.4 collective-permute-start.2
  159.6 4.6 fusion.127
  166.7 3.6 pad_maximum_fusion.4
  170.2 5.1 fusion.37
  177.6 3.4 convolution_convert_fusion.4
  181.6 3.0 collective-permute-done.7
  189.0 16.8 %collective-permute-done.8 = bf16[256,1536]{1,0:T(8,128)(2,1)} collective-permute-done((bf16[256,1536]{1,0:T(8,128)(2,1)S(1)}, bf16[256,1536]{1,0:T(8,128)(2,1)}, u32[]{:S(2)}, u32[]{:S(2)}) %collective-permute-start.8) | collective-permute-done | bytes 786464 | tf_op jit(solution)/shard_map/ppermute | solution.py:30
  205.8 2.5 multiply_reduce_fusion.4
  209.2 14.7 %collective-permute-done.9 = bf16[256,1664]{1,0:T(8,128)(2,1)S(1)} collective-permute-done((bf16[256,1664]{1,0:T(8,128)(2,1)}, bf16[256,1664]{1,0:T(8,128)(2,1)S(1)}, u32[]{:S(2)}, u32[]{:S(2)}) %collective-permute-start.9) | collective-permute-done | bytes 852000 | tf_op jit(solution)/shard_map/ppermute | solution.py:30
  223.9 2.8 pad_maximum_fusion.8
  228.7 12.1 %collective-permute-done.11 = bf16[256,1536]{1,0:T(8,128)(2,1)S(1)} collective-permute-done((bf16[256,1536]{1,0:T(8,128)(2,1)S(1)}, bf16[256,1536]{1,0:T(8,128)(2,1)S(1)}, u32[]{:S(2)}, u32[]{:S(2)}) %collective-permute-start.11) | collective-permute-done | bytes 786464 | tf_op jit(solution)/shard_map/ppermute | solution.py:30
  249.5 3.6 select_reduce_fusion
  255.1 3.1 copy.573
  258.2 14.2 %fusion.6 = f32[1024,2560]{1,0:T(8,128)} fusion(bf16[1536,3840]{1,0:T(8,128)(2,1)} %all-gather.5.cloned.1.call-done, bf16[512,1536]{1,0:T(8,128)(2,1)} %collective-permute-done.12, bf16[256,1536]{1,0:T(8,128)(2,1)} %copy-done.36, bf16[256,1536]{1,0:T(8,128)(2,1)} %copy-done.17), kind=kOutput, calls=%fused_computation.10 | convolution fusion | flops 8062500864 | bytes 21495808 | tf_op jit(solution)/shard_map/dot_general | solution.py:23
  272.4 13.6 %multiply_convert_fusion.2 = (bf16[1024,1280]{1,0:T(8,128)(2,1)}, bf16[1024,1280]{1,0:T(8,128)(2,1)}, bf16[1024,1280]{1,0:T(8,128)(2,1)}, f32[1024,1280]{1,0:T(8,128)}, f32[1024,1280]{1,0:T(8,128)}) fusion(f32[1024,2560]{1,0:T(8,128)} %fusion.6, f32[1024,1024]{1,0:T(8,128)S(1)} %bitcast.403, bf16[1536,3840]{1,0:T(8,128)(2,1)} %all-gather.5.cloned.1.call-done, ...), kind=kOutput, calls=%fused_computation.21 | convolution fusion | flops 4051435520 | bytes 40108032 | tf_op jit(solution)/shard_map/dot_general | solution.py:23
  285.9 4.4 fusion.16
  290.3 2.9 copy.441
  293.3 4.2 reduce_sum.129
  302.3 14.3 %multiply_reduce_fusion = (f32[1536]{0:T(1024)S(1)}, bf16[1024,1536]{1,0:T(8,128)(2,1)}) fusion(bf16[512,1536]{1,0:T(8,128)(2,1)} %collective-permute-done.12, bf16[256,1536]{1,0:T(8,128)(2,1)} %copy-done.36, bf16[256,1536]{1,0:T(8,128)(2,1)} %copy-done.17, f32[1024,1536]{1,0:T(8,128)S(1)} %fusion.129, bf16[1536,3840]{1,0:T(8,128)(2,1)} %all-gather.5.cloned.1.call-done, ...), kind=kOutput, calls=%fused_computation.12 | convolution fusion | flops 8080849408 | bytes 25696256 | tf_op jit(solution)/shard_map/dot_general | solution.py:23
  316.6 2.8 slice.576
  319.4 11.5 %convolution_convert_fusion = bf16[1536,2560]{1,0:T(8,128)(2,1)S(1)} fusion(bf16[1024,1280]{1,0:T(8,128)(2,1)} %get-tuple-element.109, bf16[1024,1280]{1,0:T(8,128)(2,1)} %get-tuple-element.108, bf16[512,1536]{1,0:T(8,128)(2,1)} %collective-permute-done.12, bf16[256,1536]{1,0:T(8,128)(2,1)S(1)} %copy-done.38, bf16[256,1536]{1,0:T(8,128)(2,1)S(1)} %copy-done.19), kind=kOutput, calls=%fused_computation.1 | convolution fusion | flops 8076918784 | bytes 16252928 | tf_op jit(solution)/shard_map/dot_general | solution.py:23
  331.0 6.3 convolution_convert_fusion.1
  337.3 4.8 pad_maximum_fusion
  342.1 2.5 convert_add_fusion.2
  345.3 8.1 %convolution_convert_fusion.5 = bf16[1024,1536]{1,0:T(8,128)(2,1)} fusion(bf16[1024,1280]{1,0:T(8,128)(2,1)S(1)} %copy-done.63, bf16[1536,3840]{1,0:T(8,128)(2,1)} %all-gather.5.cloned.1.call-done), kind=kOutput, calls=%fused_computation.34 | convolution fusion | flops 4028104704 | bytes 9699328 | tf_op jit(solution)/shard_map/dot_general | solution.py:23
  353.4 10.0 %collective-permute-done.14 = bf16[256,1536]{1,0:T(8,128)(2,1)S(1)} collective-permute-done((bf16[256,1536]{1,0:T(8,128)(2,1)S(1)}, bf16[256,1536]{1,0:T(8,128)(2,1)S(1)}, u32[]{:S(2)}, u32[]{:S(2)}) %collective-permute-start.14) | collective-permute-done | bytes 786464 | tf_op jit(solution)/shard_map/ppermute | solution.py:30
  369.3 17.3 %collective-permute-done.17 = bf16[256,1536]{1,0:T(8,128)(2,1)S(1)} collective-permute-done((bf16[256,1536]{1,0:T(8,128)(2,1)S(1)}, bf16[256,1536]{1,0:T(8,128)(2,1)S(1)}, u32[]{:S(2)}, u32[]{:S(2)}) %collective-permute-start.17) | collective-permute-done | bytes 786464 | tf_op jit(solution)/shard_map/ppermute | solution.py:30
  393.5 2.8 slice.508
  396.3 4.6 convolution_convert_fusion.10
  401.0 3.2 reshape.380
  404.2 2.4 fusion.52
  414.1 3.2 convolution_convert_fusion.7
  421.5 4.7 copy.370
  426.2 4.8 all-to-all-start.4
  431.0 6.2 multiply_reduce_fusion.1
  442.1 3.4 rev.17
  448.4 33.0 %collective-permute-done.21 = f32[10,1536]{1,0:T(8,128)S(1)} collective-permute-done((f32[10,1536]{1,0:T(8,128)}, f32[10,1536]{1,0:T(8,128)S(1)}, u32[]{:S(2)}, u32[]{:S(2)}) %collective-permute-start.21) | collective-permute-done | bytes 61472 | tf_op jit(solution)/shard_map/ppermute | solution.py:30
  482.3 8.5 %collective-permute-start.22 = (f32[10,1536]{1,0:T(8,128)S(1)}, f32[10,1536]{1,0:T(8,128)S(1)}, u32[]{:S(2)}, u32[]{:S(2)}) collective-permute-start(f32[10,1536]{1,0:T(8,128)S(1)} %add.246), channel_id=1, source_target_pairs={{0,128},{64,192},{128,0},{192,64},{1,129},{65,193},{129,1},{193,65... | collective-permute-start | bytes 184328 | tf_op jit(solution)/shard_map/ppermute | solution.py:30
  492.9 5.4 collective-permute-done.23
  498.4 3.5 collective-permute-done.24
  502.3 2.6 convert_add_fusion.1
  505.6 5.0 collective-permute-done.26
  510.5 5.7 collective-permute-start.27
  517.9 3.6 collective-permute-start.28
  527.3 3.2 fusion.24
  534.4 8.1 %all-to-all-start.2 = ((bf16[128,24,128]{2,1,0:T(8,128)(2,1)}), bf16[128,24,128]{2,1,0:T(8,128)(2,1)S(1)}, u32[]{:S(2)}, u32[]{:S(2)}) async-start(bf16[128,24,128]{2,1,0:T(8,128)(2,1)} %copy.353), calls=%async_computation.2 | async-start | bytes 1572864 | tf_op jit(solution)/shard_map/all_to_all | solution.py:343
  546.8 2.5 reduce_sum.138
  551.5 4.6 collective-permute-start.32
  557.1 5.3 fusion.25
  565.4 3.0 all-to-all-done.2
  568.5 5.2 all_to_all.36
  573.7 9.6 %all-to-all-start.3 = ((bf16[128,24,128]{2,1,0:T(8,128)(2,1)}), bf16[128,24,128]{2,1,0:T(8,128)(2,1)S(1)}, u32[]{:S(2)}, u32[]{:S(2)}) async-start(bf16[128,24,128]{2,1,0:T(8,128)(2,1)} %copy.366), calls=%async_computation.3 | async-start | bytes 1572864 | tf_op jit(solution)/shard_map/all_to_all | solution.py:343
  587.8 5.8 collective-permute-start.36
  598.6 13.5 %all-to-all-done.3 = bf16[128,24,128]{2,1,0:T(8,128)(2,1)S(1)} async-done(((bf16[128,24,128]{2,1,0:T(8,128)(2,1)}), bf16[128,24,128]{2,1,0:T(8,128)(2,1)S(1)}, u32[]{:S(2)}, u32[]{:S(2)}) %all-to-all-start.3) | async-done | bytes 786464 | tf_op jit(solution)/shard_map/all_to_all | solution.py:343
  613.9 4.4 collective-permute-done.35
  618.5 4.4 all_to_all.37
  (410 shorter events, 133.9 us)
Async XLA Ops:
  7.2 47.1 %copy-start = (s32[2,256,1,6]{1,2,3,0:T(1,128)S(1)}, s32[2,256,1,6]{1,2,3,0:T(1,128)}, u32[]{:S(2)}) copy-start(s32[2,256,1,6]{1,2,3,0:T(1,128)} %param.22) | copy-start | bytes 36868
  7.2 163.0 %all-gather.3.cloned.1.call-start = ((), (), s32[]{:S(2)}) async-start(), calls=%async_computation.8 | async-start | bytes 3342336 | tf_op jit(solution)/shard_map/all_gather | solution.py:78
  16.3 38.0 %copy-start.59 = (s32[2,256]{1,0:T(2,128)S(1)}, s32[2,256]{1,0:T(2,128)}, u32[]{:S(2)}) copy-start(s32[2,256]{1,0:T(2,128)} %param.20) | copy-start | bytes 6148
  16.3 38.1 %copy-start.30 = (bf16[2,128,1,1536]{3,1,2,0:T(8,128)(2,1)S(1)}, bf16[2,128,1,1536]{3,1,2,0:T(8,128)(2,1)}, u32[]{:S(2)}) copy-start(bf16[2,128,1,1536]{3,1,2,0:T(8,128)(2,1)} %param.18) | copy-start | bytes 2359300
  23.4 31.4 %copy-start.31 = (bf16[2,128,1,1536]{3,1,2,0:T(8,128)(2,1)S(1)}, bf16[2,128,1,1536]{3,1,2,0:T(8,128)(2,1)}, u32[]{:S(2)}) copy-start(bf16[2,128,1,1536]{3,1,2,0:T(8,128)(2,1)} %param.19) | copy-start | bytes 2359300
  23.4 11.0 %collective-permute-start.3 = (bf16[24,4864]{1,0:T(8,128)(2,1)S(1)}, bf16[24,4864]{1,0:T(8,128)(2,1)S(1)}, u32[]{:S(2)}, u32[]{:S(2)}) collective-permute-start(bf16[24,4864]{1,0:T(8,128)(2,1)S(1)} %reshape.333), channel_id=1, source_target_pairs={{0,0},{1,16},{16,1},{17,17},{32,32},{33,48},{48,33},{49,49},{2,2},... | collective-permute-start | bytes 700424 | tf_op jit(solution)/shard_map/ppermute | solution.py:63
  24.2 28.3 %collective-permute-start.6 = (bf16[24,4864]{1,0:T(8,128)(2,1)S(1)}, bf16[24,4864]{1,0:T(8,128)(2,1)S(1)}, u32[]{:S(2)}, u32[]{:S(2)}) collective-permute-start(bf16[24,4864]{1,0:T(8,128)(2,1)S(1)} %reshape.333), channel_id=1, source_target_pairs={{0,33},{1,49},{16,32},{17,48},{32,1},{33,17},{48,0},{49,16},{2,35}... | collective-permute-start | bytes 700424 | tf_op jit(solution)/shard_map/ppermute | solution.py:63
  30.5 21.9 %collective-permute-start.5 = (bf16[24,4864]{1,0:T(8,128)(2,1)S(1)}, bf16[24,4864]{1,0:T(8,128)(2,1)S(1)}, u32[]{:S(2)}, u32[]{:S(2)}) collective-permute-start(bf16[24,4864]{1,0:T(8,128)(2,1)S(1)} %reshape.333), channel_id=1, source_target_pairs={{0,32},{1,48},{16,33},{17,49},{32,0},{33,16},{48,1},{49,17},{2,34}... | collective-permute-start | bytes 700424 | tf_op jit(solution)/shard_map/ppermute | solution.py:63
  31.0 21.4 %collective-permute-start.4 = (bf16[24,4864]{1,0:T(8,128)(2,1)S(1)}, bf16[24,4864]{1,0:T(8,128)(2,1)S(1)}, u32[]{:S(2)}, u32[]{:S(2)}) collective-permute-start(bf16[24,4864]{1,0:T(8,128)(2,1)S(1)} %reshape.333), channel_id=1, source_target_pairs={{0,1},{1,17},{16,0},{17,16},{32,33},{33,49},{48,32},{49,48},{2,3},... | collective-permute-start | bytes 700424 | tf_op jit(solution)/shard_map/ppermute | solution.py:63
  53.2 204.9 %all-gather.5.cloned.1.call-start = ((), (), s32[]{:S(2)}) async-start(), calls=%async_computation.9 | async-start | bytes 12533760 | tf_op jit(solution)/shard_map/all_gather | solution.py:78
  57.7 21.1 %copy-start.55 = (f32[1536]{0:T(1024)S(1)}, f32[1536]{0:T(1024)}, u32[]{:S(2)}) copy-start(f32[1536]{0:T(1024)} %param.23) | copy-start | bytes 18436
  57.8 21.3 %copy-start.56 = (f32[1536]{0:T(1024)S(1)}, f32[1536]{0:T(1024)}, u32[]{:S(2)}) copy-start(f32[1536]{0:T(1024)} %param.24) | copy-start | bytes 18436
  57.8 21.4 %copy-start.50 = (bf16[1536,8]{0,1:T(8,128)(2,1)S(1)}, bf16[1536,8]{0,1:T(8,128)(2,1)}, u32[]{:S(2)}) copy-start(bf16[1536,8]{0,1:T(8,128)(2,1)} %param.29) | copy-start | bytes 73732
  60.6 64.7 %all-to-all-start = ((bf16[128,50,128]{2,1,0:T(8,128)(2,1)}), bf16[128,50,128]{2,1,0:T(8,128)(2,1)S(1)}, u32[]{:S(2)}, u32[]{:S(2)}) async-start(bf16[128,50,128]{2,1,0:T(8,128)(2,1)} %copy.303), calls=%async_computation | async-start | bytes 3670016 | tf_op jit(solution)/shard_map/all_to_all | solution.py:215
  78.8 507.0 %reduce-scatter.2.cloned.1.call-start = ((), (), s32[]{:S(2)}) async-start(), calls=%async_computation.10 | async-start | bytes 12533760 | tf_op jit(solution)/shard_map/reduce_scatter | solution.py:82
  82.5 48.5 %copy-start.48 = (f32[1536]{0:T(1024)}, f32[1536]{0:T(1024)S(1)}, u32[]{:S(2)}) copy-start(f32[1536]{0:T(1024)S(1)} %mul.227) | copy-start | bytes 18436
  82.5 77.1 %copy-start.57 = (s32[1536]{0:T(1024)}, s32[1536]{0:T(1024)S(1)}, u32[]{:S(2)}) copy-start(s32[1536]{0:T(1024)S(1)} %fusion.94) | copy-start | bytes 18436
  130.9 28.7 %copy-start.51 = (f32[256]{0:T(256)}, f32[256]{0:T(256)S(1)}, u32[]{:S(2)}) copy-start(f32[256]{0:T(256)S(1)} %add_rsqrt_fusion.1) | copy-start | bytes 3076
  132.2 18.3 %collective-permute-start = (bf16[256,1536]{1,0:T(8,128)(2,1)S(1)}, bf16[256,1536]{1,0:T(8,128)(2,1)S(1)}, u32[]{:S(2)}, u32[]{:S(2)}) collective-permute-start(bf16[256,1536]{1,0:T(8,128)(2,1)S(1)} %multiply_convert_fusion.5), channel_id=1, source_target_pairs={{0,16},{16,0},{1,17},{17,1},{2,18},{18,2},{3,19},{19,3},{4,20},{20... | collective-permute-start | bytes 2359304 | tf_op jit(solution)/shard_map/ppermute | solution.py:30
  151.8 14.9 %collective-permute-start.1 = (bf16[512,1536]{1,0:T(8,128)(2,1)}, bf16[512,1536]{1,0:T(8,128)(2,1)}, u32[]{:S(2)}, u32[]{:S(2)}) collective-permute-start(bf16[512,1536]{1,0:T(8,128)(2,1)} %pad_maximum_fusion.9), channel_id=1, source_target_pairs={{0,2},{2,0},{1,3},{3,1},{4,6},{6,4},{5,7},{7,5},{8,10},{10,8},{9,1... | collective-permute-start | bytes 4718600 | tf_op jit(solution)/shard_map/ppermute | solution.py:30
  153.9 10.3 %collective-permute-start.2 = (f32[2,8]{1,0:T(2,128)S(1)}, f32[2,8]{1,0:T(2,128)S(1)}, u32[]{:S(2)}, u32[]{:S(2)}) collective-permute-start(f32[2,8]{1,0:T(2,128)S(1)} %convert_reduce_fusion), channel_id=1, source_target_pairs={{0,1},{1,0},{2,3},{3,2},{4,5},{5,4},{6,7},{7,6},{8,9},{9,8},{10,11... | collective-permute-start | bytes 200 | tf_op jit(solution)/shard_map/ppermute | solution.py:30
  181.1 3.5 collective-permute-start.7
  186.8 18.9 %collective-permute-start.8 = (bf16[256,1536]{1,0:T(8,128)(2,1)S(1)}, bf16[256,1536]{1,0:T(8,128)(2,1)}, u32[]{:S(2)}, u32[]{:S(2)}) collective-permute-start(bf16[256,1536]{1,0:T(8,128)(2,1)S(1)} %slice.769), channel_id=1, source_target_pairs={{0,16},{16,0},{1,17},{17,1},{2,18},{18,2},{3,19},{19,3},{4,20},{20... | collective-permute-start | bytes 2359304 | tf_op jit(solution)/shard_map/ppermute | solution.py:30
  187.5 36.4 %collective-permute-start.9 = (bf16[256,1664]{1,0:T(8,128)(2,1)}, bf16[256,1664]{1,0:T(8,128)(2,1)S(1)}, u32[]{:S(2)}, u32[]{:S(2)}) collective-permute-start(bf16[256,1664]{1,0:T(8,128)(2,1)} %fusion.56), channel_id=1, source_target_pairs={{0,16},{16,0},{1,17},{17,1},{2,18},{18,2},{3,19},{19,3},{4,20},{20... | collective-permute-start | bytes 2555912 | tf_op jit(solution)/shard_map/ppermute | solution.py:30
  208.4 33.6 %copy-start.17 = (bf16[256,1536]{1,0:T(8,128)(2,1)}, bf16[256,1536]{1,0:T(8,128)(2,1)S(1)}, u32[]{:S(2)}) copy-start(bf16[256,1536]{1,0:T(8,128)(2,1)S(1)} %multiply_convert_fusion.4) | copy-start | bytes 2359300
  208.5 32.3 %collective-permute-start.11 = (bf16[256,1536]{1,0:T(8,128)(2,1)S(1)}, bf16[256,1536]{1,0:T(8,128)(2,1)S(1)}, u32[]{:S(2)}, u32[]{:S(2)}) collective-permute-start(bf16[256,1536]{1,0:T(8,128)(2,1)S(1)} %multiply_convert_fusion.4), channel_id=1, source_target_pairs={{0,16},{16,0},{1,17},{17,1},{2,18},{18,2},{3,19},{19,3},{4,20},{20... | collective-permute-start | bytes 2359304 | tf_op jit(solution)/shard_map/ppermute | solution.py:30
  223.9 18.2 %copy-start.9 = (bf16[256,1664]{1,0:T(8,128)(2,1)}, bf16[256,1664]{1,0:T(8,128)(2,1)S(1)}, u32[]{:S(2)}) copy-start(bf16[256,1664]{1,0:T(8,128)(2,1)S(1)} %collective-permute-done.9) | copy-start | bytes 2555908
  226.7 21.1 %collective-permute-start.10 = (bf16[512,1664]{1,0:T(8,128)(2,1)}, bf16[512,1664]{1,0:T(8,128)(2,1)}, u32[]{:S(2)}, u32[]{:S(2)}) collective-permute-start(bf16[512,1664]{1,0:T(8,128)(2,1)} %pad_maximum_fusion.8), channel_id=1, source_target_pairs={{0,2},{2,0},{1,3},{3,1},{4,6},{6,4},{5,7},{7,5},{8,10},{10,8},{9,1... | collective-permute-start | bytes 5111816 | tf_op jit(solution)/shard_map/ppermute | solution.py:30
  242.1 7.4 %collective-permute-start.12 = (bf16[512,1536]{1,0:T(8,128)(2,1)}, bf16[512,1536]{1,0:T(8,128)(2,1)}, u32[]{:S(2)}, u32[]{:S(2)}) collective-permute-start(bf16[512,1536]{1,0:T(8,128)(2,1)} %pad_maximum_fusion.10), channel_id=1, source_target_pairs={{0,2},{2,0},{1,3},{3,1},{4,6},{6,4},{5,7},{7,5},{8,10},{10,8},{9,1... | collective-permute-start | bytes 4718600 | tf_op jit(solution)/shard_map/ppermute | solution.py:30
  319.3 22.8 %collective-permute-start.13 = (bf16[512,1536]{1,0:T(8,128)(2,1)}, bf16[512,1536]{1,0:T(8,128)(2,1)}, u32[]{:S(2)}, u32[]{:S(2)}) collective-permute-start(bf16[512,1536]{1,0:T(8,128)(2,1)} %slice.576), channel_id=1, source_target_pairs={{0,2},{2,0},{1,3},{3,1},{4,6},{6,4},{5,7},{7,5},{8,10},{10,8},{9,1... | collective-permute-start | bytes 4718600 | tf_op jit(solution)/shard_map/ppermute | solution.py:30
  344.7 18.7 %collective-permute-start.14 = (bf16[256,1536]{1,0:T(8,128)(2,1)S(1)}, bf16[256,1536]{1,0:T(8,128)(2,1)S(1)}, u32[]{:S(2)}, u32[]{:S(2)}) collective-permute-start(bf16[256,1536]{1,0:T(8,128)(2,1)S(1)} %slice.768), channel_id=1, source_target_pairs={{0,16},{16,0},{1,17},{17,1},{2,18},{18,2},{3,19},{19,3},{4,20},{20... | collective-permute-start | bytes 2359304 | tf_op jit(solution)/shard_map/ppermute | solution.py:30
  368.7 17.9 %copy-start.13 = (bf16[256,1536]{1,0:T(8,128)(2,1)}, bf16[256,1536]{1,0:T(8,128)(2,1)S(1)}, u32[]{:S(2)}) copy-start(bf16[256,1536]{1,0:T(8,128)(2,1)S(1)} %get-tuple-element.102) | copy-start | bytes 2359300
  368.7 21.5 %copy-start.20 = (bf16[256,1536]{1,0:T(8,128)(2,1)S(1)}, bf16[256,1536]{1,0:T(8,128)(2,1)}, u32[]{:S(2)}) copy-start(bf16[256,1536]{1,0:T(8,128)(2,1)} %copy-done.17) | copy-start | bytes 2359300
  368.7 21.5 %copy-start.29 = (bf16[1024,8]{1,0:T(8,128)(2,1)S(1)}, bf16[1024,8]{1,0:T(8,128)(2,1)}, u32[]{:S(2)}) copy-start(bf16[1024,8]{1,0:T(8,128)(2,1)} %copy-done.28) | copy-start | bytes 49156
  368.7 21.5 %copy-start.39 = (bf16[256,1536]{1,0:T(8,128)(2,1)S(1)}, bf16[256,1536]{1,0:T(8,128)(2,1)}, u32[]{:S(2)}) copy-start(bf16[256,1536]{1,0:T(8,128)(2,1)} %copy-done.36) | copy-start | bytes 2359300
  368.7 17.9 %collective-permute-start.17 = (bf16[256,1536]{1,0:T(8,128)(2,1)S(1)}, bf16[256,1536]{1,0:T(8,128)(2,1)S(1)}, u32[]{:S(2)}, u32[]{:S(2)}) collective-permute-start(bf16[256,1536]{1,0:T(8,128)(2,1)S(1)} %get-tuple-element.102), channel_id=1, source_target_pairs={{0,16},{16,0},{1,17},{17,1},{2,18},{18,2},{3,19},{19,3},{4,20},{20... | collective-permute-start | bytes 2359304 | tf_op jit(solution)/shard_map/ppermute | solution.py:30
  388.1 8.3 %collective-permute-start.18 = (bf16[512,1536]{1,0:T(8,128)(2,1)}, bf16[512,1536]{1,0:T(8,128)(2,1)}, u32[]{:S(2)}, u32[]{:S(2)}) collective-permute-start(bf16[512,1536]{1,0:T(8,128)(2,1)} %pad_maximum_fusion.11), channel_id=1, source_target_pairs={{0,2},{2,0},{1,3},{3,1},{4,6},{6,4},{5,7},{7,5},{8,10},{10,8},{9,1... | collective-permute-start | bytes 4718600 | tf_op jit(solution)/shard_map/ppermute | solution.py:30
  396.3 106.0 %collective-permute-start.15 = (bf16[512,1536]{1,0:T(8,128)(2,1)}, bf16[512,1536]{1,0:T(8,128)(2,1)}, u32[]{:S(2)}, u32[]{:S(2)}) collective-permute-start(bf16[512,1536]{1,0:T(8,128)(2,1)} %slice.508), channel_id=1, source_target_pairs={{0,2},{2,0},{1,3},{3,1},{4,6},{6,4},{5,7},{7,5},{8,10},{10,8},{9,1... | collective-permute-start | bytes 4718600 | tf_op jit(solution)/shard_map/ppermute | solution.py:30
  426.2 108.2 %all-to-all-start.4 = ((bf16[16,96,1024]{2,1,0:T(8,128)(2,1)}), bf16[16,96,1024]{2,1,0:T(8,128)(2,1)}, u32[]{:S(2)}, u32[]{:S(2)}) async-start(bf16[16,96,1024]{2,1,0:T(8,128)(2,1)} %bitcast.397), calls=%async_computation.4 | async-start | bytes 6291456 | tf_op jit(solution)/shard_map/all_to_all | solution.py:88
  438.8 82.7 %collective-permute-start.19 = (bf16[512,1536]{1,0:T(8,128)(2,1)S(1)}, bf16[512,1536]{1,0:T(8,128)(2,1)}, u32[]{:S(2)}, u32[]{:S(2)}) collective-permute-start(bf16[512,1536]{1,0:T(8,128)(2,1)S(1)} %slice.582), channel_id=1, source_target_pairs={{0,2},{2,0},{1,3},{3,1},{4,6},{6,4},{5,7},{7,5},{8,10},{10,8},{9,1... | collective-permute-start | bytes 4718600 | tf_op jit(solution)/shard_map/ppermute | solution.py:30
  446.9 34.5 %collective-permute-start.21 = (f32[10,1536]{1,0:T(8,128)}, f32[10,1536]{1,0:T(8,128)S(1)}, u32[]{:S(2)}, u32[]{:S(2)}) collective-permute-start(f32[10,1536]{1,0:T(8,128)} %reshape.350), channel_id=1, source_target_pairs={{0,64},{64,0},{128,192},{192,128},{1,65},{65,1},{129,193},{193,129... | collective-permute-start | bytes 184328 | tf_op jit(solution)/shard_map/ppermute | solution.py:30
  482.3 10.5 %collective-permute-start.22 = (f32[10,1536]{1,0:T(8,128)S(1)}, f32[10,1536]{1,0:T(8,128)S(1)}, u32[]{:S(2)}, u32[]{:S(2)}) collective-permute-start(f32[10,1536]{1,0:T(8,128)S(1)} %add.246), channel_id=1, source_target_pairs={{0,128},{64,192},{128,0},{192,64},{1,129},{65,193},{129,1},{193,65... | collective-permute-start | bytes 184328 | tf_op jit(solution)/shard_map/ppermute | solution.py:30
  492.8 5.5 collective-permute-start.23
  498.3 3.6 collective-permute-start.24
  501.9 19.6 %copy-start.16 = (bf16[1024,1536]{1,0:T(8,128)(2,1)S(1)}, bf16[1024,1536]{1,0:T(8,128)(2,1)}, u32[]{:S(2)}) copy-start(bf16[1024,1536]{1,0:T(8,128)(2,1)} %get-tuple-element.212) | copy-start | bytes 9437188
  501.9 3.6 collective-permute-start.25
  505.0 22.3 %collective-permute-start.16 = (bf16[256,1536]{1,0:T(8,128)(2,1)S(1)}, bf16[256,1536]{1,0:T(8,128)(2,1)S(1)}, u32[]{:S(2)}, u32[]{:S(2)}) collective-permute-start(bf16[256,1536]{1,0:T(8,128)(2,1)S(1)} %slice.767), channel_id=1, source_target_pairs={{0,16},{16,0},{1,17},{17,1},{2,18},{18,2},{3,19},{19,3},{4,20},{20... | collective-permute-start | bytes 2359304 | tf_op jit(solution)/shard_map/ppermute | solution.py:30
  505.5 5.1 collective-permute-start.26
  510.5 6.7 %collective-permute-start.27 = (f32[10,1536]{1,0:T(8,128)S(1)}, f32[10,1536]{1,0:T(8,128)S(1)}, u32[]{:S(2)}, u32[]{:S(2)}) collective-permute-start(f32[10,1536]{1,0:T(8,128)S(1)} %add.251), channel_id=1, source_target_pairs={{0,2},{2,0},{1,3},{3,1},{4,6},{6,4},{5,7},{7,5},{8,10},{10,8},{9,1... | collective-permute-start | bytes 184328 | tf_op jit(solution)/shard_map/ppermute | solution.py:30
  517.9 15.5 %collective-permute-start.28 = (f32[10,1536]{1,0:T(8,128)}, f32[10,1536]{1,0:T(8,128)}, u32[]{:S(2)}, u32[]{:S(2)}) collective-permute-start(f32[10,1536]{1,0:T(8,128)} %add.252), channel_id=1, source_target_pairs={{0,1},{1,0},{2,3},{3,2},{4,5},{5,4},{6,7},{7,6},{8,9},{9,8},{10,11... | collective-permute-start | bytes 184328 | tf_op jit(solution)/shard_map/ppermute | solution.py:30
  526.1 18.8 %collective-permute-start.20 = (bf16[256,1536]{1,0:T(8,128)(2,1)}, bf16[256,1536]{1,0:T(8,128)(2,1)S(1)}, u32[]{:S(2)}, u32[]{:S(2)}) collective-permute-start(bf16[256,1536]{1,0:T(8,128)(2,1)} %slice.766), channel_id=1, source_target_pairs={{0,16},{16,0},{1,17},{17,1},{2,18},{18,2},{3,19},{19,3},{4,20},{20... | collective-permute-start | bytes 2359304 | tf_op jit(solution)/shard_map/ppermute | solution.py:30
  530.5 14.4 %copy-start.49 = (f32[1536]{0:T(1024)S(1)}, f32[1536]{0:T(1024)}, u32[]{:S(2)}) copy-start(f32[1536]{0:T(1024)} %copy-done.48) | copy-start | bytes 18436
  530.5 14.4 %copy-start.52 = (f32[256]{0:T(256)S(1)}, f32[256]{0:T(256)}, u32[]{:S(2)}) copy-start(f32[256]{0:T(256)} %copy-done.51) | copy-start | bytes 3076
  534.4 34.1 %all-to-all-start.2 = ((bf16[128,24,128]{2,1,0:T(8,128)(2,1)}), bf16[128,24,128]{2,1,0:T(8,128)(2,1)S(1)}, u32[]{:S(2)}, u32[]{:S(2)}) async-start(bf16[128,24,128]{2,1,0:T(8,128)(2,1)} %copy.353), calls=%async_computation.2 | async-start | bytes 1572864 | tf_op jit(solution)/shard_map/all_to_all | solution.py:343
  550.0 15.2 %collective-permute-start.29 = (bf16[24,1024]{1,0:T(8,128)(2,1)}, bf16[24,1024]{1,0:T(8,128)(2,1)S(1)}, u32[]{:S(2)}, u32[]{:S(2)}) collective-permute-start(bf16[24,1024]{1,0:T(8,128)(2,1)} %get-tuple-element.130), channel_id=1, source_target_pairs={{0,0},{16,1},{1,16},{17,17},{32,32},{48,33},{33,48},{49,49},{2,2},... | collective-permute-start | bytes 147464 | tf_op jit(solution)/shard_map/ppermute | solution.py:73
  551.5 13.7 %collective-permute-start.32 = (bf16[24,1024]{1,0:T(8,128)(2,1)}, bf16[24,1024]{1,0:T(8,128)(2,1)S(1)}, u32[]{:S(2)}, u32[]{:S(2)}) collective-permute-start(bf16[24,1024]{1,0:T(8,128)(2,1)} %get-tuple-element.131), channel_id=1, source_target_pairs={{33,0},{49,1},{32,16},{48,17},{1,32},{17,33},{0,48},{16,49},{35,2}... | collective-permute-start | bytes 147464 | tf_op jit(solution)/shard_map/ppermute | solution.py:73
  556.0 9.3 %collective-permute-start.31 = (bf16[24,1024]{1,0:T(8,128)(2,1)S(1)}, bf16[24,1024]{1,0:T(8,128)(2,1)S(1)}, u32[]{:S(2)}, u32[]{:S(2)}) collective-permute-start(bf16[24,1024]{1,0:T(8,128)(2,1)S(1)} %get-tuple-element.132), channel_id=1, source_target_pairs={{32,0},{48,1},{33,16},{49,17},{0,32},{16,33},{1,48},{17,49},{34,2}... | collective-permute-start | bytes 147464 | tf_op jit(solution)/shard_map/ppermute | solution.py:73
  556.4 9.0 %collective-permute-start.30 = (bf16[24,1024]{1,0:T(8,128)(2,1)S(1)}, bf16[24,1024]{1,0:T(8,128)(2,1)S(1)}, u32[]{:S(2)}, u32[]{:S(2)}) collective-permute-start(bf16[24,1024]{1,0:T(8,128)(2,1)S(1)} %get-tuple-element.133), channel_id=1, source_target_pairs={{1,0},{17,1},{0,16},{16,17},{33,32},{49,33},{32,48},{48,49},{3,2},... | collective-permute-start | bytes 147464 | tf_op jit(solution)/shard_map/ppermute | solution.py:73
  562.4 22.1 %copy-start.54 = (s32[2,1,128]{2,1,0:T(1,128)S(1)}, s32[2,1,128]{2,1,0:T(1,128)}, u32[]{:S(2)}) copy-start(s32[2,1,128]{2,1,0:T(1,128)} %copy-done.53) | copy-start | bytes 3076
  573.7 38.4 %all-to-all-start.3 = ((bf16[128,24,128]{2,1,0:T(8,128)(2,1)}), bf16[128,24,128]{2,1,0:T(8,128)(2,1)S(1)}, u32[]{:S(2)}, u32[]{:S(2)}) async-start(bf16[128,24,128]{2,1,0:T(8,128)(2,1)} %copy.366), calls=%async_computation.3 | async-start | bytes 1572864 | tf_op jit(solution)/shard_map/all_to_all | solution.py:343
  587.1 26.9 %collective-permute-start.33 = (bf16[24,3840]{1,0:T(8,128)(2,1)S(1)}, bf16[24,3840]{1,0:T(8,128)(2,1)S(1)}, u32[]{:S(2)}, u32[]{:S(2)}) collective-permute-start(bf16[24,3840]{1,0:T(8,128)(2,1)S(1)} %get-tuple-element.116), channel_id=1, source_target_pairs={{0,0},{16,1},{1,16},{17,17},{32,32},{48,33},{33,48},{49,49},{2,2},... | collective-permute-start | bytes 552968 | tf_op jit(solution)/shard_map/ppermute | solution.py:73
  587.8 26.2 %collective-permute-start.36 = (bf16[24,3840]{1,0:T(8,128)(2,1)S(1)}, bf16[24,3840]{1,0:T(8,128)(2,1)S(1)}, u32[]{:S(2)}, u32[]{:S(2)}) collective-permute-start(bf16[24,3840]{1,0:T(8,128)(2,1)S(1)} %get-tuple-element.117), channel_id=1, source_target_pairs={{33,0},{49,1},{32,16},{48,17},{1,32},{17,33},{0,48},{16,49},{35,2}... | collective-permute-start | bytes 552968 | tf_op jit(solution)/shard_map/ppermute | solution.py:73
  593.6 24.8 %collective-permute-start.35 = (bf16[24,3840]{1,0:T(8,128)(2,1)S(1)}, bf16[24,3840]{1,0:T(8,128)(2,1)S(1)}, u32[]{:S(2)}, u32[]{:S(2)}) collective-permute-start(bf16[24,3840]{1,0:T(8,128)(2,1)S(1)} %get-tuple-element.118), channel_id=1, source_target_pairs={{32,0},{48,1},{33,16},{49,17},{0,32},{16,33},{1,48},{17,49},{34,2}... | collective-permute-start | bytes 552968 | tf_op jit(solution)/shard_map/ppermute | solution.py:73
  593.6 24.8 %collective-permute-start.34 = (bf16[24,3840]{1,0:T(8,128)(2,1)S(1)}, bf16[24,3840]{1,0:T(8,128)(2,1)S(1)}, u32[]{:S(2)}, u32[]{:S(2)}) collective-permute-start(bf16[24,3840]{1,0:T(8,128)(2,1)S(1)} %get-tuple-element.119), channel_id=1, source_target_pairs={{1,0},{17,1},{0,16},{16,17},{33,32},{49,33},{32,48},{48,49},{3,2},... | collective-permute-start | bytes 552968 | tf_op jit(solution)/shard_map/ppermute | solution.py:73
  (44 other events, 199.8 us)
Sparse Core Ops, SparseCore 0:
  53.4 73.4 all-gather.2
  129.3 90.2 all-gather.4
  364.9 123.2 reduce-scatter.1

commit v3 on v2

--- a/solution.py
+++ b/solution.py
@@ -4,6 +4,8 @@
 import jax.numpy as jnp
 import numpy as np
 from jax import lax
+from jax.experimental import pallas as pl
+from jax.experimental.pallas import tpu as pltpu
 from jax.sharding import Mesh
 from jax.sharding import PartitionSpec as P
 
@@ -35,12 +37,25 @@
     return jnp.concatenate([pair, swapped(pair, "c")], axis=0)
 
 
-def rows_back(part):
+def core_sum(part, tied):
     half = part.shape[0] // 2
     both = part[:half].astype(F32) + swapped(part[half:], "c").astype(F32)
-    quarter = half // 2
+    return lax.optimization_barrier((both, tied))
+
+
+def pair_sum(both):
+    quarter = both.shape[0] // 2
     sent = swapped(both[quarter:].astype(BF16), "z0")
     return both[:quarter] + sent.astype(F32)
+
+
+def z_halves(both):
+    halves = both.reshape(2, -1, both.shape[1])
+    return jnp.where(lax.axis_index("z0") == 1, halves[::-1], halves)
+
+
+def rows_back(part, tied=()):
+    return pair_sum(core_sum(part, tied)[0])
 
 
 def z_routes():
@@ -64,14 +79,21 @@
     )
 
 
-def z_scattered(near):
+def z_scattered(near, small):
     routes = z_routes()
-    pieces = near.reshape(len(routes), -1, near.shape[1])
+    rows = near.shape[0] // len(routes)
+    cols = near.shape[1]
+    pieces = near.reshape(len(routes), rows, cols)
+    lines = small.astype(BF16).reshape(rows, -1)
     total = 0.0
     for piece, pairs in zip(pieces, routes):
         back = [(goal, start) for start, goal in pairs]
-        total = total + lax.ppermute(piece, ("z1", "z0", "zh"), back).astype(F32)
-    return total.astype(BF16)
+        sent = jnp.concatenate([piece, lines], axis=1)
+        total = total + lax.ppermute(sent, ("z1", "z0", "zh"), back).astype(F32)
+    small_sum = total[:, cols:]
+    small_sum = small_sum + swapped(small_sum, "c")
+    small_sum = small_sum + swapped(small_sum, "zh")
+    return total[:, :cols].astype(BF16), small_sum.reshape(small.shape)
 
 
 def xy_gathered(near):
@@ -82,25 +104,222 @@
     return lax.psum_scatter(total, ("x", "y"), scatter_dimension=0, tiled=True)
 
 
-def xy_scattered_apart(total):
+def xy_scattered_apart(total, small):
     count = lax.axis_size(("x", "y"))
-    pieces = total.reshape(count, -1, total.shape[1])
-    got = lax.all_to_all(pieces, ("x", "y"), 0, 0, tiled=True)
-    return jnp.sum(got.astype(F32), axis=0).astype(BF16)
-
-
-def summed_everywhere(value):
-    for axis in EVERY:
-        bit = 1
-        while bit < lax.axis_size(axis):
-            value = value + swapped(value, axis, bit)
-            bit *= 2
-    return value
-
-
-def silu_slope(value):
-    sigma = jax.nn.sigmoid(value)
-    return sigma * (1.0 + value * (1.0 - sigma))
+    cols = total.shape[1]
+    pieces = total.reshape(count, -1, cols)
+    lines = -(-small.size // (8 * cols)) * 8
+    flat = jnp.pad(small.astype(BF16).reshape(-1), (0, lines * cols - small.size))
+    flat = jnp.broadcast_to(flat.reshape(1, lines, cols), (count, lines, cols))
+    got = lax.all_to_all(jnp.concatenate([pieces, flat], axis=1), ("x", "y"), 0, 0, tiled=True)
+    summed = jnp.sum(got.astype(F32), axis=0)
+    rows = pieces.shape[1]
+    return summed[:rows].astype(BF16), summed[rows:].reshape(-1)[: small.size].reshape(small.shape)
+
+
+def expert_kernel(
+    experts,
+    n2_pair_ref,
+    n2_other_ref,
+    gy_pair_ref,
+    gy_other_ref,
+    w_ref,
+    router_ref,
+    n2_ref,
+    gy_ref,
+    dab_ref,
+    weighted_ref,
+    dn2_ref,
+    out_ref,
+    dlogits_ref,
+    small_ref,
+):
+    hidden = weighted_ref.shape[1]
+    each = hidden // (experts + 2)
+    width = n2_ref.shape[1]
+    second = pl.program_id(0) == 1
+    n2 = jnp.where(second, n2_other_ref[...], n2_pair_ref[...])
+    gy = jnp.where(second, gy_other_ref[:, :width], gy_pair_ref[:, :width])
+    flags = jnp.where(second, gy_other_ref[:, width:], gy_pair_ref[:, width:]).astype(F32)
+    n2_ref[...] = n2
+    gy_ref[...] = gy
+    named, kept = flags > 0.5, flags > 1.5
+    logits = dot(n2, router_ref[...], (1, 1))
+    top = jnp.max(jnp.where(named, logits, -1e30), axis=1, keepdims=True)
+    powers = jnp.where(named, jnp.exp(jnp.where(named, logits - top, 0.0)), 0.0)
+    gates = powers / jnp.maximum(jnp.sum(powers, axis=1, keepdims=True), 1e-30)
+    kept_gates = jnp.where(kept, gates, 0.0)
+    lane = lax.broadcasted_iota(jnp.int32, flags.shape, 1)
+    dgates = jnp.zeros(flags.shape, F32)
+    step = 2 * each
+    for at in range(0, hidden, step):
+        a = dot(n2, w_ref[:, at : at + step], (1, 0))
+        b = dot(n2, w_ref[:, hidden + at : hidden + at + step], (1, 0))
+        dhid = dot(gy, w_ref[:, 2 * hidden + at : 2 * hidden + at + step], (1, 0))
+        sigma = 1.0 / (1.0 + jnp.exp(-a))
+        silu = a * sigma
+        inner = (silu * b).astype(BF16).astype(F32)
+        first = at // each
+        if first < experts:
+            scale = jnp.concatenate(
+                [
+                    jnp.broadcast_to(kept_gates[:, e : e + 1], (flags.shape[0], each))
+                    for e in (first, first + 1)
+                ],
+                axis=1,
+            )
+            product = inner * dhid
+            for e in (first, first + 1):
+                lo = (e - first) * each
+                total = jnp.sum(product[:, lo : lo + each], axis=1, keepdims=True)
+                dgates = jnp.where(lane == e, total, dgates)
+            weighted = scale * inner
+            dinner = scale * dhid
+        else:
+            weighted, dinner = inner, dhid
+        weighted_ref[:, at : at + step] = weighted.astype(BF16)
+        slope = sigma * (1.0 + a * (1.0 - sigma))
+        dab_ref[:, at : at + step] = (dinner * b * slope).astype(BF16)
+        dab_ref[:, hidden + at : hidden + at + step] = (dinner * silu).astype(BF16)
+    dgates = jnp.where(kept, dgates, 0.0)
+    dlogits = gates * (dgates - jnp.sum(gates * dgates, axis=1, keepdims=True))
+    dlogits = dlogits.astype(BF16)
+    dlogits_ref[...] = dlogits
+    tile = width // 3
+    dab = dab_ref[...]
+    weighted = weighted_ref[...]
+
+    @pl.when(pl.program_id(0) == 0)
+    def _():
+        small_ref[...] = jnp.zeros_like(small_ref)
+
+    for at in range(0, width, tile):
+        dn2 = dot(dab, w_ref[at : at + tile, : 2 * hidden], (1, 1))
+        dn2 = dn2 + dot(dlogits, router_ref[:, at : at + tile], (1, 0))
+        dn2_ref[:, at : at + tile] = dn2.astype(BF16)
+        small_ref[:, at : at + tile] += jnp.sum(
+            dn2 * n2_ref[:, at : at + tile].astype(F32), axis=0, keepdims=True
+        )
+        out_ref[:, at : at + tile] = dot(
+            weighted, w_ref[at : at + tile, 2 * hidden :], (1, 1), BF16
+        )
+
+
+def experts_both_ways(n2_pair, n2_other, gy_pair, gy_other, ffn_w, router, experts):
+    tile, width = n2_pair.shape
+    rows = 2 * tile
+    hidden = ffn_w.shape[1] // 3
+
+    def by_tile(cols):
+        return pl.BlockSpec((tile, cols), lambda i: (i, 0))
+
+    operands = (n2_pair, n2_other, gy_pair, gy_other, ffn_w, router)
+    shapes = (width, width, 2 * hidden, hidden, width, width, 128)
+    return pl.pallas_call(
+        lambda *refs: expert_kernel(experts, *refs),
+        grid=(2,),
+        in_specs=[
+            pl.BlockSpec(v.shape, lambda i: (0, 0), pipeline_mode=pl.Buffered(1)) for v in operands
+        ],
+        out_specs=[by_tile(n) for n in shapes] + [pl.BlockSpec((1, width), lambda i: (0, 0))],
+        out_shape=[jax.ShapeDtypeStruct((rows, n), BF16) for n in shapes]
+        + [jax.ShapeDtypeStruct((1, width), F32)],
+        compiler_params=pltpu.CompilerParams(vmem_limit_bytes=54 << 20),
+        cost_estimate=pl.CostEstimate(
+            flops=12 * rows * width * hidden,
+            transcendentals=2 * rows * hidden,
+            bytes_accessed=2 * (ffn_w.size + rows * (8 * width + 3 * hidden)),
+        ),
+        name="experts",
+    )(*operands)
+
+
+def attention_backward_kernel(
+    seq_len,
+    pair_ref,
+    other_ref,
+    qkv_ref,
+    n1_ref,
+    w_ref,
+    dattn_ref,
+    dqkv_ref,
+    dn1_ref,
+    small_ref,
+):
+    tile, width = dattn_ref.shape
+    cols = dqkv_ref.shape[1]
+    q_cols = GROUP * HEAD_SIZE
+    root = 1.0 / math.sqrt(HEAD_SIZE)
+    dattn = jnp.where(pl.program_id(0) == 1, other_ref[...], pair_ref[...])
+    dattn_ref[...] = dattn
+    dmixed = dot(dattn, w_ref[:, cols:], (1, 0), BF16)
+    row = lax.broadcasted_iota(jnp.int32, (seq_len, seq_len), 0)
+    seen = lax.broadcasted_iota(jnp.int32, (seq_len, seq_len), 1) <= row
+    for start in range(0, tile, seq_len):
+        at = slice(start, start + seq_len)
+        key = qkv_ref[at, q_cols : q_cols + HEAD_SIZE]
+        value = qkv_ref[at, q_cols + HEAD_SIZE :]
+        dkey = jnp.zeros((seq_len, HEAD_SIZE), F32)
+        dvalue = jnp.zeros((seq_len, HEAD_SIZE), F32)
+        for head in range(0, q_cols, HEAD_SIZE):
+            query = qkv_ref[at, head : head + HEAD_SIZE]
+            grad = dmixed[at, head : head + HEAD_SIZE]
+            scores = jnp.where(seen, dot(query, key, (1, 1)) * root, -1e30)
+            powers = jnp.exp(scores - jnp.max(scores, axis=1, keepdims=True))
+            probs = powers / jnp.sum(powers, axis=1, keepdims=True)
+            dprobs = dot(grad, value, (1, 1))
+            inside = jnp.sum(probs * dprobs, axis=1, keepdims=True)
+            dscores = (probs * (dprobs - inside)).astype(BF16)
+            dqkv_ref[at, head : head + HEAD_SIZE] = (dot(dscores, key, (1, 0)) * root).astype(BF16)
+            dkey = dkey + dot(dscores, query, (0, 0))
+            dvalue = dvalue + dot(probs.astype(BF16), grad, (0, 0))
+        dqkv_ref[at, q_cols : q_cols + HEAD_SIZE] = (dkey * root).astype(BF16)
+        dqkv_ref[at, q_cols + HEAD_SIZE :] = dvalue.astype(BF16)
+    dqkv = dqkv_ref[...]
+
+    @pl.when(pl.program_id(0) == 0)
+    def _():
+        small_ref[...] = jnp.zeros_like(small_ref)
+
+    step = width // 3
+    for at in range(0, width, step):
+        dn1 = dot(dqkv, w_ref[at : at + step, :cols], (1, 1))
+        dn1_ref[:, at : at + step] = dn1.astype(BF16)
+        small_ref[:, at : at + step] += jnp.sum(
+            dn1 * n1_ref[:, at : at + step].astype(F32), axis=0, keepdims=True
+        )
+
+
+def attention_backward(pair, other, qkv, n1, attn_w, seq_len):
+    tile, width = pair.shape
+    rows, cols = qkv.shape
+
+    def whole(value):
+        return pl.BlockSpec(value.shape, lambda i: (0, 0), pipeline_mode=pl.Buffered(1))
+
+    def by_tile(cols):
+        return pl.BlockSpec((tile, cols), lambda i: (i, 0))
+
+    return pl.pallas_call(
+        lambda *refs: attention_backward_kernel(seq_len, *refs),
+        grid=(2,),
+        in_specs=[whole(pair), whole(other), by_tile(cols), by_tile(width), whole(attn_w)],
+        out_specs=[
+            by_tile(width),
+            by_tile(cols),
+            by_tile(width),
+            pl.BlockSpec((1, width), lambda i: (0, 0)),
+        ],
+        out_shape=[jax.ShapeDtypeStruct((rows, n), BF16) for n in (width, cols, width)]
+        + [jax.ShapeDtypeStruct((1, width), F32)],
+        compiler_params=pltpu.CompilerParams(vmem_limit_bytes=44 << 20),
+        cost_estimate=pl.CostEstimate(
+            flops=2 * rows * width * attn_w.shape[1],
+            transcendentals=rows * seq_len * GROUP,
+            bytes_accessed=2 * (attn_w.size + rows * (5 * width + 2 * cols)),
+        ),
+        name="attention_backward",
+    )(pair, other, qkv, n1, attn_w)
 
 
 def attention_scores(query, key):
@@ -164,16 +383,12 @@
     )
     chip_rows = lax.all_to_all(both_shards, "c", 0, 0, tiled=True)
     chip_rows = chip_rows.reshape(2 * rows_here, -1)
-    near = z_gathered(chip_rows)
-    attn_w = xy_gathered(near[:, :attn_cols])
-    ffn_w = xy_gathered(near[:, attn_cols:])
+    near_w = z_gathered(chip_rows)
     q_cols = query_matrix.shape[1] // 2
     k_cols = key_matrix.shape[1] // 2
     qkv_cols = q_cols + 2 * k_cols
-    qkv_w, out_w = attn_w[:, :qkv_cols], attn_w[:, qkv_cols:]
     hidden_e = w_gate.shape[2] // 2
     hidden = experts * hidden_e + s_gate.shape[1] // 2
-    up_w, down_w = ffn_w[:, : 2 * hidden], ffn_w[:, 2 * hidden :]
 
     def flipped(value, axes):
         for axis, flip in zip(axes, flips):
@@ -212,7 +427,12 @@
     rows_in = jnp.concatenate([tokens[:, :, 0], marks, cotangent[:, :, 0]], axis=2)
     sent = jnp.einsum("mjs,msd->jmd", deal, rows_in, preferred_element_type=F32)
     sent = sent.astype(BF16).reshape(seqs, -1, 128)
-    got = lax.all_to_all(sent, DP, 0, 0, tiled=True).reshape(seq_len, batches, -1)
+    near_w, sent = lax.optimization_barrier((near_w, sent))
+    attn_w = xy_gathered(near_w[:, :attn_cols])
+    ffn_w = xy_gathered(near_w[:, attn_cols:])
+    qkv_w, out_w = attn_w[:, :qkv_cols], attn_w[:, qkv_cols:]
+    got = lax.all_to_all(sent, DP, 0, 0, tiled=True)
+    got = got.reshape(seq_len, batches, -1)
     own_in = jnp.swapaxes(got, 0, 1)
     x_own = dot(own_in[:, :, :width].reshape(batches * seq_len, width), features, (1, 0))
     own_marks = own_in[:, :, width : width + 128]
@@ -229,8 +449,17 @@
     other_totals = swapped(totals, "zh")
     rank = before + jnp.where(t == 1, other_totals, 0.0)[:, None, :]
     own_kept = jnp.where(rank < CAP, own_hits, jnp.zeros_like(own_hits))
-    flags = jnp.concatenate([own_hits, own_kept], axis=2).reshape(batches * seq_len, -1)
+    flags = (own_hits + own_kept).reshape(batches * seq_len, -1)
     flags = jnp.pad(flags, ((0, 0), (0, 128 - flags.shape[1])))
+
+    def to_send(own):
+        natural = dot(own, features, (1, 1), BF16).reshape(batches, seq_len, -1)
+        return jnp.swapaxes(natural, 0, 1).reshape(seq_len, -1, 128)
+
+    def placed(got):
+        got = got.reshape(seqs, batches, -1)
+        back = jnp.einsum("mjs,jmd->msd", deal, got, preferred_element_type=F32)
+        return back.astype(BF16)[:, :, None]
 
     small_in = to_local(
         jnp.concatenate([gain_attn[None], gain_ffn[None], w_router.T.astype(F32)], axis=0)
@@ -238,11 +467,14 @@
     gain_a, gain_f, router = small_in[0:1], small_in[1:2], small_in[2:].astype(BF16)
     scale_attn = lax.rsqrt(jnp.mean(x_own * x_own, axis=-1, keepdims=True) + EPS)
     unit_attn = x_own * scale_attn
-    n1 = whole_rows((unit_attn * gain_a).astype(BF16))
+    n1_own = (unit_attn * gain_a).astype(BF16)
     gy_own_low = jnp.concatenate([gy_own.astype(BF16), flags], axis=1)
-    n1, gy_own_low = lax.optimization_barrier((n1, gy_own_low))
-    both = whole_rows(gy_own_low)
-    gy, flags_all = both[:, :width], both[:, width:]
+    n1_other, gy_own_low = lax.optimization_barrier((swapped(n1_own, "z0"), gy_own_low))
+    n1 = jnp.concatenate([n1_own, n1_other], axis=0)
+    n1 = jnp.concatenate([n1, swapped(n1, "c")], axis=0)
+    gy_pair = lax.all_to_all(
+        jnp.broadcast_to(gy_own_low[None], (2, *gy_own_low.shape)), "z0", 0, 0, tiled=True
+    )
     rows = n1.shape[0]
     count = rows // seq_len
     qkv = dot(n1, qkv_w, (1, 0), BF16)
@@ -255,105 +487,66 @@
     probs_low = probs.astype(BF16)
     mixed = jnp.einsum("sglm,smd->slgd", probs_low, value, preferred_element_type=F32)
     mixed = mixed.astype(BF16).reshape(rows, q_cols)
+    mixed, gy_pair = lax.optimization_barrier((mixed, gy_pair))
+    gy_pair = jnp.where(lax.axis_index("z0") == 1, gy_pair[::-1], gy_pair)
+    gy_pair = gy_pair.reshape(-1, gy_own_low.shape[1])
+    gy_other = swapped(gy_pair, "c")
     h_own = x_own + rows_back(dot(mixed, out_w, (1, 1), BF16))
 
     scale_ffn = lax.rsqrt(jnp.mean(h_own * h_own, axis=-1, keepdims=True) + EPS)
     unit_ffn = h_own * scale_ffn
-    n2 = whole_rows((unit_ffn * gain_f).astype(BF16))
-    logits = dot(n2, router, (1, 1))
-    named_all = flags_all[:, :experts] > 0
-    kept = flags_all[:, experts : 2 * experts] > 0
-    top = jnp.max(jnp.where(named_all, logits, -1e30), axis=1, keepdims=True)
-    powers = jnp.where(named_all, jnp.exp(jnp.where(named_all, logits - top, 0.0)), 0.0)
-    gates = powers / jnp.maximum(jnp.sum(powers, axis=1, keepdims=True), 1e-30)
-    kept_gates = jnp.where(kept, gates, 0.0)
-
-    def spread(per_expert):
-        wide = jnp.broadcast_to(per_expert[:, :, None], (rows, experts, hidden_e))
-        return jnp.concatenate(
-            [wide.reshape(rows, -1), jnp.ones((rows, hidden - experts * hidden_e), F32)], axis=1
-        )
-
-    weight = spread(kept_gates)
-    ab = dot(n2, up_w, (1, 0))
-    a, b = ab[:, :hidden], ab[:, hidden:]
-    silu_a = jax.nn.silu(a)
-    inner = (silu_a * b).astype(BF16)
-    weighted = (weight * inner.astype(F32)).astype(BF16)
-    dhid = dot(gy, down_w, (1, 0))
-    dgates = jnp.sum(
-        (inner.astype(F32) * dhid)[:, : experts * hidden_e].reshape(rows, experts, hidden_e), axis=2
-    )
-    dgates = jnp.where(kept, dgates, 0.0)
-    dlogits = gates * (dgates - jnp.sum(gates * dgates, axis=1, keepdims=True))
-    dlogits = dlogits.astype(BF16)
-    dinner = weight * dhid
-    dab = jnp.concatenate(
-        [(dinner * b * silu_slope(a)).astype(BF16), (dinner * silu_a).astype(BF16)], axis=1
-    )
-    dn2_part = (dot(dab, up_w, (1, 1)) + dot(dlogits, router, (1, 0))).astype(BF16)
-    big_ffn = jnp.concatenate(
-        [dot(n2, dab, (0, 0), BF16), dot(gy, weighted, (0, 0), BF16)], axis=1
-    )
-    out_part = dot(weighted, down_w, (1, 1), BF16)
-    small_router = dot(dlogits, n2, (0, 0))
-    small_ffn = jnp.sum(dn2_part.astype(F32) * n2.astype(F32), axis=0, keepdims=True) / gain_f
-    dn2 = rows_back(dn2_part)
-    dn2, big_ffn, out_part = lax.optimization_barrier((dn2, big_ffn, out_part))
+    n2_own = (unit_ffn * gain_f).astype(BF16)
+    n2_pair = jnp.concatenate([n2_own, swapped(n2_own, "z0")], axis=0)
+    n2_other = swapped(n2_pair, "c")
+    router_low = jnp.pad(router, ((0, 128 - experts), (0, 0)))
+    n2, gy, dab, weighted, dn2_part, out_part, dlogits, small_ffn = experts_both_ways(
+        n2_pair, n2_other, gy_pair, gy_other, ffn_w, router_low, experts
+    )
+    big_down = dot(gy, weighted, (0, 0), BF16)
+    dn2_sum, dab = core_sum(dn2_part, dab)
+    dn2 = pair_sum(dn2_sum)
+    big_ffn = jnp.concatenate([dot(n2, dab, (0, 0), BF16), big_down], axis=1)
+    small_router = dot(dlogits, n2, (0, 0))[:experts]
+    small_ffn = small_ffn / gain_f
+    dn2, big_ffn = lax.optimization_barrier((dn2, big_ffn))
     near_ffn = xy_scattered(big_ffn)
     scaled = dn2 * gain_f
     dh = gy_own + scale_ffn * (
         scaled - unit_ffn * jnp.mean(scaled * unit_ffn, axis=-1, keepdims=True)
     )
 
-    dattn = whole_rows(dh.astype(BF16))
-    dmixed = dot(dattn, out_w, (1, 0), BF16)
-    big_out = dot(dattn, mixed, (0, 0), BF16)
-    dheads = dmixed.reshape(count, seq_len, GROUP, HEAD_SIZE)
-    dprobs = jnp.einsum("slgd,smd->sglm", dheads, value, preferred_element_type=F32)
-    dscores = (probs * (dprobs - jnp.sum(probs * dprobs, axis=-1, keepdims=True))).astype(BF16)
-    root = 1.0 / math.sqrt(HEAD_SIZE)
-    dq = jnp.einsum("sglm,smd->slgd", dscores, key, preferred_element_type=F32) * root
-    dk = jnp.einsum("sglm,slgd->smd", dscores, query, preferred_element_type=F32) * root
-    dv = jnp.einsum("sglm,slgd->smd", probs_low, dheads, preferred_element_type=F32)
-    dqkv = jnp.concatenate(
-        [
-            dq.astype(BF16).reshape(rows, -1),
-            dk.astype(BF16).reshape(rows, -1),
-            dv.astype(BF16).reshape(rows, -1),
-        ],
-        axis=1,
-    )
-    dn1_part = dot(dqkv, qkv_w, (1, 1), BF16)
-    big_attn = jnp.concatenate([dot(n1, dqkv, (0, 0), BF16), big_out], axis=1)
-    near_attn = xy_scattered_apart(big_attn)
-    small_attn = jnp.sum(dn1_part.astype(F32) * n1.astype(F32), axis=0, keepdims=True) / gain_a
-    small = jnp.concatenate([small_attn, small_ffn, small_router], axis=0)
-    final = summed_everywhere(to_natural(small))
-    dn1 = rows_back(dn1_part)
+    dattn_own, out_part = lax.optimization_barrier((dh.astype(BF16), out_part))
+    out_halves = z_halves(core_sum(out_part, ())[0].astype(BF16))
+    dattn_other, small_router, out_halves = lax.optimization_barrier(
+        (swapped(dattn_own, "z0"), small_router, out_halves)
+    )
+    dattn_pair = jnp.concatenate([dattn_own, dattn_other], axis=0)
+    dattn, dqkv, dn1_part, small_attn = attention_backward(
+        dattn_pair, swapped(dattn_pair, "c"), qkv, n1, attn_w, seq_len
+    )
+    dqkv, halves_got = lax.optimization_barrier(
+        (dqkv, lax.all_to_all(out_halves, "z0", 0, 0, tiled=True))
+    )
+    branch = jnp.sum(halves_got.astype(F32), axis=0)
+    out_own = (own_keep * (h_own + branch)).astype(BF16)
+    out_got = lax.all_to_all(to_send(out_own), DP, 0, 0, tiled=True)
+    big_attn = jnp.concatenate([dot(n1, dqkv, (0, 0), BF16), dot(dattn, mixed, (0, 0), BF16)], axis=1)
+    small = jnp.concatenate([small_attn / gain_a, small_ffn, small_router], axis=0)
+    dn1_sum, big_attn = core_sum(dn1_part, big_attn)
+    dn1 = pair_sum(dn1_sum)
     scaled = dn1 * gain_a
     dx_own = dh + scale_attn * (
         scaled - unit_attn * jnp.mean(scaled * unit_attn, axis=-1, keepdims=True)
     )
-    dx_own = dx_own.astype(BF16)
-
-    def returned(own):
-        natural = dot(own, features, (1, 1), BF16).reshape(batches, seq_len, -1)
-        sent = jnp.swapaxes(natural, 0, 1).reshape(seq_len, -1, 128)
-        got = lax.all_to_all(sent, DP, 0, 0, tiled=True).reshape(seqs, batches, -1)
-        back = jnp.einsum("mjs,jmd->msd", deal, got, preferred_element_type=F32)
-        return back.astype(BF16)[:, :, None]
-
-    branch = rows_back(out_part)
-    out_own = (own_keep * (h_own + branch)).astype(BF16)
-    out_tokens = returned(out_own)
-    grad_tokens = returned(dx_own)
-
-    def exchanged(near_grads):
-        chip = z_scattered(near_grads).reshape(2, rows_here, -1)
-        return lax.all_to_all(chip, "c", 0, 0, tiled=True).astype(F32)
-
-    mine = jnp.concatenate([exchanged(near_attn), exchanged(near_ffn)], axis=2)
+    big_attn, out_got = lax.optimization_barrier((big_attn, out_got))
+    near_attn, small = xy_scattered_apart(big_attn, to_natural(small))
+    dx_own, near_ffn = lax.optimization_barrier((dx_own.astype(BF16), near_ffn))
+    dx_got = lax.all_to_all(to_send(dx_own), DP, 0, 0, tiled=True)
+
+    chip, final = z_scattered(jnp.concatenate([near_attn, near_ffn], axis=1), small)
+    chip, dx_got = lax.optimization_barrier((chip, dx_got))
+    out_tokens, grad_tokens = placed(out_got), placed(dx_got)
+    mine = lax.all_to_all(chip.reshape(2, rows_here, -1), "c", 0, 0, tiled=True).astype(F32)
 
     def join(start, cols):
         part = mine[:, :, start : start + cols]

time: 645 us -> 572 us (0.89)
  matrix products: 125 us -> 49.7 us
  Pallas kernels: 0 us -> 54 us
  waiting for transfers between devices: 226 us -> 204 us
  local copies, waits for them, and re-layouts: 86.2 us -> 70.3 us
  other arithmetic: 59.4 us -> 49.1 us
    dot_general x19 -> x11, matrix products: 114 us -> 43.6 us  [dot(): lax.dot_general(left, right, (((contract[0],), (contract[1],)), ((), ()))...]
    pallas_call x0 -> x2, Pallas kernels: none -> 54 us  [the longest x1 35.9 us: experts_both_ways(): pl.pallas_call(lambda *refs: expert_kernel(experts, *refs), grid=(2,), in...]
    ppermute x25 -> x17, waiting for transfers between devices: 144 us -> 90.9 us  [swapped(): lax.ppermute(value, axis, [(i, i ^ bit) for i in range(lax.axis_size(axis...]
    all_to_all x4 -> x6, waiting for transfers between devices: 59.4 us -> 88.3 us  [the longest x1 44.1 us: on_device(): got = lax.all_to_all(sent, DP, 0, 0, tiled=True)]
    all_to_all x4 -> x6, starting transfers between devices: 40.7 us -> 61.6 us  [the longest x1 21.5 us: on_device(): got = lax.all_to_all(sent, DP, 0, 0, tiled=True)]
    ppermute x25 -> x17, starting transfers between devices: 37.5 us -> 27.3 us  [swapped(): lax.ppermute(value, axis, [(i, i ^ bit) for i in range(lax.axis_size(axis...]
    reshape x11 -> x8, local copies, waits for them, and re-layouts: 15.5 us -> 5.79 us  [the longest x2 3.89 us: to_send(): return jnp.swapaxes(natural, 0, 1).reshape(seq_len, -1, 128)]
    optimization_barrier x0 -> x4, local copies, waits for them, and re-layouts: none -> 9.51 us  [the longest x2 6.26 us: on_device(): big_attn, out_got = lax.optimization_barrier((big_attn, out_got))]
  transfers between devices with their start and end apart: 44 -> 34, of which waited for: 21 -> 18; matrix products, arithmetic and copies ran while one was open for 29% -> 23% of each run, Pallas kernels for 0% -> 3%
where the time goes in v3:
time: 572 us; the launch traced here: 563 us
  waiting for transfers between devices  204 us (36%)
  starting transfers between devices  109 us (19%)
  local copies, waits for them, and re-layouts  70.3 us (12%)
  Pallas kernels  54 us (9%)
  matrix products  49.7 us (9%)
  other arithmetic  49.1 us (9%)
  between operations  15.3 us (3%)
  blocking collectives  10.9 us (2%)
    ppermute x17, waiting for transfers between devices, swapped(): lax.ppermute(value, axis, [(i, i ^ bit) for i in range(lax.axis_size(axis...  90.9 us
    all_to_all x1, waiting for transfers between devices, on_device(): got = lax.all_to_all(sent, DP, 0, 0, tiled=True)  44.1 us
    dot_general x11, matrix products, dot(): lax.dot_general(left, right, (((contract[0],), (contract[1],)), ((), ()))...  43.6 us
    pallas_call x1, Pallas kernels, experts_both_ways(): pl.pallas_call(lambda *refs: expert_kernel(experts, *refs), grid=(2,), in...  35.9 us
    ppermute x17, starting transfers between devices, swapped(): lax.ppermute(value, axis, [(i, i ^ bit) for i in range(lax.axis_size(axis...  27.3 us
    all_to_all x1, waiting for transfers between devices, xy_scattered_apart(): lax.all_to_all(jnp.concatenate([pieces, flat], axis=1), ('x', 'y'), 0, 0,...  26.1 us
    unnamed x144, local copies, waits for them, and re-layouts  25 us
    all_to_all x1, starting transfers between devices, on_device(): got = lax.all_to_all(sent, DP, 0, 0, tiled=True)  21.5 us
  transfers between devices with their start and end apart: 34, of which 18 were waited for; matrix products, arithmetic and copies ran while one was open for 23% of the time, Pallas kernels for 3%

profile of v3, /device:TPU:1, one launch (start us, length us, event | category | flops | bytes accessed | tf_op | source)
XLA Modules:
  0.0 563.0 jit_solution(8490106964241077897)
XLA Ops:
  16.4 7.0 %all_to_all.40 = bf16[2,12,4864]{2,1,0:T(8,128)(2,1)S(1)} all-to-all(bf16[2,12,4864]{2,1,0:T(8,128)(2,1)S(1)} %pad_maximum_fusion.11), channel_id=1, replica_groups=mesh['x'=4,'z1'=2,'z0'=2,'y'=4,'c'=2,'zh'=2] {'c'}, dimensions={0} | all-to-all | bytes 466944 | tf_op jit(solution)/shard_map/all_to_all | solution.py:384
  24.1 4.3 collective-permute-start.3
  30.9 3.5 collective-permute-start
  36.0 7.4 %collective-permute-done.2 = bf16[24,4864]{1,0:T(8,128)(2,1)} collective-permute-done((bf16[24,4864]{1,0:T(8,128)(2,1)}, bf16[24,4864]{1,0:T(8,128)(2,1)}, u32[]{:S(2)}, u32[]{:S(2)}) %collective-permute-start.2) | collective-permute-done | bytes 233504 | tf_op jit(solution)/shard_map/ppermute | solution.py:78
  43.4 5.5 collective-permute-done.1
  51.9 2.7 copy.306
  54.7 21.5 %all-to-all-start.1 = ((bf16[128,50,128]{2,1,0:T(8,128)(2,1)}), bf16[128,50,128]{2,1,0:T(8,128)(2,1)S(1)}, u32[]{:S(2)}, u32[]{:S(2)}) async-start(bf16[128,50,128]{2,1,0:T(8,128)(2,1)} %copy.306), calls=%async_computation.1 | async-start | bytes 3670016 | tf_op jit(solution)/shard_map/all_to_all | solution.py:434
  78.6 44.1 %all-to-all-done.1 = bf16[128,50,128]{2,1,0:T(8,128)(2,1)S(1)} async-done(((bf16[128,50,128]{2,1,0:T(8,128)(2,1)}), bf16[128,50,128]{2,1,0:T(8,128)(2,1)S(1)}, u32[]{:S(2)}, u32[]{:S(2)}) %all-to-all-start.1) | async-done | bytes 1638432 | tf_op jit(solution)/shard_map/all_to_all | solution.py:434
  122.7 2.1 copy.307
  124.9 4.7 collective-permute-start.5
  132.1 3.3 multiply_reduce_fusion.3
  137.0 3.5 fusion.80
  142.9 10.7 %collective-permute-done.4 = bf16[256,1536]{1,0:T(8,128)(2,1)} collective-permute-done((bf16[256,1536]{1,0:T(8,128)(2,1)S(1)}, bf16[256,1536]{1,0:T(8,128)(2,1)}, u32[]{:S(2)}, u32[]{:S(2)}) %collective-permute-start.4) | collective-permute-done | bytes 786464 | tf_op jit(solution)/shard_map/ppermute | solution.py:32
  153.6 2.4 pad_maximum_fusion.4
  156.0 2.4 collective-permute-start.6
  159.7 4.7 all-to-all-start.2
  164.5 5.1 fusion.21.refs_2_
  170.5 3.3 reshape.339
  178.0 7.3 %all-to-all-done.2 = bf16[2,256,1664]{2,1,0:T(8,128)(2,1)} async-done(((bf16[2,256,1664]{2,1,0:T(8,128)(2,1)}), bf16[2,256,1664]{2,1,0:T(8,128)(2,1)}, u32[]{:S(2)}, u32[]{:S(2)}) %all-to-all-start.2) | async-done | bytes 1703968 | tf_op jit(solution)/shard_map/all_to_all | solution.py:475
  185.3 3.4 convolution_convert_fusion.3
  189.7 3.0 collective-permute-done.7
  195.9 18.9 %collective-permute-done.8 = bf16[256,1536]{1,0:T(8,128)(2,1)} collective-permute-done((bf16[256,1536]{1,0:T(8,128)(2,1)}, bf16[256,1536]{1,0:T(8,128)(2,1)}, u32[]{:S(2)}, u32[]{:S(2)}) %collective-permute-start.8) | collective-permute-done | bytes 786464 | tf_op jit(solution)/shard_map/ppermute | solution.py:32
  214.9 2.0 multiply_reduce_fusion.2
  218.3 9.5 %collective-permute-start.9 = (bf16[256,1536]{1,0:T(8,128)(2,1)S(1)}, bf16[256,1536]{1,0:T(8,128)(2,1)S(1)}, u32[]{:S(2)}, u32[]{:S(2)}) collective-permute-start(bf16[256,1536]{1,0:T(8,128)(2,1)S(1)} %multiply_convert_fusion.1), channel_id=1, source_target_pairs={{0,16},{16,0},{1,17},{17,1},{2,18},{18,2},{3,19},{19,3},{4,20},{20... | collective-permute-start | bytes 2359304 | tf_op jit(solution)/shard_map/ppermute | solution.py:32
  227.8 3.6 reverse_select_fusion
  232.8 12.8 %collective-permute-done.9 = bf16[256,1536]{1,0:T(8,128)(2,1)S(1)} collective-permute-done((bf16[256,1536]{1,0:T(8,128)(2,1)S(1)}, bf16[256,1536]{1,0:T(8,128)(2,1)S(1)}, u32[]{:S(2)}, u32[]{:S(2)}) %collective-permute-start.9) | collective-permute-done | bytes 786464 | tf_op jit(solution)/shard_map/ppermute | solution.py:32
  246.8 2.1 collective-permute-start.10
  252.3 35.9 %experts.1 = (bf16[1024,1536]{1,0:T(8,128)(2,1)}, bf16[1024,1536]{1,0:T(8,128)(2,1)}, bf16[1024,2560]{1,0:T(8,128)(2,1)}, bf16[1024,1280]{1,0:T(8,128)(2,1)}, bf...) custom-call(bf16[512,1536]{1,0:T(8,128)(2,1)} %pad_maximum_fusion.5.refs_0, ...), custom_call_target="tpu_custom_call" | custom-call | flops 24159191040 | bytes 44826624 | tf_op jit(solution)/shard_map/experts/pallas_call | solution.py:218
  290.6 6.6 %convolution_convert_fusion.1 = bf16[1536,1280]{1,0:T(8,128)(2,1)S(1)} fusion(bf16[1024,1536]{1,0:T(8,128)(2,1)S(1)} %copy-done.37, bf16[1024,1280]{1,0:T(8,128)(2,1)} %get-tuple-element.64), kind=kOutput, calls=%fused_computation.7 | convolution fusion | flops 4028497920 | bytes 9699328 | tf_op jit(solution)/shard_map/dot_general | solution.py:25
  300.2 8.8 %convolution_convert_fusion = bf16[1536,2560]{1,0:T(8,128)(2,1)S(1)} fusion(bf16[1024,1536]{1,0:T(8,128)(2,1)S(1)} %copy-done.18, bf16[1024,2560]{1,0:T(8,128)(2,1)S(1)} %bitcast.409), kind=kOutput, calls=%fused_computation.1 | convolution fusion | flops 8056995840 | bytes 16252928 | tf_op jit(solution)/shard_map/dot_general | solution.py:25
  309.0 5.0 pad_maximum_fusion
  314.0 4.4 collective-permute-done.13
  318.4 2.8 convert_add_fusion.4
  322.5 1.9 multiply_reduce_fusion.1
  329.6 2.3 collective-permute-done.15
  333.8 13.9 %collective-permute-done.14 = bf16[256,1536]{1,0:T(8,128)(2,1)S(1)} collective-permute-done((bf16[256,1536]{1,0:T(8,128)(2,1)S(1)}, bf16[256,1536]{1,0:T(8,128)(2,1)S(1)}, u32[]{:S(2)}, u32[]{:S(2)}) %collective-permute-start.14) | collective-permute-done | bytes 786464 | tf_op jit(solution)/shard_map/ppermute | solution.py:32
  347.7 2.0 collective-permute-start.16
  349.7 5.1 all-to-all-start.3
  355.0 3.8 pad_maximum_fusion.2.refs_3_
  358.9 18.1 %attention_backward.1 = (bf16[1024,1536]{1,0:T(8,128)(2,1)S(1)}, bf16[1024,640]{1,0:T(8,128)(2,1)S(1)}, bf16[1024,1536]{1,0:T(8,128)(2,1)}, f32[1,1536]{1,0:T(1,128)S(1)}) custom-call(bf16[512,1536]{1,0:T(8,128)(2,1)S(1)} %constant_dynamic-update-slice_fusion.62.refs_0_, bf16[512,1536]{1,0:T(8,128)(2,1)} %collective-permute-done.16.refs_1_, ...), custom_call_target="tpu_custom_call" | custom-call | flops 3221225472 | bytes 21495808 | tf_op jit(solution)/shard_map/attention_backward/pallas_call | solution.py:303
  380.1 2.7 slice.490
  383.1 2.0 convert_reduce_fusion
  385.0 2.1 fusion.9
  388.4 2.6 copy.321
  391.0 6.9 %all-to-all-start.4 = ((bf16[128,24,128]{2,1,0:T(8,128)(2,1)}), bf16[128,24,128]{2,1,0:T(8,128)(2,1)}, u32[]{:S(2)}, u32[]{:S(2)}) async-start(bf16[128,24,128]{2,1,0:T(8,128)(2,1)} %copy.321), calls=%async_computation.4 | async-start | bytes 1572864 | tf_op jit(solution)/shard_map/all_to_all | solution.py:532
  397.9 3.6 convolution_convert_fusion.5
  401.9 4.6 convolution_convert_fusion.4
  406.5 1.9 pad_maximum_fusion.3
  409.6 1.9 convert_add_fusion
  411.5 10.0 %all-to-all-done.4 = bf16[128,24,128]{2,1,0:T(8,128)(2,1)} async-done(((bf16[128,24,128]{2,1,0:T(8,128)(2,1)}), bf16[128,24,128]{2,1,0:T(8,128)(2,1)}, u32[]{:S(2)}, u32[]{:S(2)}) %all-to-all-start.4) | async-done | bytes 786464 | tf_op jit(solution)/shard_map/all_to_all | solution.py:532
  421.5 4.7 copy.324
  426.2 4.2 pad_maximum_fusion.1
  430.5 4.5 all-to-all-start.5
  435.7 17.4 %collective-permute-done.18 = bf16[256,1536]{1,0:T(8,128)(2,1)S(1)} collective-permute-done((bf16[256,1536]{1,0:T(8,128)(2,1)S(1)}, bf16[256,1536]{1,0:T(8,128)(2,1)S(1)}, u32[]{:S(2)}, u32[]{:S(2)}) %collective-permute-start.18) | collective-permute-done | bytes 786464 | tf_op jit(solution)/shard_map/ppermute | solution.py:32
  455.0 26.1 %all-to-all-done.5 = bf16[16,112,1024]{2,1,0:T(8,128)(2,1)} async-done(((bf16[16,112,1024]{2,1,0:T(8,128)(2,1)}), bf16[16,112,1024]{2,1,0:T(8,128)(2,1)}, u32[]{:S(2)}, u32[]{:S(2)}) %all-to-all-start.5) | async-done | bytes 3670048 | tf_op jit(solution)/shard_map/all_to_all | solution.py:114
  481.1 2.8 reduce
  486.3 4.7 collective-permute-start.20
  491.1 2.2 collective-permute-start.21
  493.3 2.4 collective-permute-start.22
  495.6 2.1 fusion.10
  499.4 19.0 %all-to-all-start.6 = ((bf16[128,24,128]{2,1,0:T(8,128)(2,1)}), bf16[128,24,128]{2,1,0:T(8,128)(2,1)S(1)}, u32[]{:S(2)}, u32[]{:S(2)}) async-start(bf16[128,24,128]{2,1,0:T(8,128)(2,1)} %copy.330), calls=%async_computation.7 | async-start | bytes 1572864 | tf_op jit(solution)/shard_map/all_to_all | solution.py:544
  518.4 12.1 %collective-permute-done.22 = bf16[24,5504]{1,0:T(8,128)(2,1)} collective-permute-done((bf16[24,5504]{1,0:T(8,128)(2,1)S(1)}, bf16[24,5504]{1,0:T(8,128)(2,1)}, u32[]{:S(2)}, u32[]{:S(2)}) %collective-permute-start.22) | collective-permute-done | bytes 264224 | tf_op jit(solution)/shard_map/ppermute | solution.py:92
  535.4 6.2 %collective-permute-done.24 = f32[24,640]{1,0:T(8,128)S(1)} collective-permute-done((f32[24,640]{1,0:T(8,128)S(1)}, f32[24,640]{1,0:T(8,128)S(1)}, u32[]{:S(2)}, u32[]{:S(2)}) %collective-permute-start.24) | collective-permute-done | bytes 61472 | tf_op jit(solution)/shard_map/ppermute | solution.py:32
  543.8 3.9 all_to_all.41
  (314 shorter events, 85.8 us)
Async XLA Ops:
  7.2 27.3 %copy-start = (s32[2,256,1,6]{1,2,3,0:T(1,128)S(1)}, s32[2,256,1,6]{1,2,3,0:T(1,128)}, u32[]{:S(2)}) copy-start(s32[2,256,1,6]{1,2,3,0:T(1,128)} %param.22) | copy-start | bytes 36868
  7.2 27.3 %copy-start.35 = (s32[2,256]{1,0:T(2,128)S(1)}, s32[2,256]{1,0:T(2,128)}, u32[]{:S(2)}) copy-start(s32[2,256]{1,0:T(2,128)} %param.20) | copy-start | bytes 6148
  7.2 27.4 %copy-start.25 = (bf16[2,128,1,1536]{3,1,2,0:T(8,128)(2,1)S(1)}, bf16[2,128,1,1536]{3,1,2,0:T(8,128)(2,1)}, u32[]{:S(2)}) copy-start(bf16[2,128,1,1536]{3,1,2,0:T(8,128)(2,1)} %param.18) | copy-start | bytes 2359300
  7.2 157.2 %all-gather.3.cloned.1.call-start = ((), (), s32[]{:S(2)}) async-start(), calls=%async_computation.9 | async-start | bytes 3342336 | tf_op jit(solution)/shard_map/all_gather | solution.py:100
  16.3 18.7 %copy-start.26 = (bf16[2,128,1,1536]{3,1,2,0:T(8,128)(2,1)S(1)}, bf16[2,128,1,1536]{3,1,2,0:T(8,128)(2,1)}, u32[]{:S(2)}) copy-start(bf16[2,128,1,1536]{3,1,2,0:T(8,128)(2,1)} %param.19) | copy-start | bytes 2359300
  24.1 11.3 %copy-start.36 = (s32[2,2,128]{2,1,0:T(2,128)S(1)}, s32[2,2,128]{2,1,0:T(2,128)}, u32[]{:S(2)}) copy-start(s32[2,2,128]{2,1,0:T(2,128)} %param.21) | copy-start | bytes 6148
  24.1 11.9 %collective-permute-start.3 = (bf16[24,4864]{1,0:T(8,128)(2,1)}, bf16[24,4864]{1,0:T(8,128)(2,1)}, u32[]{:S(2)}, u32[]{:S(2)}) collective-permute-start(bf16[24,4864]{1,0:T(8,128)(2,1)} %reshape.299), channel_id=1, source_target_pairs={{0,33},{1,49},{16,32},{17,48},{32,1},{33,17},{48,0},{49,16},{2,35}... | collective-permute-start | bytes 700424 | tf_op jit(solution)/shard_map/ppermute | solution.py:78
  28.4 15.0 %collective-permute-start.2 = (bf16[24,4864]{1,0:T(8,128)(2,1)}, bf16[24,4864]{1,0:T(8,128)(2,1)}, u32[]{:S(2)}, u32[]{:S(2)}) collective-permute-start(bf16[24,4864]{1,0:T(8,128)(2,1)} %reshape.299), channel_id=1, source_target_pairs={{0,32},{1,48},{16,33},{17,49},{32,0},{33,16},{48,1},{49,17},{2,34}... | collective-permute-start | bytes 700424 | tf_op jit(solution)/shard_map/ppermute | solution.py:78
  29.6 19.3 %collective-permute-start.1 = (bf16[24,4864]{1,0:T(8,128)(2,1)}, bf16[24,4864]{1,0:T(8,128)(2,1)}, u32[]{:S(2)}, u32[]{:S(2)}) collective-permute-start(bf16[24,4864]{1,0:T(8,128)(2,1)} %reshape.299), channel_id=1, source_target_pairs={{0,1},{1,17},{16,0},{17,16},{32,33},{33,49},{48,32},{49,48},{2,3},... | collective-permute-start | bytes 700424 | tf_op jit(solution)/shard_map/ppermute | solution.py:78
  30.9 17.9 %collective-permute-start = (bf16[24,4864]{1,0:T(8,128)(2,1)}, bf16[24,4864]{1,0:T(8,128)(2,1)}, u32[]{:S(2)}, u32[]{:S(2)}) collective-permute-start(bf16[24,4864]{1,0:T(8,128)(2,1)} %reshape.299), channel_id=1, source_target_pairs={{0,0},{1,16},{16,1},{17,17},{32,32},{33,48},{48,33},{49,49},{2,2},... | collective-permute-start | bytes 700424 | tf_op jit(solution)/shard_map/ppermute | solution.py:78
  50.9 201.4 %all-gather.5.cloned.1.call-start = ((), (), s32[]{:S(2)}) async-start(), calls=%async_computation.10 | async-start | bytes 12533760 | tf_op jit(solution)/shard_map/all_gather | solution.py:100
  54.7 21.6 %copy-start.32 = (f32[1536]{0:T(1024)S(1)}, f32[1536]{0:T(1024)}, u32[]{:S(2)}) copy-start(f32[1536]{0:T(1024)} %param.23) | copy-start | bytes 18436
  54.7 21.7 %copy-start.33 = (f32[1536]{0:T(1024)S(1)}, f32[1536]{0:T(1024)}, u32[]{:S(2)}) copy-start(f32[1536]{0:T(1024)} %param.24) | copy-start | bytes 18436
  54.7 21.8 %copy-start.31 = (bf16[1536,8]{0,1:T(8,128)(2,1)S(1)}, bf16[1536,8]{0,1:T(8,128)(2,1)}, u32[]{:S(2)}) copy-start(bf16[1536,8]{0,1:T(8,128)(2,1)} %param.29) | copy-start | bytes 73732
  54.7 68.0 %all-to-all-start.1 = ((bf16[128,50,128]{2,1,0:T(8,128)(2,1)}), bf16[128,50,128]{2,1,0:T(8,128)(2,1)S(1)}, u32[]{:S(2)}, u32[]{:S(2)}) async-start(bf16[128,50,128]{2,1,0:T(8,128)(2,1)} %copy.306), calls=%async_computation.1 | async-start | bytes 3670016 | tf_op jit(solution)/shard_map/all_to_all | solution.py:434
  124.8 6.0 %copy-start.14 = (bf16[128,50,128]{0,2,1:T(8,128)(2,1)}, bf16[128,50,128]{0,2,1:T(8,128)(2,1)S(1)}, u32[]{:S(2)}) copy-start(bf16[128,50,128]{0,2,1:T(8,128)(2,1)S(1)} %copy.307) | copy-start | bytes 4915204
  124.9 15.6 %collective-permute-start.5 = (f32[2,8]{1,0:T(2,128)S(1)}, f32[2,8]{1,0:T(2,128)S(1)}, u32[]{:S(2)}, u32[]{:S(2)}) collective-permute-start(f32[2,8]{1,0:T(2,128)S(1)} %convert_reduce_fusion.1), channel_id=1, source_target_pairs={{0,1},{1,0},{2,3},{3,2},{4,5},{5,4},{6,7},{7,6},{8,9},{9,8},{10,11... | collective-permute-start | bytes 200 | tf_op jit(solution)/shard_map/ppermute | solution.py:32
  135.3 79.5 %copy-start.5 = (f32[256,1536]{1,0:T(8,128)}, f32[256,1536]{1,0:T(8,128)S(1)}, u32[]{:S(2)}) copy-start(f32[256,1536]{1,0:T(8,128)S(1)} %get-tuple-element.256) | copy-start | bytes 4718596
  135.6 18.0 %copy-start.13 = (bf16[256,1536]{1,0:T(8,128)(2,1)}, bf16[256,1536]{1,0:T(8,128)(2,1)S(1)}, u32[]{:S(2)}) copy-start(bf16[256,1536]{1,0:T(8,128)(2,1)S(1)} %multiply_convert_fusion.2) | copy-start | bytes 2359300
  135.6 18.0 %collective-permute-start.4 = (bf16[256,1536]{1,0:T(8,128)(2,1)S(1)}, bf16[256,1536]{1,0:T(8,128)(2,1)}, u32[]{:S(2)}, u32[]{:S(2)}) collective-permute-start(bf16[256,1536]{1,0:T(8,128)(2,1)S(1)} %multiply_convert_fusion.2), channel_id=1, source_target_pairs={{0,16},{16,0},{1,17},{17,1},{2,18},{18,2},{3,19},{19,3},{4,20},{20... | collective-permute-start | bytes 2359304 | tf_op jit(solution)/shard_map/ppermute | solution.py:32
  156.0 8.4 %collective-permute-start.6 = (bf16[512,1536]{1,0:T(8,128)(2,1)}, bf16[512,1536]{1,0:T(8,128)(2,1)}, u32[]{:S(2)}, u32[]{:S(2)}) collective-permute-start(bf16[512,1536]{1,0:T(8,128)(2,1)} %pad_maximum_fusion.4), channel_id=1, source_target_pairs={{0,2},{2,0},{1,3},{3,1},{4,6},{6,4},{5,7},{7,5},{8,10},{10,8},{9,1... | collective-permute-start | bytes 4718600 | tf_op jit(solution)/shard_map/ppermute | solution.py:32
  159.7 25.5 %all-to-all-start.2 = ((bf16[2,256,1664]{2,1,0:T(8,128)(2,1)}), bf16[2,256,1664]{2,1,0:T(8,128)(2,1)}, u32[]{:S(2)}, u32[]{:S(2)}) async-start(bf16[2,256,1664]{2,1,0:T(8,128)(2,1)} %broadcast_in_dim.34), calls=%async_computation.2 | async-start | bytes 3407872 | tf_op jit(solution)/shard_map/all_to_all | solution.py:475
  164.4 319.7 %reduce-scatter.2.cloned.1.call-start = ((), (), s32[]{:S(2)}) async-start(), calls=%async_computation.11 | async-start | bytes 12533760 | tf_op jit(solution)/shard_map/reduce_scatter | solution.py:104
  188.8 7.0 %copy-start.30 = (f32[1,4,4,2,2,24]{5,2,4,3,1,0:T(4,128)S(1)}, f32[1,4,4,2,2,24]{5,2,4,3,1,0:T(4,128)}, u32[]{:S(2)}) copy-start(f32[1,4,4,2,2,24]{5,2,4,3,1,0:T(4,128)} %get-tuple-element.184) | copy-start | bytes 18436
  188.8 3.9 collective-permute-start.7
  195.8 19.1 %collective-permute-start.8 = (bf16[256,1536]{1,0:T(8,128)(2,1)}, bf16[256,1536]{1,0:T(8,128)(2,1)}, u32[]{:S(2)}, u32[]{:S(2)}) collective-permute-start(bf16[256,1536]{1,0:T(8,128)(2,1)} %slice.676), channel_id=1, source_target_pairs={{0,16},{16,0},{1,17},{17,1},{2,18},{18,2},{3,19},{19,3},{4,20},{20... | collective-permute-start | bytes 2359304 | tf_op jit(solution)/shard_map/ppermute | solution.py:32
  218.3 27.3 %collective-permute-start.9 = (bf16[256,1536]{1,0:T(8,128)(2,1)S(1)}, bf16[256,1536]{1,0:T(8,128)(2,1)S(1)}, u32[]{:S(2)}, u32[]{:S(2)}) collective-permute-start(bf16[256,1536]{1,0:T(8,128)(2,1)S(1)} %multiply_convert_fusion.1), channel_id=1, source_target_pairs={{0,16},{16,0},{1,17},{17,1},{2,18},{18,2},{3,19},{19,3},{4,20},{20... | collective-permute-start | bytes 2359304 | tf_op jit(solution)/shard_map/ppermute | solution.py:32
  231.4 19.7 %collective-permute-start.11 = (bf16[512,1664]{1,0:T(8,128)(2,1)}, bf16[512,1664]{1,0:T(8,128)(2,1)}, u32[]{:S(2)}, u32[]{:S(2)}) collective-permute-start(bf16[512,1664]{1,0:T(8,128)(2,1)} %bitcast.78.refs_2_), channel_id=1, source_target_pairs={{0,2},{2,0},{1,3},{3,1},{4,6},{6,4},{5,7},{7,5},{8,10},{10,8},{9,1... | collective-permute-start | bytes 5111816 | tf_op jit(solution)/shard_map/ppermute | solution.py:32
  246.8 5.5 collective-permute-start.10
  288.2 2.4 copy-start.37
  288.2 11.5 %slice-start = ((s8[5242880]{0:T(1024)(128)(4,1)}), s8[4194304]{0:T(1024)(128)(4,1)S(1)}, s32[]{:S(2)}) async-start(s8[5242880]{0:T(1024)(128)(4,1)} %bitcast.408), calls=%async_computation.12 | async-start | bytes 8388608
  289.9 7.3 %collective-permute-start.12 = (bf16[512,1536]{1,0:T(8,128)(2,1)S(1)}, bf16[512,1536]{1,0:T(8,128)(2,1)S(1)}, u32[]{:S(2)}, u32[]{:S(2)}) collective-permute-start(bf16[512,1536]{1,0:T(8,128)(2,1)S(1)} %slice.483), channel_id=1, source_target_pairs={{0,2},{2,0},{1,3},{3,1},{4,6},{6,4},{5,7},{7,5},{8,10},{10,8},{9,1... | collective-permute-start | bytes 4718600 | tf_op jit(solution)/shard_map/ppermute | solution.py:32
  290.6 6.7 %copy-start.20 = (bf16[1024,1536]{1,0:T(8,128)(2,1)S(1)}, bf16[1024,1536]{1,0:T(8,128)(2,1)}, u32[]{:S(2)}) copy-start(bf16[1024,1536]{1,0:T(8,128)(2,1)} %get-tuple-element.58) | copy-start | bytes 9437188
  290.6 9.1 %slice-start.1 = ((s8[5242880]{0:T(1024)(128)(4,1)}), s8[1048576]{0:T(1024)(128)(4,1)S(1)}, s32[]{:S(2)}) async-start(s8[5242880]{0:T(1024)(128)(4,1)} %bitcast.408), calls=%async_computation.13 | async-start | bytes 2097152
  297.2 3.0 copy-start.18
  299.5 18.8 %collective-permute-start.13 = (bf16[256,1536]{1,0:T(8,128)(2,1)S(1)}, bf16[256,1536]{1,0:T(8,128)(2,1)S(1)}, u32[]{:S(2)}, u32[]{:S(2)}) collective-permute-start(bf16[256,1536]{1,0:T(8,128)(2,1)S(1)} %slice.675), channel_id=1, source_target_pairs={{0,16},{16,0},{1,17},{17,1},{2,18},{18,2},{3,19},{19,3},{4,20},{20... | collective-permute-start | bytes 2359304 | tf_op jit(solution)/shard_map/ppermute | solution.py:32
  322.5 2.4 copy-start.22
  324.9 2.7 copy-start.16
  324.9 4.0 copy-start.29
  326.5 2.5 copy-start.19
  327.7 4.2 collective-permute-start.15
  329.5 18.1 %collective-permute-start.14 = (bf16[256,1536]{1,0:T(8,128)(2,1)S(1)}, bf16[256,1536]{1,0:T(8,128)(2,1)S(1)}, u32[]{:S(2)}, u32[]{:S(2)}) collective-permute-start(bf16[256,1536]{1,0:T(8,128)(2,1)S(1)} %get-tuple-element.67), channel_id=1, source_target_pairs={{0,16},{16,0},{1,17},{17,1},{2,18},{18,2},{3,19},{19,3},{4,20},{20... | collective-permute-start | bytes 2359304 | tf_op jit(solution)/shard_map/ppermute | solution.py:32
  347.7 11.1 %collective-permute-start.16 = (bf16[512,1536]{1,0:T(8,128)(2,1)S(1)}, bf16[512,1536]{1,0:T(8,128)(2,1)}, u32[]{:S(2)}, u32[]{:S(2)}) collective-permute-start(bf16[512,1536]{1,0:T(8,128)(2,1)S(1)} %constant_dynamic-update-slice_fusion.62.refs_0_), channel_id=1, source_target_pairs={{0,2},{2,0},{1,3},{3,1},{4,6},{6,4},{5,7},{7,5},{8,10},{10,8},{9,1... | collective-permute-start | bytes 4718600 | tf_op jit(solution)/shard_map/ppermute | solution.py:32
  349.7 30.0 %all-to-all-start.3 = ((bf16[2,256,1536]{2,1,0:T(8,128)(2,1)}), bf16[2,256,1536]{2,1,0:T(8,128)(2,1)}, u32[]{:S(2)}, u32[]{:S(2)}) async-start(bf16[2,256,1536]{2,1,0:T(8,128)(2,1)} %reverse_select_fusion.1), calls=%async_computation.3 | async-start | bytes 3145728 | tf_op jit(solution)/shard_map/all_to_all | solution.py:528
  355.0 3.8 copy-start.34
  382.8 2.2 copy-start.9
  382.8 25.6 %collective-permute-start.17 = (bf16[512,1536]{1,0:T(8,128)(2,1)}, bf16[512,1536]{1,0:T(8,128)(2,1)}, u32[]{:S(2)}, u32[]{:S(2)}) collective-permute-start(bf16[512,1536]{1,0:T(8,128)(2,1)} %slice.490), channel_id=1, source_target_pairs={{0,2},{2,0},{1,3},{3,1},{4,6},{6,4},{5,7},{7,5},{8,10},{10,8},{9,1... | collective-permute-start | bytes 4718600 | tf_op jit(solution)/shard_map/ppermute | solution.py:32
  388.4 9.5 %copy-start.3 = (bf16[1024,1536]{1,0:T(8,128)(2,1)S(1)}, bf16[1024,1536]{1,0:T(8,128)(2,1)}, u32[]{:S(2)}) copy-start(bf16[1024,1536]{1,0:T(8,128)(2,1)} %copy-done.2) | copy-start | bytes 9437188
  391.0 30.5 %all-to-all-start.4 = ((bf16[128,24,128]{2,1,0:T(8,128)(2,1)}), bf16[128,24,128]{2,1,0:T(8,128)(2,1)}, u32[]{:S(2)}, u32[]{:S(2)}) async-start(bf16[128,24,128]{2,1,0:T(8,128)(2,1)} %copy.321), calls=%async_computation.4 | async-start | bytes 1572864 | tf_op jit(solution)/shard_map/all_to_all | solution.py:532
  401.9 4.6 copy-start.23
  406.5 3.0 copy-start.17
  430.5 50.6 %all-to-all-start.5 = ((bf16[16,112,1024]{2,1,0:T(8,128)(2,1)}), bf16[16,112,1024]{2,1,0:T(8,128)(2,1)}, u32[]{:S(2)}, u32[]{:S(2)}) async-start(bf16[16,112,1024]{2,1,0:T(8,128)(2,1)} %pad_maximum_fusion.1), calls=%async_computation.5 | async-start | bytes 7340032 | tf_op jit(solution)/shard_map/all_to_all | solution.py:114
  435.0 18.2 %copy-start.6 = (f32[256,1536]{1,0:T(8,128)S(1)}, f32[256,1536]{1,0:T(8,128)}, u32[]{:S(2)}) copy-start(f32[256,1536]{1,0:T(8,128)} %copy-done.5) | copy-start | bytes 4718596
  435.1 18.5 %copy-start.15 = (f32[256,1536]{1,0:T(8,128)S(1)}, f32[256,1536]{1,0:T(8,128)}, u32[]{:S(2)}) copy-start(f32[256,1536]{1,0:T(8,128)} %get-tuple-element.167) | copy-start | bytes 4718596
  435.1 18.1 %collective-permute-start.18 = (bf16[256,1536]{1,0:T(8,128)(2,1)S(1)}, bf16[256,1536]{1,0:T(8,128)(2,1)S(1)}, u32[]{:S(2)}, u32[]{:S(2)}) collective-permute-start(bf16[256,1536]{1,0:T(8,128)(2,1)S(1)} %slice.674), channel_id=1, source_target_pairs={{0,16},{16,0},{1,17},{17,1},{2,18},{18,2},{3,19},{19,3},{4,20},{20... | collective-permute-start | bytes 2359304 | tf_op jit(solution)/shard_map/ppermute | solution.py:32
  485.3 10.4 %copy-start.28 = (bf16[256,1536]{1,0:T(8,128)(2,1)S(1)}, bf16[256,1536]{1,0:T(8,128)(2,1)}, u32[]{:S(2)}) copy-start(bf16[256,1536]{1,0:T(8,128)(2,1)} %add_convert_fusion) | copy-start | bytes 2359300
  485.5 32.8 %collective-permute-start.19 = (bf16[24,5504]{1,0:T(8,128)(2,1)S(1)}, bf16[24,5504]{1,0:T(8,128)(2,1)S(1)}, u32[]{:S(2)}, u32[]{:S(2)}) collective-permute-start(bf16[24,5504]{1,0:T(8,128)(2,1)S(1)} %get-tuple-element.237), channel_id=1, source_target_pairs={{0,0},{16,1},{1,16},{17,17},{32,32},{48,33},{33,48},{49,49},{2,2},... | collective-permute-start | bytes 792584 | tf_op jit(solution)/shard_map/ppermute | solution.py:92
  486.3 32.0 %collective-permute-start.20 = (bf16[24,5504]{1,0:T(8,128)(2,1)S(1)}, bf16[24,5504]{1,0:T(8,128)(2,1)S(1)}, u32[]{:S(2)}, u32[]{:S(2)}) collective-permute-start(bf16[24,5504]{1,0:T(8,128)(2,1)S(1)} %get-tuple-element.238), channel_id=1, source_target_pairs={{1,0},{17,1},{0,16},{16,17},{33,32},{49,33},{32,48},{48,49},{3,2},... | collective-permute-start | bytes 792584 | tf_op jit(solution)/shard_map/ppermute | solution.py:92
  491.1 27.3 %collective-permute-start.21 = (bf16[24,5504]{1,0:T(8,128)(2,1)S(1)}, bf16[24,5504]{1,0:T(8,128)(2,1)S(1)}, u32[]{:S(2)}, u32[]{:S(2)}) collective-permute-start(bf16[24,5504]{1,0:T(8,128)(2,1)S(1)} %get-tuple-element.239), channel_id=1, source_target_pairs={{32,0},{48,1},{33,16},{49,17},{0,32},{16,33},{1,48},{17,49},{34,2}... | collective-permute-start | bytes 792584 | tf_op jit(solution)/shard_map/ppermute | solution.py:92
  493.3 37.2 %collective-permute-start.22 = (bf16[24,5504]{1,0:T(8,128)(2,1)S(1)}, bf16[24,5504]{1,0:T(8,128)(2,1)}, u32[]{:S(2)}, u32[]{:S(2)}) collective-permute-start(bf16[24,5504]{1,0:T(8,128)(2,1)S(1)} %get-tuple-element.240), channel_id=1, source_target_pairs={{33,0},{49,1},{32,16},{48,17},{1,32},{17,33},{0,48},{16,49},{35,2}... | collective-permute-start | bytes 792584 | tf_op jit(solution)/shard_map/ppermute | solution.py:92
  499.4 44.3 %all-to-all-start.6 = ((bf16[128,24,128]{2,1,0:T(8,128)(2,1)}), bf16[128,24,128]{2,1,0:T(8,128)(2,1)S(1)}, u32[]{:S(2)}, u32[]{:S(2)}) async-start(bf16[128,24,128]{2,1,0:T(8,128)(2,1)} %copy.330), calls=%async_computation.7 | async-start | bytes 1572864 | tf_op jit(solution)/shard_map/all_to_all | solution.py:544
  531.5 2.5 collective-permute-start.23
  534.0 7.6 %collective-permute-start.24 = (f32[24,640]{1,0:T(8,128)S(1)}, f32[24,640]{1,0:T(8,128)S(1)}, u32[]{:S(2)}, u32[]{:S(2)}) collective-permute-start(f32[24,640]{1,0:T(8,128)S(1)} %slice_add_fusion.1), channel_id=1, source_target_pairs={{0,1},{1,0},{2,3},{3,2},{4,5},{5,4},{6,7},{7,6},{8,9},{9,8},{10,11... | collective-permute-start | bytes 184328 | tf_op jit(solution)/shard_map/ppermute | solution.py:32
  548.3 7.9 %copy-start.1 = (s32[2,256,1,6]{1,2,3,0:T(1,128)S(1)}, s32[2,256,1,6]{1,2,3,0:T(1,128)}, u32[]{:S(2)}) copy-start(s32[2,256,1,6]{1,2,3,0:T(1,128)} %param.22) | copy-start | bytes 36868
  (10 other events, 14.4 us)
Sparse Core Ops, SparseCore 0:
  51.1 76.5 all-gather.2
  130.1 90.5 all-gather.4
  321.3 97.1 reduce-scatter.1

commit v4 on v3

--- a/solution.py
+++ b/solution.py
@@ -79,21 +79,14 @@
     )
 
 
-def z_scattered(near, small):
+def z_scattered(near):
     routes = z_routes()
-    rows = near.shape[0] // len(routes)
-    cols = near.shape[1]
-    pieces = near.reshape(len(routes), rows, cols)
-    lines = small.astype(BF16).reshape(rows, -1)
+    pieces = near.reshape(len(routes), -1, near.shape[1])
     total = 0.0
     for piece, pairs in zip(pieces, routes):
         back = [(goal, start) for start, goal in pairs]
-        sent = jnp.concatenate([piece, lines], axis=1)
-        total = total + lax.ppermute(sent, ("z1", "z0", "zh"), back).astype(F32)
-    small_sum = total[:, cols:]
-    small_sum = small_sum + swapped(small_sum, "c")
-    small_sum = small_sum + swapped(small_sum, "zh")
-    return total[:, :cols].astype(BF16), small_sum.reshape(small.shape)
+        total = total + lax.ppermute(piece, ("z1", "z0", "zh"), back).astype(F32)
+    return total
 
 
 def xy_gathered(near):
@@ -104,17 +97,17 @@
     return lax.psum_scatter(total, ("x", "y"), scatter_dimension=0, tiled=True)
 
 
-def xy_scattered_apart(total, small):
-    count = lax.axis_size(("x", "y"))
-    cols = total.shape[1]
-    pieces = total.reshape(count, -1, cols)
-    lines = -(-small.size // (8 * cols)) * 8
-    flat = jnp.pad(small.astype(BF16).reshape(-1), (0, lines * cols - small.size))
-    flat = jnp.broadcast_to(flat.reshape(1, lines, cols), (count, lines, cols))
-    got = lax.all_to_all(jnp.concatenate([pieces, flat], axis=1), ("x", "y"), 0, 0, tiled=True)
-    summed = jnp.sum(got.astype(F32), axis=0)
-    rows = pieces.shape[1]
-    return summed[:rows].astype(BF16), summed[rows:].reshape(-1)[: small.size].reshape(small.shape)
+def in_lines(small, cols):
+    first = min(small.shape[1], cols)
+    lines = jnp.pad(small[:, :first], ((0, 0), (0, cols - first)))
+    lines = jnp.concatenate([lines, small[:, first:].reshape(-1, cols)], axis=0)
+    return jnp.pad(lines, ((0, 16 - lines.shape[0]), (0, 0)))
+
+
+def from_lines(lines, rows, width):
+    first = min(width, lines.shape[1])
+    rest = lines[rows : rows + rows * (width - first) // lines.shape[1]]
+    return jnp.concatenate([lines[:rows, :first], rest.reshape(rows, -1)], axis=1)
 
 
 def expert_kernel(
@@ -314,12 +307,50 @@
         + [jax.ShapeDtypeStruct((1, width), F32)],
         compiler_params=pltpu.CompilerParams(vmem_limit_bytes=44 << 20),
         cost_estimate=pl.CostEstimate(
-            flops=2 * rows * width * attn_w.shape[1],
+            flops=12 * rows * width * attn_w.shape[1],
             transcendentals=rows * seq_len * GROUP,
             bytes_accessed=2 * (attn_w.size + rows * (5 * width + 2 * cols)),
         ),
         name="attention_backward",
     )(pair, other, qkv, n1, attn_w)
+
+
+def gradients_kernel(n1_ref, dattn_ref, dqkv_ref, mixed_ref, lines_ref, out_ref):
+    blocks = out_ref.shape[0]
+    rows = n1_ref.shape[1] // blocks
+    split = dqkv_ref.shape[1]
+    qkv = dot(n1_ref[...], dqkv_ref[...], (0, 0), BF16)
+    out = dot(dattn_ref[...], mixed_ref[...], (0, 0), BF16)
+    for b in range(blocks):
+        out_ref[b, :rows, :split] = qkv[b * rows : (b + 1) * rows]
+        out_ref[b, :rows, split:] = out[b * rows : (b + 1) * rows]
+        out_ref[b, rows:, :] = lines_ref[...]
+
+
+def attention_gradients(n1, dqkv, dattn, mixed, small, places):
+    rows, width = n1.shape
+    cols = dqkv.shape[1] + mixed.shape[1]
+    lines = width // places + small.shape[0]
+    step = width // 4
+
+    def whole(value):
+        return pl.BlockSpec(value.shape, lambda i: (0, 0), pipeline_mode=pl.Buffered(1))
+
+    by_features = pl.BlockSpec((rows, step), lambda i: (0, i))
+    return pl.pallas_call(
+        gradients_kernel,
+        grid=(4,),
+        in_specs=[by_features, by_features, whole(dqkv), whole(mixed), whole(small)],
+        out_specs=pl.BlockSpec((places // 4, lines, cols), lambda i: (i, 0, 0)),
+        out_shape=jax.ShapeDtypeStruct((places, lines, cols), BF16),
+        compiler_params=pltpu.CompilerParams(vmem_limit_bytes=40 << 20),
+        cost_estimate=pl.CostEstimate(
+            flops=2 * rows * width * cols,
+            transcendentals=0,
+            bytes_accessed=2 * (2 * rows * width + rows * cols + places * lines * cols),
+        ),
+        name="attention_gradients",
+    )(n1, dattn, dqkv, mixed, small)
 
 
 def attention_scores(query, key):
@@ -378,12 +409,6 @@
         halves(s_down.T),
     ]
     attn_cols = sum(p[0].shape[1] for p in attn_parts)
-    both_shards = jnp.stack(
-        [jnp.concatenate([p[c] for p in attn_parts + ffn_parts], axis=1) for c in (0, 1)]
-    )
-    chip_rows = lax.all_to_all(both_shards, "c", 0, 0, tiled=True)
-    chip_rows = chip_rows.reshape(2 * rows_here, -1)
-    near_w = z_gathered(chip_rows)
     q_cols = query_matrix.shape[1] // 2
     k_cols = key_matrix.shape[1] // 2
     qkv_cols = q_cols + 2 * k_cols
@@ -412,6 +437,13 @@
     ) * unit + iota % unit
     features = (iota[:, None] == mate[None, :]).astype(BF16)
 
+    def both_cores(chip):
+        low = chip.astype(BF16)
+        kept = jnp.where(core == 0, low[:rows_here], low[rows_here:])
+        got = swapped(jnp.where(core == 0, low[rows_here:], low[:rows_here]), "c")
+        pair = jnp.where(core == 0, jnp.stack([kept, got]), jnp.stack([got, kept]))
+        return pair.astype(F32)
+
     order = lax.dynamic_index_in_dim(perm, t, 1, False)
     deal = (order[:, :, None] == jnp.arange(seqs, dtype=jnp.int32)[None, None, :]).astype(BF16)
     own_routes = lax.dynamic_slice_in_dim(routes[:, :, 0], t * seqs, seqs, 1)
@@ -424,50 +456,71 @@
         [jnp.logical_and(named, own_valid[:, :, None]), own_valid[:, :, None]], axis=2
     ).astype(BF16)
     marks = jnp.pad(marks, ((0, 0), (0, 0), (0, 128 - marks.shape[2])))
-    rows_in = jnp.concatenate([tokens[:, :, 0], marks, cotangent[:, :, 0]], axis=2)
-    sent = jnp.einsum("mjs,msd->jmd", deal, rows_in, preferred_element_type=F32)
-    sent = sent.astype(BF16).reshape(seqs, -1, 128)
-    near_w, sent = lax.optimization_barrier((near_w, sent))
+
+    def dealt(value):
+        sent = jnp.einsum("mjs,msd->jmd", deal, value, preferred_element_type=F32)
+        return sent.astype(BF16).reshape(seqs, -1, 128)
+
+    def arrived(got):
+        return jnp.swapaxes(got.reshape(seq_len, batches, -1), 0, 1)
+
+    tokens_sent = dealt(jnp.concatenate([tokens[:, :, 0], marks], axis=2))
+    tokens_got = lax.all_to_all(tokens_sent, DP, 0, 0, tiled=True)
+    shards = [
+        jnp.concatenate([p[c] for p in attn_parts + ffn_parts], axis=1) for c in (0, 1)
+    ]
+    core = lax.axis_index("c")
+    kept_shard = jnp.where(core == 0, shards[0], shards[1])
+    got_shard = swapped(jnp.where(core == 0, shards[1], shards[0]), "c")
+    chip_rows = jnp.where(
+        core == 0,
+        jnp.concatenate([kept_shard, got_shard], axis=0),
+        jnp.concatenate([got_shard, kept_shard], axis=0),
+    )
+    cot_sent = dealt(cotangent[:, :, 0])
+    near_w, tokens_got, cot_sent = lax.optimization_barrier(
+        (z_gathered(chip_rows), tokens_got, cot_sent)
+    )
     attn_w = xy_gathered(near_w[:, :attn_cols])
     ffn_w = xy_gathered(near_w[:, attn_cols:])
     qkv_w, out_w = attn_w[:, :qkv_cols], attn_w[:, qkv_cols:]
-    got = lax.all_to_all(sent, DP, 0, 0, tiled=True)
-    got = got.reshape(seq_len, batches, -1)
-    own_in = jnp.swapaxes(got, 0, 1)
+    own_in = arrived(tokens_got)
     x_own = dot(own_in[:, :, :width].reshape(batches * seq_len, width), features, (1, 0))
     own_marks = own_in[:, :, width : width + 128]
     own_hits = own_marks[:, :, :experts]
     own_keep = own_marks[:, :, experts].reshape(-1, 1).astype(F32)
-    gy_own = own_keep * dot(
-        own_in[:, :, width + 128 :].reshape(batches * seq_len, width), features, (1, 0)
-    )
 
     place = jnp.arange(seq_len, dtype=jnp.int32)
     earlier = (place[None, :] < place[:, None]).astype(BF16)
     before = jnp.einsum("pq,mqe->mpe", earlier, own_hits, preferred_element_type=F32)
     totals = jnp.sum(own_hits.astype(F32), axis=1)
+
+    def to_send(own):
+        natural = dot(own, features, (1, 1), BF16).reshape(batches, seq_len, -1)
+        return jnp.swapaxes(natural, 0, 1).reshape(seq_len, -1, 128)
+
+    def placed(got):
+        got = got.reshape(seqs, batches, -1)
+        back = jnp.einsum("mjs,jmd->msd", deal, got, preferred_element_type=F32)
+        return back.astype(BF16)[:, :, None]
+
+    small_in = to_local(
+        jnp.concatenate([gain_attn[None], gain_ffn[None], w_router.T.astype(F32)], axis=0)
+    )
+    gain_a, gain_f, router = small_in[0:1], small_in[1:2], small_in[2:].astype(BF16)
+    scale_attn = lax.rsqrt(jnp.mean(x_own * x_own, axis=-1, keepdims=True) + EPS)
+    unit_attn = x_own * scale_attn
+    n1_own = (unit_attn * gain_a).astype(BF16)
+    n1_own, totals, cot_sent = lax.optimization_barrier((n1_own, totals, cot_sent))
+    own_cot = arrived(lax.all_to_all(cot_sent, DP, 0, 0, tiled=True))
+    gy_own = own_keep * dot(
+        own_cot.reshape(batches * seq_len, width), features, (1, 0)
+    )
     other_totals = swapped(totals, "zh")
     rank = before + jnp.where(t == 1, other_totals, 0.0)[:, None, :]
     own_kept = jnp.where(rank < CAP, own_hits, jnp.zeros_like(own_hits))
     flags = (own_hits + own_kept).reshape(batches * seq_len, -1)
     flags = jnp.pad(flags, ((0, 0), (0, 128 - flags.shape[1])))
-
-    def to_send(own):
-        natural = dot(own, features, (1, 1), BF16).reshape(batches, seq_len, -1)
-        return jnp.swapaxes(natural, 0, 1).reshape(seq_len, -1, 128)
-
-    def placed(got):
-        got = got.reshape(seqs, batches, -1)
-        back = jnp.einsum("mjs,jmd->msd", deal, got, preferred_element_type=F32)
-        return back.astype(BF16)[:, :, None]
-
-    small_in = to_local(
-        jnp.concatenate([gain_attn[None], gain_ffn[None], w_router.T.astype(F32)], axis=0)
-    )
-    gain_a, gain_f, router = small_in[0:1], small_in[1:2], small_in[2:].astype(BF16)
-    scale_attn = lax.rsqrt(jnp.mean(x_own * x_own, axis=-1, keepdims=True) + EPS)
-    unit_attn = x_own * scale_attn
-    n1_own = (unit_attn * gain_a).astype(BF16)
     gy_own_low = jnp.concatenate([gy_own.astype(BF16), flags], axis=1)
     n1_other, gy_own_low = lax.optimization_barrier((swapped(n1_own, "z0"), gy_own_low))
     n1 = jnp.concatenate([n1_own, n1_other], axis=0)
@@ -502,9 +555,9 @@
     n2, gy, dab, weighted, dn2_part, out_part, dlogits, small_ffn = experts_both_ways(
         n2_pair, n2_other, gy_pair, gy_other, ffn_w, router_low, experts
     )
+    dn2_sum, (dab, weighted) = core_sum(dn2_part, (dab, weighted))
+    dn2 = pair_sum(dn2_sum)
     big_down = dot(gy, weighted, (0, 0), BF16)
-    dn2_sum, dab = core_sum(dn2_part, dab)
-    dn2 = pair_sum(dn2_sum)
     big_ffn = jnp.concatenate([dot(n2, dab, (0, 0), BF16), big_down], axis=1)
     small_router = dot(dlogits, n2, (0, 0))[:experts]
     small_ffn = small_ffn / gain_f
@@ -528,25 +581,39 @@
         (dqkv, lax.all_to_all(out_halves, "z0", 0, 0, tiled=True))
     )
     branch = jnp.sum(halves_got.astype(F32), axis=0)
-    out_own = (own_keep * (h_own + branch)).astype(BF16)
-    out_got = lax.all_to_all(to_send(out_own), DP, 0, 0, tiled=True)
-    big_attn = jnp.concatenate([dot(n1, dqkv, (0, 0), BF16), dot(dattn, mixed, (0, 0), BF16)], axis=1)
+    out_sent = to_send((own_keep * (h_own + branch)).astype(BF16))
+    out_got = lax.all_to_all(out_sent, DP, 0, 0, tiled=True)
     small = jnp.concatenate([small_attn / gain_a, small_ffn, small_router], axis=0)
+    lines = in_lines(small.astype(BF16), q_cols + qkv_cols)
+    big_attn = attention_gradients(n1, dqkv, dattn, mixed, lines, side_x * side_y)
     dn1_sum, big_attn = core_sum(dn1_part, big_attn)
+    big_attn, out_got = lax.optimization_barrier((big_attn, out_got))
     dn1 = pair_sum(dn1_sum)
+    dn1, near_ffn = lax.optimization_barrier((dn1, near_ffn))
     scaled = dn1 * gain_a
     dx_own = dh + scale_attn * (
         scaled - unit_attn * jnp.mean(scaled * unit_attn, axis=-1, keepdims=True)
     )
-    big_attn, out_got = lax.optimization_barrier((big_attn, out_got))
-    near_attn, small = xy_scattered_apart(big_attn, to_natural(small))
-    dx_own, near_ffn = lax.optimization_barrier((dx_own.astype(BF16), near_ffn))
-    dx_got = lax.all_to_all(to_send(dx_own), DP, 0, 0, tiled=True)
-
-    chip, final = z_scattered(jnp.concatenate([near_attn, near_ffn], axis=1), small)
-    chip, dx_got = lax.optimization_barrier((chip, dx_got))
+    xy_got = lax.all_to_all(big_attn, ("x", "y"), 0, 0, tiled=True)
+    ffn_mine = both_cores(z_scattered(near_ffn))
+    xy_got, dx_sent, ffn_mine = lax.optimization_barrier(
+        (xy_got, to_send(dx_own.astype(BF16)), ffn_mine)
+    )
+    dx_got = lax.all_to_all(dx_sent, DP, 0, 0, tiled=True)
+    summed = jnp.sum(xy_got.astype(F32), axis=0)
+    near_attn = summed[:-16].astype(BF16)
+    small = to_natural(from_lines(summed[-16:], 2 + experts, width))
+    places = len(z_routes())
+    lines = jnp.tile(small.reshape(near_attn.shape[0] // places, -1), (places, 1))
+    attn_cols = near_attn.shape[1]
+    near_attn = jnp.concatenate([near_attn, lines.astype(BF16)], axis=1)
+    chip = z_scattered(near_attn)
+    attn_mine = both_cores(chip[:, :attn_cols])
+    final = chip[:, attn_cols:]
+    final = final + swapped(final, "c")
+    final = (final + swapped(final, "zh")).reshape(small.shape)
     out_tokens, grad_tokens = placed(out_got), placed(dx_got)
-    mine = lax.all_to_all(chip.reshape(2, rows_here, -1), "c", 0, 0, tiled=True).astype(F32)
+    mine = jnp.concatenate([attn_mine, ffn_mine], axis=2)
 
     def join(start, cols):
         part = mine[:, :, start : start + cols]

time: 572 us -> 531 us (0.928)
  waiting for transfers between devices: 204 us -> 187 us
  local copies, waits for them, and re-layouts: 70.3 us -> 58.3 us
  blocking collectives: 10.9 us -> 0 us
  matrix products: 49.7 us -> 40 us
  starting transfers between devices: 109 us -> 118 us
  other arithmetic: 49.1 us -> 42.5 us
  Pallas kernels: 54 us -> 59.8 us
    all_to_all x4 -> x5, waiting for transfers between devices: 81 us -> 27 us  [the longest x1 10.3 us: on_device(): own_cot = arrived(lax.all_to_all(cot_sent, DP, 0, 0, tiled=True))]
    ppermute x4 -> x8, waiting for transfers between devices: 12.1 us -> 31 us  [z_scattered(): total = total + lax.ppermute(piece, ('z1', 'z0', 'zh'), back).astype(F32)]
    ppermute x4, waiting for transfers between devices: 12.8 us -> 30 us  [z_gathered(): lax.ppermute(shard, ('z1', 'z0', 'zh'), pairs)]
    ppermute x17 -> x20, waiting for transfers between devices: 90.9 us -> 78.8 us  [swapped(): lax.ppermute(value, axis, [(i, i ^ bit) for i in range(lax.axis_size(axis...]
    concatenate x5 -> x3, other arithmetic: 11.2 us -> 0.05 us  [the longest x1 0.02 us: on_device(): near_attn = jnp.concatenate([near_attn, lines.astype(BF16)], axis=1)]
    all_to_all x2 -> x0, blocking collectives: 10.9 us -> none  [the longest x1 6.98 us: on_device(): chip_rows = lax.all_to_all(both_shards, 'c', 0, 0, tiled=True)]
    all_gather x2, waiting for transfers between devices: 0.02 us -> 10.3 us  [xy_gathered(): return lax.all_gather(near, ('x', 'y'), axis=0, tiled=True)]
    all_to_all x4 -> x5, starting transfers between devices: 51.9 us -> 61.8 us  [the longest x1 19.6 us: on_device(): dx_got = lax.all_to_all(dx_sent, DP, 0, 0, tiled=True)]
  transfers between devices with their start and end apart: 34 -> 42, of which waited for: 18 -> 24; matrix products, arithmetic and copies ran while one was open for 23% -> 20% of each run, Pallas kernels for 3% -> 5%
where the time goes in v4:
time: 531 us; the launch traced here: 522 us
  waiting for transfers between devices  187 us (35%)
  starting transfers between devices  118 us (22%)
  Pallas kernels  59.8 us (11%)
  local copies, waits for them, and re-layouts  58.3 us (11%)
  other arithmetic  42.5 us (8%)
  matrix products  40 us (8%)
  between operations  15.7 us (3%)
    ppermute x20, waiting for transfers between devices, swapped(): lax.ppermute(value, axis, [(i, i ^ bit) for i in range(lax.axis_size(axis...  78.8 us
    pallas_call x1, Pallas kernels, experts_both_ways(): pl.pallas_call(lambda *refs: expert_kernel(experts, *refs), grid=(2,), in...  35.8 us
    dot_general x9, matrix products, dot(): lax.dot_general(left, right, (((contract[0],), (contract[1],)), ((), ()))...  35.7 us
    ppermute x8, waiting for transfers between devices, z_scattered(): total = total + lax.ppermute(piece, ('z1', 'z0', 'zh'), back).astype(F32)  31 us
    ppermute x4, waiting for transfers between devices, z_gathered(): lax.ppermute(shard, ('z1', 'z0', 'zh'), pairs)  30 us
    unnamed x181, local copies, waits for them, and re-layouts  25.2 us
    ppermute x20, starting transfers between devices, swapped(): lax.ppermute(value, axis, [(i, i ^ bit) for i in range(lax.axis_size(axis...  20.5 us
    all_to_all x1, starting transfers between devices, on_device(): dx_got = lax.all_to_all(dx_sent, DP, 0, 0, tiled=True)  19.6 us
  transfers between devices with their start and end apart: 42, of which 24 were waited for; matrix products, arithmetic and copies ran while one was open for 20% of the time, Pallas kernels for 5%

profile of v4, /device:TPU:1, one launch (start us, length us, event | category | flops | bytes accessed | tf_op | source)
XLA Modules:
  0.0 521.7 jit_solution(9127325958086362897)
XLA Ops:
  11.4 2.0 copy.494
  13.5 14.0 %all-to-all-start = ((bf16[128,26,128]{2,1,0:T(8,128)(2,1)}), bf16[128,26,128]{2,1,0:T(8,128)(2,1)S(1)}, u32[]{:S(2)}, u32[]{:S(2)}) async-start(bf16[128,26,128]{2,1,0:T(8,128)(2,1)} %copy.494), calls=%async_computation | async-start | bytes 2097152 | tf_op jit(solution)/shard_map/all_to_all | solution.py:468
  31.3 3.9 collective-permute-start.4
  35.8 2.4 collective-permute-start.2
  38.2 3.5 collective-permute-start.1
  42.5 20.3 %collective-permute-done.4 = bf16[24,4864]{1,0:T(8,128)(2,1)} collective-permute-done((bf16[24,4864]{1,0:T(8,128)(2,1)}, bf16[24,4864]{1,0:T(8,128)(2,1)}, u32[]{:S(2)}, u32[]{:S(2)}) %collective-permute-start.4) | collective-permute-done | bytes 233504 | tf_op jit(solution)/shard_map/ppermute | solution.py:78
  62.8 9.7 %collective-permute-done.3 = bf16[24,4864]{1,0:T(8,128)(2,1)} collective-permute-done((bf16[24,4864]{1,0:T(8,128)(2,1)}, bf16[24,4864]{1,0:T(8,128)(2,1)}, u32[]{:S(2)}, u32[]{:S(2)}) %collective-permute-start.3) | collective-permute-done | bytes 233504 | tf_op jit(solution)/shard_map/ppermute | solution.py:78
  79.0 2.1 multiply_reduce_fusion.3
  83.7 13.4 %all-to-all-start.1 = ((bf16[128,24,128]{2,1,0:T(8,128)(2,1)}), bf16[128,24,128]{2,1,0:T(8,128)(2,1)S(1)}, u32[]{:S(2)}, u32[]{:S(2)}) async-start(bf16[128,24,128]{2,1,0:T(8,128)(2,1)} %copy.500), calls=%async_computation.1 | async-start | bytes 1572864 | tf_op jit(solution)/shard_map/all_to_all | solution.py:515
  99.7 10.8 %collective-permute-done.6 = f32[2,8]{1,0:T(2,128)S(1)} collective-permute-done((f32[2,8]{1,0:T(2,128)S(1)}, f32[2,8]{1,0:T(2,128)S(1)}, u32[]{:S(2)}, u32[]{:S(2)}) %collective-permute-start.6) | collective-permute-done | bytes 96 | tf_op jit(solution)/shard_map/ppermute | solution.py:32
  110.8 10.3 %all-to-all-done.1 = bf16[128,24,128]{2,1,0:T(8,128)(2,1)S(1)} async-done(((bf16[128,24,128]{2,1,0:T(8,128)(2,1)}), bf16[128,24,128]{2,1,0:T(8,128)(2,1)S(1)}, u32[]{:S(2)}, u32[]{:S(2)}) %all-to-all-start.1) | async-done | bytes 786464 | tf_op jit(solution)/shard_map/all_to_all | solution.py:515
  122.0 3.3 fusion.90
  125.3 3.0 collective-permute-done.5
  132.6 4.7 all-to-all-start.2
  140.0 5.1 fusion.17.refs_2_
  148.1 10.0 %all-to-all-done.2 = bf16[2,256,1664]{2,1,0:T(8,128)(2,1)} async-done(((bf16[2,256,1664]{2,1,0:T(8,128)(2,1)}), bf16[2,256,1664]{2,1,0:T(8,128)(2,1)}, u32[]{:S(2)}, u32[]{:S(2)}) %all-to-all-start.2) | async-done | bytes 1703968 | tf_op jit(solution)/shard_map/all_to_all | solution.py:528
  158.1 3.1 convolution_convert_fusion.2
  162.3 3.0 collective-permute-done.8
  165.8 1.6 copy-done.17
  168.2 18.2 %collective-permute-done.9 = bf16[256,1536]{1,0:T(8,128)(2,1)} collective-permute-done((bf16[256,1536]{1,0:T(8,128)(2,1)S(1)}, bf16[256,1536]{1,0:T(8,128)(2,1)}, u32[]{:S(2)}, u32[]{:S(2)}) %collective-permute-start.9) | collective-permute-done | bytes 786464 | tf_op jit(solution)/shard_map/ppermute | solution.py:32
  186.4 2.6 multiply_reduce_fusion.2
  189.4 3.9 reverse_select_fusion
  194.5 12.8 %collective-permute-done.10 = bf16[256,1536]{1,0:T(8,128)(2,1)} collective-permute-done((bf16[256,1536]{1,0:T(8,128)(2,1)S(1)}, bf16[256,1536]{1,0:T(8,128)(2,1)}, u32[]{:S(2)}, u32[]{:S(2)}) %collective-permute-start.10) | collective-permute-done | bytes 786464 | tf_op jit(solution)/shard_map/ppermute | solution.py:32
  207.3 2.4 pad_maximum_fusion.2.refs_0_
  209.7 2.2 collective-permute-start.11
  215.3 10.3 %all-gather.5.cloned.1.call-done.refs_4_ = bf16[1536,3840]{1,0:T(8,128)(2,1)} async-done(((bf16[96,3840]{1,0:T(8,128)(2,1)}), bf16[1536,3840]{1,0:T(8,128)(2,1)}) %all-gather.5.cloned.1.call-update) | async-done | bytes 11796496 | tf_op jit(solution)/shard_map/all_gather | solution.py:93
  225.7 35.8 %experts.1 = (bf16[1024,1536]{1,0:T(8,128)(2,1)}, bf16[1024,1536]{1,0:T(8,128)(2,1)}, bf16[1024,2560]{1,0:T(8,128)(2,1)}, bf16[1024,1280]{1,0:T(8,128)(2,1)}, bf...) custom-call(bf16[512,1536]{1,0:T(8,128)(2,1)} %pad_maximum_fusion.2.refs_0, ...), custom_call_target="tpu_custom_call" | custom-call | flops 24159191040 | bytes 44826624 | tf_op jit(solution)/shard_map/experts/pallas_call | solution.py:211
  261.5 1.7 slice.507
  263.9 3.0 collective-permute-done.13
  267.4 1.6 copy-done.16
  270.7 11.5 %convolution_convert_fusion = bf16[1536,2560]{1,0:T(8,128)(2,1)S(1)} fusion(bf16[1024,1536]{1,0:T(8,128)(2,1)S(1)} %copy-done.20, bf16[1024,2560]{1,0:T(8,128)(2,1)} %get-tuple-element.73), kind=kOutput, calls=%fused_computation.1 | convolution fusion | flops 8056995840 | bytes 16252928 | tf_op jit(solution)/shard_map/dot_general | solution.py:25
  282.2 4.6 convolution_convert_fusion.1
  286.8 5.1 pad_maximum_fusion
  291.9 3.0 convert_add_fusion.5
  295.0 1.9 multiply_reduce_fusion.1
  297.3 1.6 fusion.82
  305.5 15.3 %collective-permute-done.15 = bf16[256,1536]{1,0:T(8,128)(2,1)S(1)} collective-permute-done((bf16[256,1536]{1,0:T(8,128)(2,1)S(1)}, bf16[256,1536]{1,0:T(8,128)(2,1)S(1)}, u32[]{:S(2)}, u32[]{:S(2)}) %collective-permute-start.15) | collective-permute-done | bytes 786464 | tf_op jit(solution)/shard_map/ppermute | solution.py:32
  323.0 5.0 all-to-all-start.3
  330.9 18.4 %attention_backward.1 = (bf16[1024,1536]{1,0:T(8,128)(2,1)S(1)}, bf16[1024,640]{1,0:T(8,128)(2,1)S(1)}, bf16[1024,1536]{1,0:T(8,128)(2,1)}, f32[1,1536]{1,0:T(1,128)S(1)}) custom-call(bf16[512,1536]{1,0:T(8,128)(2,1)S(1)} %copy-done.9, bf16[512,1536]{1,0:T(8,128)(2,1)} %collective-permute-done.17.refs_1_, bf16[1024,640]{1,0:T(8,128)(2,1)S(1)} %copy-done.7, ...), custom_call_target="tpu_custom_call" | custom-call | flops 19327352832 | bytes 21495808 | tf_op jit(solution)/shard_map/attention_backward/pallas_call | solution.py:296
  349.3 3.8 slice.514
  353.4 1.9 convert_reduce_fusion.1
  355.3 3.1 fusion.9
  361.1 10.2 %all-to-all-start.4 = ((bf16[128,24,128]{2,1,0:T(8,128)(2,1)}), bf16[128,24,128]{2,1,0:T(8,128)(2,1)S(1)}, u32[]{:S(2)}, u32[]{:S(2)}) async-start(bf16[128,24,128]{2,1,0:T(8,128)(2,1)} %copy.516), calls=%async_computation.4 | async-start | bytes 1572864 | tf_op jit(solution)/shard_map/all_to_all | solution.py:585
  371.4 1.9 copy-done.3
  373.3 2.4 copy-done.5
  375.6 5.6 %attention_gradients.1 = bf16[16,112,1024]{2,1,0:T(8,128)(2,1)S(1)} custom-call(bf16[1024,1536]{1,0:T(8,128)(2,1)S(1)} %copy-done.3, bf16[1024,1536]{1,0:T(8,128)(2,1)S(1)} %copy-done.5, bf16[1024,640]{1,0:T(8,128)(2,1)S(1)} %get-tuple-element.86.dqkv_ref, bf16[1024,384]{1,0:T(8,128)(2,1)S(1)} %copy.514.mixed_ref, bf16[16,1024]{1,0:T(8,128)(2,1)S(1)} %fusion.53.lines_ref), custom_call_target="tpu_custom_call" | custom-call | flops 3221225472 | bytes 12058624 | tf_op jit(solution)/shard_map/attention_gradients/pallas_call | solution.py:340
  381.3 3.1 convert_add_fusion
  387.6 7.7 %all-to-all-done.4 = bf16[128,24,128]{2,1,0:T(8,128)(2,1)S(1)} async-done(((bf16[128,24,128]{2,1,0:T(8,128)(2,1)}), bf16[128,24,128]{2,1,0:T(8,128)(2,1)S(1)}, u32[]{:S(2)}, u32[]{:S(2)}) %all-to-all-start.4) | async-done | bytes 786464 | tf_op jit(solution)/shard_map/all_to_all | solution.py:585
  395.8 4.5 all-to-all-start.5
  401.6 4.9 collective-permute-done.19
  406.6 3.1 convert_add_fusion.4
  411.6 4.9 collective-permute-start.23
  418.3 1.7 multiply_reduce_fusion
  420.6 13.3 %collective-permute-done.22 = bf16[24,3840]{1,0:T(8,128)(2,1)S(1)} collective-permute-done((bf16[24,3840]{1,0:T(8,128)(2,1)S(1)}, bf16[24,3840]{1,0:T(8,128)(2,1)S(1)}, u32[]{:S(2)}, u32[]{:S(2)}) %collective-permute-start.22) | collective-permute-done | bytes 184352 | tf_op jit(solution)/shard_map/ppermute | solution.py:88
  434.7 2.4 fusion.10
  437.6 8.9 %all-to-all-done.5 = bf16[16,112,1024]{2,1,0:T(8,128)(2,1)} async-done(((bf16[16,112,1024]{2,1,0:T(8,128)(2,1)}), bf16[16,112,1024]{2,1,0:T(8,128)(2,1)}, u32[]{:S(2)}, u32[]{:S(2)}) %all-to-all-start.5) | async-done | bytes 3670048 | tf_op jit(solution)/shard_map/all_to_all | solution.py:597
  446.5 2.7 convert_reduce_fusion
  450.5 19.6 %all-to-all-start.6 = ((bf16[128,24,128]{2,1,0:T(8,128)(2,1)}), bf16[128,24,128]{2,1,0:T(8,128)(2,1)S(1)}, u32[]{:S(2)}, u32[]{:S(2)}) async-start(bf16[128,24,128]{2,1,0:T(8,128)(2,1)} %copy.520), calls=%async_computation.7 | async-start | bytes 1572864 | tf_op jit(solution)/shard_map/all_to_all | solution.py:602
  471.8 4.7 collective-permute-start.26
  476.5 2.3 collective-permute-start.28
  479.2 11.6 %collective-permute-done.26 = bf16[24,1664]{1,0:T(8,128)(2,1)S(1)} collective-permute-done((bf16[24,1664]{1,0:T(8,128)(2,1)S(1)}, bf16[24,1664]{1,0:T(8,128)(2,1)S(1)}, u32[]{:S(2)}, u32[]{:S(2)}) %collective-permute-start.26) | collective-permute-done | bytes 79904 | tf_op jit(solution)/shard_map/ppermute | solution.py:88
  490.7 5.6 %collective-permute-done.27 = bf16[24,1664]{1,0:T(8,128)(2,1)S(1)} collective-permute-done((bf16[24,1664]{1,0:T(8,128)(2,1)S(1)}, bf16[24,1664]{1,0:T(8,128)(2,1)S(1)}, u32[]{:S(2)}, u32[]{:S(2)}) %collective-permute-start.27) | collective-permute-done | bytes 79904 | tf_op jit(solution)/shard_map/ppermute | solution.py:88
  502.6 3.2 collective-permute-start.30
  508.4 3.4 collective-permute-done.30
  (373 shorter events, 82.2 us)
Async XLA Ops:
  7.2 34.5 %copy-start = (bf16[2,128,1,1536]{3,1,2,0:T(8,128)(2,1)S(1)}, bf16[2,128,1,1536]{3,1,2,0:T(8,128)(2,1)}, u32[]{:S(2)}) copy-start(bf16[2,128,1,1536]{3,1,2,0:T(8,128)(2,1)} %param.19) | copy-start | bytes 2359300
  11.0 30.7 %copy-start.44 = (s32[2,1,128]{2,1,0:T(1,128)}, s32[2,1,128]{2,1,0:T(1,128)S(1)}, u32[]{:S(2)}) copy-start(s32[2,1,128]{2,1,0:T(1,128)S(1)} %constant_dynamic-slice_fusion.1) | copy-start | bytes 3076
  11.4 16.1 %copy-start.37 = (bf16[8,256,12]{1,0,2:T(8,128)(2,1)S(1)}, bf16[8,256,12]{1,0,2:T(8,128)(2,1)}, u32[]{:S(2)}) copy-start(bf16[8,256,12]{1,0,2:T(8,128)(2,1)} %param.32) | copy-start | bytes 147460
  13.4 14.1 %copy-start.31 = (bf16[8,12,256]{2,0,1:T(8,128)(2,1)S(1)}, bf16[8,12,256]{2,0,1:T(8,128)(2,1)}, u32[]{:S(2)}) copy-start(bf16[8,12,256]{2,0,1:T(8,128)(2,1)} %param.30) | copy-start | bytes 147460
  13.4 14.2 %copy-start.32 = (bf16[8,12,256]{2,0,1:T(8,128)(2,1)S(1)}, bf16[8,12,256]{2,0,1:T(8,128)(2,1)}, u32[]{:S(2)}) copy-start(bf16[8,12,256]{2,0,1:T(8,128)(2,1)} %param.31) | copy-start | bytes 147460
  13.4 14.4 %copy-start.38 = (bf16[12,768]{1,0:T(8,128)(2,1)S(1)}, bf16[12,768]{1,0:T(8,128)(2,1)}, u32[]{:S(2)}) copy-start(bf16[12,768]{1,0:T(8,128)(2,1)} %param.25) | copy-start | bytes 55300
  13.4 14.4 %copy-start.50 = (bf16[12,256]{1,0:T(8,128)(2,1)S(1)}, bf16[12,256]{1,0:T(8,128)(2,1)}, u32[]{:S(2)}) copy-start(bf16[12,256]{1,0:T(8,128)(2,1)} %param.26) | copy-start | bytes 18436
  13.4 14.4 %copy-start.51 = (bf16[12,256]{1,0:T(8,128)(2,1)S(1)}, bf16[12,256]{1,0:T(8,128)(2,1)}, u32[]{:S(2)}) copy-start(bf16[12,256]{1,0:T(8,128)(2,1)} %param.27) | copy-start | bytes 18436
  13.4 14.4 %copy-start.39 = (bf16[768,12]{0,1:T(8,128)(2,1)S(1)}, bf16[768,12]{0,1:T(8,128)(2,1)}, u32[]{:S(2)}) copy-start(bf16[768,12]{0,1:T(8,128)(2,1)} %param.28) | copy-start | bytes 55300
  13.4 14.6 %copy-start.41 = (bf16[12,512]{1,0:T(8,128)(2,1)S(1)}, bf16[12,512]{1,0:T(8,128)(2,1)}, u32[]{:S(2)}) copy-start(bf16[12,512]{1,0:T(8,128)(2,1)} %param.33) | copy-start | bytes 36868
  13.4 14.8 %copy-start.42 = (bf16[12,512]{1,0:T(8,128)(2,1)S(1)}, bf16[12,512]{1,0:T(8,128)(2,1)}, u32[]{:S(2)}) copy-start(bf16[12,512]{1,0:T(8,128)(2,1)} %param.34) | copy-start | bytes 36868
  13.5 14.9 %copy-start.43 = (bf16[512,12]{0,1:T(8,128)(2,1)S(1)}, bf16[512,12]{0,1:T(8,128)(2,1)}, u32[]{:S(2)}) copy-start(bf16[512,12]{0,1:T(8,128)(2,1)} %param.35) | copy-start | bytes 36868
  13.5 60.4 %all-to-all-start = ((bf16[128,26,128]{2,1,0:T(8,128)(2,1)}), bf16[128,26,128]{2,1,0:T(8,128)(2,1)S(1)}, u32[]{:S(2)}, u32[]{:S(2)}) async-start(bf16[128,26,128]{2,1,0:T(8,128)(2,1)} %copy.494), calls=%async_computation | async-start | bytes 2097152 | tf_op jit(solution)/shard_map/all_to_all | solution.py:468
  27.5 112.5 %all-gather.3.cloned.1.call-start = ((), (), s32[]{:S(2)}) async-start(), calls=%async_computation.8 | async-start | bytes 3342336 | tf_op jit(solution)/shard_map/all_gather | solution.py:93
  28.4 2.0 collective-permute-start
  31.3 31.5 %collective-permute-start.4 = (bf16[24,4864]{1,0:T(8,128)(2,1)}, bf16[24,4864]{1,0:T(8,128)(2,1)}, u32[]{:S(2)}, u32[]{:S(2)}) collective-permute-start(bf16[24,4864]{1,0:T(8,128)(2,1)} %maximum_select_fusion.1), channel_id=1, source_target_pairs={{0,33},{1,49},{16,32},{17,48},{32,1},{33,17},{48,0},{49,16},{2,35}... | collective-permute-start | bytes 700424 | tf_op jit(solution)/shard_map/ppermute | solution.py:78
  35.1 37.3 %collective-permute-start.3 = (bf16[24,4864]{1,0:T(8,128)(2,1)}, bf16[24,4864]{1,0:T(8,128)(2,1)}, u32[]{:S(2)}, u32[]{:S(2)}) collective-permute-start(bf16[24,4864]{1,0:T(8,128)(2,1)} %maximum_select_fusion.1), channel_id=1, source_target_pairs={{0,32},{1,48},{16,33},{17,49},{32,0},{33,16},{48,1},{49,17},{2,34}... | collective-permute-start | bytes 700424 | tf_op jit(solution)/shard_map/ppermute | solution.py:78
  35.8 36.7 %collective-permute-start.2 = (bf16[24,4864]{1,0:T(8,128)(2,1)}, bf16[24,4864]{1,0:T(8,128)(2,1)}, u32[]{:S(2)}, u32[]{:S(2)}) collective-permute-start(bf16[24,4864]{1,0:T(8,128)(2,1)} %maximum_select_fusion.1), channel_id=1, source_target_pairs={{0,1},{1,17},{16,0},{17,16},{32,33},{33,49},{48,32},{49,48},{2,3},... | collective-permute-start | bytes 700424 | tf_op jit(solution)/shard_map/ppermute | solution.py:78
  38.2 34.3 %collective-permute-start.1 = (bf16[24,4864]{1,0:T(8,128)(2,1)}, bf16[24,4864]{1,0:T(8,128)(2,1)}, u32[]{:S(2)}, u32[]{:S(2)}) collective-permute-start(bf16[24,4864]{1,0:T(8,128)(2,1)} %maximum_select_fusion.1), channel_id=1, source_target_pairs={{0,0},{1,16},{16,1},{17,17},{32,32},{33,48},{48,33},{49,49},{2,2},... | collective-permute-start | bytes 700424 | tf_op jit(solution)/shard_map/ppermute | solution.py:78
  74.6 151.1 %all-gather.5.cloned.1.call-start = ((), (), s32[]{:S(2)}) async-start(), calls=%async_computation.9 | async-start | bytes 12533760 | tf_op jit(solution)/shard_map/all_gather | solution.py:93
  83.7 37.4 %all-to-all-start.1 = ((bf16[128,24,128]{2,1,0:T(8,128)(2,1)}), bf16[128,24,128]{2,1,0:T(8,128)(2,1)S(1)}, u32[]{:S(2)}, u32[]{:S(2)}) async-start(bf16[128,24,128]{2,1,0:T(8,128)(2,1)} %copy.500), calls=%async_computation.1 | async-start | bytes 1572864 | tf_op jit(solution)/shard_map/all_to_all | solution.py:515
  97.2 13.4 %collective-permute-start.6 = (f32[2,8]{1,0:T(2,128)S(1)}, f32[2,8]{1,0:T(2,128)S(1)}, u32[]{:S(2)}, u32[]{:S(2)}) collective-permute-start(f32[2,8]{1,0:T(2,128)S(1)} %convert_reduce_fusion.2), channel_id=1, source_target_pairs={{0,1},{1,0},{2,3},{3,2},{4,5},{5,4},{6,7},{7,6},{8,9},{9,8},{10,11... | collective-permute-start | bytes 200 | tf_op jit(solution)/shard_map/ppermute | solution.py:32
  98.3 30.0 %collective-permute-start.5 = (bf16[256,1536]{1,0:T(8,128)(2,1)S(1)}, bf16[256,1536]{1,0:T(8,128)(2,1)S(1)}, u32[]{:S(2)}, u32[]{:S(2)}) collective-permute-start(bf16[256,1536]{1,0:T(8,128)(2,1)S(1)} %multiply_convert_fusion.2), channel_id=1, source_target_pairs={{0,16},{16,0},{1,17},{17,1},{2,18},{18,2},{3,19},{19,3},{4,20},{20... | collective-permute-start | bytes 2359304 | tf_op jit(solution)/shard_map/ppermute | solution.py:32
  129.5 9.1 %collective-permute-start.7 = (bf16[512,1536]{1,0:T(8,128)(2,1)}, bf16[512,1536]{1,0:T(8,128)(2,1)S(1)}, u32[]{:S(2)}, u32[]{:S(2)}) collective-permute-start(bf16[512,1536]{1,0:T(8,128)(2,1)} %pad_maximum_fusion.1), channel_id=1, source_target_pairs={{0,2},{2,0},{1,3},{3,1},{4,6},{6,4},{5,7},{7,5},{8,10},{10,8},{9,1... | collective-permute-start | bytes 4718600 | tf_op jit(solution)/shard_map/ppermute | solution.py:32
  132.6 25.5 %all-to-all-start.2 = ((bf16[2,256,1664]{2,1,0:T(8,128)(2,1)}), bf16[2,256,1664]{2,1,0:T(8,128)(2,1)}, u32[]{:S(2)}, u32[]{:S(2)}) async-start(bf16[2,256,1664]{2,1,0:T(8,128)(2,1)} %broadcast_in_dim.30), calls=%async_computation.2 | async-start | bytes 3407872 | tf_op jit(solution)/shard_map/all_to_all | solution.py:528
  137.2 272.4 %reduce-scatter.2.cloned.1.call-start = ((), (), s32[]{:S(2)}) async-start(), calls=%async_computation.10 | async-start | bytes 12533760 | tf_op jit(solution)/shard_map/reduce_scatter | solution.py:97
  161.4 3.9 collective-permute-start.8
  167.5 18.9 %collective-permute-start.9 = (bf16[256,1536]{1,0:T(8,128)(2,1)S(1)}, bf16[256,1536]{1,0:T(8,128)(2,1)}, u32[]{:S(2)}, u32[]{:S(2)}) collective-permute-start(bf16[256,1536]{1,0:T(8,128)(2,1)S(1)} %slice.708), channel_id=1, source_target_pairs={{0,16},{16,0},{1,17},{17,1},{2,18},{18,2},{3,19},{19,3},{4,20},{20... | collective-permute-start | bytes 2359304 | tf_op jit(solution)/shard_map/ppermute | solution.py:32
  189.0 107.9 %copy-start.10 = (f32[256,1536]{1,0:T(8,128)}, f32[256,1536]{1,0:T(8,128)S(1)}, u32[]{:S(2)}) copy-start(f32[256,1536]{1,0:T(8,128)S(1)} %get-tuple-element.213) | copy-start | bytes 4718596
  189.2 18.0 %collective-permute-start.10 = (bf16[256,1536]{1,0:T(8,128)(2,1)S(1)}, bf16[256,1536]{1,0:T(8,128)(2,1)}, u32[]{:S(2)}, u32[]{:S(2)}) collective-permute-start(bf16[256,1536]{1,0:T(8,128)(2,1)S(1)} %multiply_convert_fusion.1), channel_id=1, source_target_pairs={{0,16},{16,0},{1,17},{17,1},{2,18},{18,2},{3,19},{19,3},{4,20},{20... | collective-permute-start | bytes 2359304 | tf_op jit(solution)/shard_map/ppermute | solution.py:32
  193.2 20.8 %collective-permute-start.12 = (bf16[512,1664]{1,0:T(8,128)(2,1)}, bf16[512,1664]{1,0:T(8,128)(2,1)}, u32[]{:S(2)}, u32[]{:S(2)}) collective-permute-start(bf16[512,1664]{1,0:T(8,128)(2,1)} %bitcast.80.refs_2_), channel_id=1, source_target_pairs={{0,2},{2,0},{1,3},{3,1},{4,6},{6,4},{5,7},{7,5},{8,10},{10,8},{9,1... | collective-permute-start | bytes 5111816 | tf_op jit(solution)/shard_map/ppermute | solution.py:32
  209.7 5.6 %collective-permute-start.11 = (bf16[512,1536]{1,0:T(8,128)(2,1)}, bf16[512,1536]{1,0:T(8,128)(2,1)}, u32[]{:S(2)}, u32[]{:S(2)}) collective-permute-start(bf16[512,1536]{1,0:T(8,128)(2,1)} %pad_maximum_fusion.2.refs_0_), channel_id=1, source_target_pairs={{0,2},{2,0},{1,3},{3,1},{4,6},{6,4},{5,7},{7,5},{8,10},{10,8},{9,1... | collective-permute-start | bytes 4718600 | tf_op jit(solution)/shard_map/ppermute | solution.py:32
  263.1 3.8 collective-permute-start.13
  269.1 22.8 %collective-permute-start.14 = (bf16[256,1536]{1,0:T(8,128)(2,1)S(1)}, bf16[256,1536]{1,0:T(8,128)(2,1)}, u32[]{:S(2)}, u32[]{:S(2)}) collective-permute-start(bf16[256,1536]{1,0:T(8,128)(2,1)S(1)} %slice.707), channel_id=1, source_target_pairs={{0,16},{16,0},{1,17},{17,1},{2,18},{18,2},{3,19},{19,3},{4,20},{20... | collective-permute-start | bytes 2359304 | tf_op jit(solution)/shard_map/ppermute | solution.py:32
  270.7 11.5 %copy-start.56 = (bf16[1024,1536]{1,0:T(8,128)(2,1)S(1)}, bf16[1024,1536]{1,0:T(8,128)(2,1)}, u32[]{:S(2)}) copy-start(bf16[1024,1536]{1,0:T(8,128)(2,1)} %get-tuple-element.74) | copy-start | bytes 9437188
  270.7 11.5 %copy-start.57 = (bf16[1024,1280]{1,0:T(8,128)(2,1)S(1)}, bf16[1024,1280]{1,0:T(8,128)(2,1)}, u32[]{:S(2)}) copy-start(bf16[1024,1280]{1,0:T(8,128)(2,1)} %get-tuple-element.75) | copy-start | bytes 7864324
  299.9 3.8 collective-permute-start.16
  302.2 18.6 %collective-permute-start.15 = (bf16[256,1536]{1,0:T(8,128)(2,1)S(1)}, bf16[256,1536]{1,0:T(8,128)(2,1)S(1)}, u32[]{:S(2)}, u32[]{:S(2)}) collective-permute-start(bf16[256,1536]{1,0:T(8,128)(2,1)S(1)} %get-tuple-element.78), channel_id=1, source_target_pairs={{0,16},{16,0},{1,17},{17,1},{2,18},{18,2},{3,19},{19,3},{4,20},{20... | collective-permute-start | bytes 2359304 | tf_op jit(solution)/shard_map/ppermute | solution.py:32
  305.5 17.0 %copy-start.29 = (f32[1,4,4,2,2,24]{5,4,3,2,1,0:T(2,128)S(1)}, f32[1,4,4,2,2,24]{5,4,3,2,1,0:T(2,128)}, u32[]{:S(2)}) copy-start(f32[1,4,4,2,2,24]{5,4,3,2,1,0:T(2,128)} %copy-done.28) | copy-start | bytes 18436
  305.5 17.5 %copy-start.54 = (f32[1,1536]{1,0:T(1,128)S(1)}, f32[1,1536]{1,0:T(1,128)}, u32[]{:S(2)}) copy-start(f32[1,1536]{1,0:T(1,128)} %get-tuple-element.88) | copy-start | bytes 18436
  320.9 7.2 %collective-permute-start.17 = (bf16[512,1536]{1,0:T(8,128)(2,1)S(1)}, bf16[512,1536]{1,0:T(8,128)(2,1)}, u32[]{:S(2)}, u32[]{:S(2)}) collective-permute-start(bf16[512,1536]{1,0:T(8,128)(2,1)S(1)} %constant_dynamic-update-slice_fusion.65.refs_0_), channel_id=1, source_target_pairs={{0,2},{2,0},{1,3},{3,1},{4,6},{6,4},{5,7},{7,5},{8,10},{10,8},{9,1... | collective-permute-start | bytes 4718600 | tf_op jit(solution)/shard_map/ppermute | solution.py:32
  323.0 30.2 %all-to-all-start.3 = ((bf16[2,256,1536]{2,1,0:T(8,128)(2,1)}), bf16[2,256,1536]{2,1,0:T(8,128)(2,1)}, u32[]{:S(2)}, u32[]{:S(2)}) async-start(bf16[2,256,1536]{2,1,0:T(8,128)(2,1)} %reverse_select_fusion.1), calls=%async_computation.3 | async-start | bytes 3145728 | tf_op jit(solution)/shard_map/all_to_all | solution.py:581
  353.1 28.2 %collective-permute-start.18 = (bf16[512,1536]{1,0:T(8,128)(2,1)}, bf16[512,1536]{1,0:T(8,128)(2,1)}, u32[]{:S(2)}, u32[]{:S(2)}) collective-permute-start(bf16[512,1536]{1,0:T(8,128)(2,1)} %slice.514), channel_id=1, source_target_pairs={{0,2},{2,0},{1,3},{3,1},{4,6},{6,4},{5,7},{7,5},{8,10},{10,8},{9,1... | collective-permute-start | bytes 4718600 | tf_op jit(solution)/shard_map/ppermute | solution.py:32
  361.1 34.1 %all-to-all-start.4 = ((bf16[128,24,128]{2,1,0:T(8,128)(2,1)}), bf16[128,24,128]{2,1,0:T(8,128)(2,1)S(1)}, u32[]{:S(2)}, u32[]{:S(2)}) async-start(bf16[128,24,128]{2,1,0:T(8,128)(2,1)} %copy.516), calls=%async_computation.4 | async-start | bytes 1572864 | tf_op jit(solution)/shard_map/all_to_all | solution.py:585
  386.0 20.5 %collective-permute-start.19 = (bf16[256,1536]{1,0:T(8,128)(2,1)S(1)}, bf16[256,1536]{1,0:T(8,128)(2,1)}, u32[]{:S(2)}, u32[]{:S(2)}) collective-permute-start(bf16[256,1536]{1,0:T(8,128)(2,1)S(1)} %slice.706), channel_id=1, source_target_pairs={{0,16},{16,0},{1,17},{17,1},{2,18},{18,2},{3,19},{19,3},{4,20},{20... | collective-permute-start | bytes 2359304 | tf_op jit(solution)/shard_map/ppermute | solution.py:32
  395.8 50.7 %all-to-all-start.5 = ((bf16[16,112,1024]{2,1,0:T(8,128)(2,1)}), bf16[16,112,1024]{2,1,0:T(8,128)(2,1)}, u32[]{:S(2)}, u32[]{:S(2)}) async-start(bf16[16,112,1024]{2,1,0:T(8,128)(2,1)} %copy-done.2), calls=%async_computation.5 | async-start | bytes 7340032 | tf_op jit(solution)/shard_map/all_to_all | solution.py:597
  401.6 16.7 %copy-start.36 = (f32[1536]{0:T(1024)S(1)}, f32[1536]{0:T(1024)}, u32[]{:S(2)}) copy-start(f32[1536]{0:T(1024)} %copy-done.35) | copy-start | bytes 18436
  401.6 16.7 %copy-start.47 = (f32[256]{0:T(256)S(1)}, f32[256]{0:T(256)}, u32[]{:S(2)}) copy-start(f32[256]{0:T(256)} %copy-done.46) | copy-start | bytes 3076
  406.6 11.8 %copy-start.13 = (f32[256,1536]{1,0:T(8,128)S(1)}, f32[256,1536]{1,0:T(8,128)}, u32[]{:S(2)}) copy-start(f32[256,1536]{1,0:T(8,128)} %copy-done.12) | copy-start | bytes 4718596
  410.9 9.2 %collective-permute-start.20 = (bf16[24,3840]{1,0:T(8,128)(2,1)S(1)}, bf16[24,3840]{1,0:T(8,128)(2,1)S(1)}, u32[]{:S(2)}, u32[]{:S(2)}) collective-permute-start(bf16[24,3840]{1,0:T(8,128)(2,1)S(1)} %get-tuple-element.216), channel_id=1, source_target_pairs={{0,0},{16,1},{1,16},{17,17},{32,32},{48,33},{33,48},{49,49},{2,2},... | collective-permute-start | bytes 552968 | tf_op jit(solution)/shard_map/ppermute | solution.py:88
  411.6 9.0 %collective-permute-start.23 = (bf16[24,3840]{1,0:T(8,128)(2,1)S(1)}, bf16[24,3840]{1,0:T(8,128)(2,1)S(1)}, u32[]{:S(2)}, u32[]{:S(2)}) collective-permute-start(bf16[24,3840]{1,0:T(8,128)(2,1)S(1)} %get-tuple-element.217), channel_id=1, source_target_pairs={{33,0},{49,1},{32,16},{48,17},{1,32},{17,33},{0,48},{16,49},{35,2}... | collective-permute-start | bytes 552968 | tf_op jit(solution)/shard_map/ppermute | solution.py:88
  416.5 17.4 %collective-permute-start.22 = (bf16[24,3840]{1,0:T(8,128)(2,1)S(1)}, bf16[24,3840]{1,0:T(8,128)(2,1)S(1)}, u32[]{:S(2)}, u32[]{:S(2)}) collective-permute-start(bf16[24,3840]{1,0:T(8,128)(2,1)S(1)} %get-tuple-element.218), channel_id=1, source_target_pairs={{32,0},{48,1},{33,16},{49,17},{0,32},{16,33},{1,48},{17,49},{34,2}... | collective-permute-start | bytes 552968 | tf_op jit(solution)/shard_map/ppermute | solution.py:88
  416.9 17.8 %copy-start.18 = (f32[256,1536]{1,0:T(8,128)S(1)}, f32[256,1536]{1,0:T(8,128)}, u32[]{:S(2)}) copy-start(f32[256,1536]{1,0:T(8,128)} %convert_add_fusion.4) | copy-start | bytes 4718596
  416.9 17.8 %copy-start.25 = (f32[256,1536]{1,0:T(8,128)S(1)}, f32[256,1536]{1,0:T(8,128)}, u32[]{:S(2)}) copy-start(f32[256,1536]{1,0:T(8,128)} %get-tuple-element.211) | copy-start | bytes 4718596
  416.9 17.0 %collective-permute-start.21 = (bf16[24,3840]{1,0:T(8,128)(2,1)S(1)}, bf16[24,3840]{1,0:T(8,128)(2,1)S(1)}, u32[]{:S(2)}, u32[]{:S(2)}) collective-permute-start(bf16[24,3840]{1,0:T(8,128)(2,1)S(1)} %get-tuple-element.219), channel_id=1, source_target_pairs={{1,0},{17,1},{0,16},{16,17},{33,32},{49,33},{32,48},{48,49},{3,2},... | collective-permute-start | bytes 552968 | tf_op jit(solution)/shard_map/ppermute | solution.py:88
  434.1 3.4 collective-permute-start.24
  450.5 62.6 %all-to-all-start.6 = ((bf16[128,24,128]{2,1,0:T(8,128)(2,1)}), bf16[128,24,128]{2,1,0:T(8,128)(2,1)S(1)}, u32[]{:S(2)}, u32[]{:S(2)}) async-start(bf16[128,24,128]{2,1,0:T(8,128)(2,1)} %copy.520), calls=%async_computation.7 | async-start | bytes 1572864 | tf_op jit(solution)/shard_map/all_to_all | solution.py:602
  471.2 8.0 %collective-permute-start.25 = (bf16[24,1664]{1,0:T(8,128)(2,1)S(1)}, bf16[24,1664]{1,0:T(8,128)(2,1)S(1)}, u32[]{:S(2)}, u32[]{:S(2)}) collective-permute-start(bf16[24,1664]{1,0:T(8,128)(2,1)S(1)} %get-tuple-element.228), channel_id=1, source_target_pairs={{0,0},{16,1},{1,16},{17,17},{32,32},{48,33},{33,48},{49,49},{2,2},... | collective-permute-start | bytes 239624 | tf_op jit(solution)/shard_map/ppermute | solution.py:88
  471.8 18.9 %collective-permute-start.26 = (bf16[24,1664]{1,0:T(8,128)(2,1)S(1)}, bf16[24,1664]{1,0:T(8,128)(2,1)S(1)}, u32[]{:S(2)}, u32[]{:S(2)}) collective-permute-start(bf16[24,1664]{1,0:T(8,128)(2,1)S(1)} %get-tuple-element.229), channel_id=1, source_target_pairs={{1,0},{17,1},{0,16},{16,17},{33,32},{49,33},{32,48},{48,49},{3,2},... | collective-permute-start | bytes 239624 | tf_op jit(solution)/shard_map/ppermute | solution.py:88
  476.5 14.2 %collective-permute-start.28 = (bf16[24,1664]{1,0:T(8,128)(2,1)S(1)}, bf16[24,1664]{1,0:T(8,128)(2,1)S(1)}, u32[]{:S(2)}, u32[]{:S(2)}) collective-permute-start(bf16[24,1664]{1,0:T(8,128)(2,1)S(1)} %get-tuple-element.230), channel_id=1, source_target_pairs={{33,0},{49,1},{32,16},{48,17},{1,32},{17,33},{0,48},{16,49},{35,2}... | collective-permute-start | bytes 239624 | tf_op jit(solution)/shard_map/ppermute | solution.py:88
  478.8 17.5 %collective-permute-start.27 = (bf16[24,1664]{1,0:T(8,128)(2,1)S(1)}, bf16[24,1664]{1,0:T(8,128)(2,1)S(1)}, u32[]{:S(2)}, u32[]{:S(2)}) collective-permute-start(bf16[24,1664]{1,0:T(8,128)(2,1)S(1)} %get-tuple-element.231), channel_id=1, source_target_pairs={{32,0},{48,1},{33,16},{49,17},{0,32},{16,33},{1,48},{17,49},{34,2}... | collective-permute-start | bytes 239624 | tf_op jit(solution)/shard_map/ppermute | solution.py:88
  496.4 5.0 collective-permute-start.31
  501.3 1.2 collective-permute-start.29
  502.6 9.2 %collective-permute-start.30 = (f32[24,640]{1,0:T(8,128)S(1)}, f32[24,640]{1,0:T(8,128)S(1)}, u32[]{:S(2)}, u32[]{:S(2)}) collective-permute-start(f32[24,640]{1,0:T(8,128)S(1)} %slice_add_fusion.1), channel_id=1, source_target_pairs={{0,1},{1,0},{2,3},{3,2},{4,5},{5,4},{6,7},{7,6},{8,9},{9,8},{10,11... | collective-permute-start | bytes 184328 | tf_op jit(solution)/shard_map/ppermute | solution.py:32
  (38 other events, 107.6 us)
Sparse Core Ops, SparseCore 0:
  74.7 57.3 all-gather.2
  135.1 90.5 all-gather.4
  295.1 102.5 reduce-scatter.1

commit v5 on v4

--- a/solution.py
+++ b/solution.py
@@ -130,7 +130,7 @@
     hidden = weighted_ref.shape[1]
     each = hidden // (experts + 2)
     width = n2_ref.shape[1]
-    second = pl.program_id(0) == 1
+    second = pl.program_id(0) * 2 >= pl.num_programs(0)
     n2 = jnp.where(second, n2_other_ref[...], n2_pair_ref[...])
     gy = jnp.where(second, gy_other_ref[:, :width], gy_pair_ref[:, :width])
     flags = jnp.where(second, gy_other_ref[:, width:], gy_pair_ref[:, width:]).astype(F32)
@@ -199,9 +199,16 @@
 
 
 def experts_both_ways(n2_pair, n2_other, gy_pair, gy_other, ffn_w, router, experts):
-    tile, width = n2_pair.shape
-    rows = 2 * tile
+    half, width = n2_pair.shape
+    rows = 2 * half
+    tile = half // 2
     hidden = ffn_w.shape[1] // 3
+
+    def first_half(cols):
+        return pl.BlockSpec((tile, cols), lambda i: (jnp.minimum(i, 1), 0))
+
+    def second_half(cols):
+        return pl.BlockSpec((tile, cols), lambda i: (jnp.maximum(i - 2, 0), 0))
 
     def by_tile(cols):
         return pl.BlockSpec((tile, cols), lambda i: (i, 0))
@@ -210,9 +217,16 @@
     shapes = (width, width, 2 * hidden, hidden, width, width, 128)
     return pl.pallas_call(
         lambda *refs: expert_kernel(experts, *refs),
-        grid=(2,),
+        grid=(4,),
         in_specs=[
-            pl.BlockSpec(v.shape, lambda i: (0, 0), pipeline_mode=pl.Buffered(1)) for v in operands
+            first_half(width),
+            second_half(width),
+            first_half(gy_pair.shape[1]),
+            second_half(gy_pair.shape[1]),
+        ]
+        + [
+            pl.BlockSpec(v.shape, lambda i: (0, 0), pipeline_mode=pl.Buffered(1))
+            for v in operands[4:]
         ],
         out_specs=[by_tile(n) for n in shapes] + [pl.BlockSpec((1, width), lambda i: (0, 0))],
         out_shape=[jax.ShapeDtypeStruct((rows, n), BF16) for n in shapes]
@@ -353,6 +367,45 @@
     )(n1, dattn, dqkv, mixed, small)
 
 
+def norm_backward_kernel(sum_ref, got_ref, value_ref, scale_ref, gain_ref, grad_ref, out_ref, low_ref):
+    unit = value_ref[...] * scale_ref[...]
+    scaled = (sum_ref[...] + got_ref[...].astype(F32)) * gain_ref[...]
+    inside = jnp.mean(scaled * unit, axis=1, keepdims=True)
+    out = grad_ref[...].astype(F32) + scale_ref[...] * (scaled - unit * inside)
+    out_ref[...] = out
+    low_ref[...] = out.astype(BF16)
+
+
+def norm_backward(both, got, value, scale, gain, grad):
+    rows, width = got.shape
+    tile = rows // 4
+
+    def by_tile(cols):
+        return pl.BlockSpec((tile, cols), lambda i: (i, 0))
+
+    return pl.pallas_call(
+        norm_backward_kernel,
+        grid=(4,),
+        in_specs=[
+            by_tile(width),
+            by_tile(width),
+            by_tile(width),
+            by_tile(1),
+            pl.BlockSpec((1, width), lambda i: (0, 0)),
+            by_tile(width),
+        ],
+        out_specs=[by_tile(width), by_tile(width)],
+        out_shape=[
+            jax.ShapeDtypeStruct((rows, width), F32),
+            jax.ShapeDtypeStruct((rows, width), BF16),
+        ],
+        cost_estimate=pl.CostEstimate(
+            flops=10 * rows * width, transcendentals=0, bytes_accessed=18 * rows * width
+        ),
+        name="norm_backward",
+    )(both, got, value, scale, gain, grad)
+
+
 def attention_scores(query, key):
     scaled = jnp.einsum("slgd,smd->sglm", query, key, preferred_element_type=F32) * (
         1.0 / math.sqrt(HEAD_SIZE)
@@ -556,19 +609,17 @@
         n2_pair, n2_other, gy_pair, gy_other, ffn_w, router_low, experts
     )
     dn2_sum, (dab, weighted) = core_sum(dn2_part, (dab, weighted))
-    dn2 = pair_sum(dn2_sum)
+    quarter = dn2_sum.shape[0] // 2
+    dn2_got = swapped(dn2_sum[quarter:].astype(BF16), "z0")
     big_down = dot(gy, weighted, (0, 0), BF16)
     big_ffn = jnp.concatenate([dot(n2, dab, (0, 0), BF16), big_down], axis=1)
     small_router = dot(dlogits, n2, (0, 0))[:experts]
     small_ffn = small_ffn / gain_f
-    dn2, big_ffn = lax.optimization_barrier((dn2, big_ffn))
+    dn2_got, big_ffn = lax.optimization_barrier((dn2_got, big_ffn))
     near_ffn = xy_scattered(big_ffn)
-    scaled = dn2 * gain_f
-    dh = gy_own + scale_ffn * (
-        scaled - unit_ffn * jnp.mean(scaled * unit_ffn, axis=-1, keepdims=True)
-    )
-
-    dattn_own, out_part = lax.optimization_barrier((dh.astype(BF16), out_part))
+    dh, dattn_own = norm_backward(dn2_sum, dn2_got, h_own, scale_ffn, gain_f, gy_own_low[:, :width])
+
+    dattn_own, out_part = lax.optimization_barrier((dattn_own, out_part))
     out_halves = z_halves(core_sum(out_part, ())[0].astype(BF16))
     dattn_other, small_router, out_halves = lax.optimization_barrier(
         (swapped(dattn_own, "z0"), small_router, out_halves)

time: 531 us -> 524 us (0.987)
  other arithmetic: 42.5 us -> 35.3 us
  waiting for transfers between devices: 187 us -> 180 us
    ppermute x8, waiting for transfers between devices: 31 us -> 18.2 us  [z_scattered(): total = total + lax.ppermute(piece, ('z1', 'z0', 'zh'), back).astype(F32)]
    all_to_all x1, waiting for transfers between devices: 0.01 us -> 10.5 us  [on_device(): dx_got = lax.all_to_all(dx_sent, DP, 0, 0, tiled=True)]
    pallas_call x1 -> x2, Pallas kernels: 35.8 us -> 39.6 us  [the longest x1 34.8 us: experts_both_ways(): pl.pallas_call(lambda *refs: expert_kernel(experts, *refs), grid=(4,), in...]
    unnamed x181 -> x189, local copies, waits for them, and re-layouts: 25.2 us -> 26.2 us
  transfers between devices with their start and end apart: 42 -> 42, of which waited for: 24 -> 24; matrix products, arithmetic and copies ran while one was open for 20% -> 21% of each run, Pallas kernels for 5% -> 6%
where the time goes in v5:
time: 524 us; the launch traced here: 514 us
  waiting for transfers between devices  180 us (34%)
  starting transfers between devices  116 us (22%)
  Pallas kernels  63.3 us (12%)
  local copies, waits for them, and re-layouts  63 us (12%)
  matrix products  40.2 us (8%)
  other arithmetic  35.3 us (7%)
  between operations  15.7 us (3%)
    ppermute x20, waiting for transfers between devices, swapped(): lax.ppermute(value, axis, [(i, i ^ bit) for i in range(lax.axis_size(axis...  81 us
    pallas_call x1, Pallas kernels, experts_both_ways(): pl.pallas_call(lambda *refs: expert_kernel(experts, *refs), grid=(4,), in...  34.8 us
    dot_general x9, matrix products, dot(): lax.dot_general(left, right, (((contract[0],), (contract[1],)), ((), ()))...  34.6 us
    ppermute x4, waiting for transfers between devices, z_gathered(): lax.ppermute(shard, ('z1', 'z0', 'zh'), pairs)  30.5 us
    unnamed x189, local copies, waits for them, and re-layouts  26.2 us
    ppermute x20, starting transfers between devices, swapped(): lax.ppermute(value, axis, [(i, i ^ bit) for i in range(lax.axis_size(axis...  23.1 us
    all_to_all x1, starting transfers between devices, on_device(): dx_got = lax.all_to_all(dx_sent, DP, 0, 0, tiled=True)  18.7 us
    ppermute x8, waiting for transfers between devices, z_scattered(): total = total + lax.ppermute(piece, ('z1', 'z0', 'zh'), back).astype(F32)  18.2 us
  transfers between devices with their start and end apart: 42, of which 24 were waited for; matrix products, arithmetic and copies ran while one was open for 21% of the time, Pallas kernels for 6%

profile of v5, /device:TPU:1, one launch (start us, length us, event | category | flops | bytes accessed | tf_op | source)
XLA Modules:
  0.0 514.1 jit_solution(17821980666228962358)
XLA Ops:
  11.4 2.0 copy.499
  13.5 14.0 %all-to-all-start = ((bf16[128,26,128]{2,1,0:T(8,128)(2,1)}), bf16[128,26,128]{2,1,0:T(8,128)(2,1)S(1)}, u32[]{:S(2)}, u32[]{:S(2)}) async-start(bf16[128,26,128]{2,1,0:T(8,128)(2,1)} %copy.499), calls=%async_computation | async-start | bytes 2097152 | tf_op jit(solution)/shard_map/all_to_all | solution.py:521
  31.3 3.5 collective-permute-start.1
  34.7 3.5 collective-permute-start.2
  38.3 2.1 collective-permute-start.3
  41.9 16.4 %collective-permute-done.2 = bf16[24,4864]{1,0:T(8,128)(2,1)} collective-permute-done((bf16[24,4864]{1,0:T(8,128)(2,1)}, bf16[24,4864]{1,0:T(8,128)(2,1)}, u32[]{:S(2)}, u32[]{:S(2)}) %collective-permute-start.2) | collective-permute-done | bytes 233504 | tf_op jit(solution)/shard_map/ppermute | solution.py:78
  58.3 14.1 %collective-permute-done.3 = bf16[24,4864]{1,0:T(8,128)(2,1)} collective-permute-done((bf16[24,4864]{1,0:T(8,128)(2,1)}, bf16[24,4864]{1,0:T(8,128)(2,1)}, u32[]{:S(2)}, u32[]{:S(2)}) %collective-permute-start.3) | collective-permute-done | bytes 233504 | tf_op jit(solution)/shard_map/ppermute | solution.py:78
  79.0 2.1 multiply_reduce_fusion.2
  83.7 9.6 %all-to-all-start.1 = ((bf16[128,24,128]{2,1,0:T(8,128)(2,1)}), bf16[128,24,128]{2,1,0:T(8,128)(2,1)S(1)}, u32[]{:S(2)}, u32[]{:S(2)}) async-start(bf16[128,24,128]{2,1,0:T(8,128)(2,1)} %copy.505), calls=%async_computation.1 | async-start | bytes 1572864 | tf_op jit(solution)/shard_map/all_to_all | solution.py:568
  93.4 5.1 collective-permute-start.6
  99.9 10.8 %collective-permute-done.6 = f32[2,8]{1,0:T(2,128)S(1)} collective-permute-done((f32[2,8]{1,0:T(2,128)S(1)}, f32[2,8]{1,0:T(2,128)S(1)}, u32[]{:S(2)}, u32[]{:S(2)}) %collective-permute-start.6) | collective-permute-done | bytes 96 | tf_op jit(solution)/shard_map/ppermute | solution.py:32
  111.0 6.3 %all-to-all-done.1 = bf16[128,24,128]{2,1,0:T(8,128)(2,1)S(1)} async-done(((bf16[128,24,128]{2,1,0:T(8,128)(2,1)}), bf16[128,24,128]{2,1,0:T(8,128)(2,1)S(1)}, u32[]{:S(2)}, u32[]{:S(2)}) %all-to-all-start.1) | async-done | bytes 786464 | tf_op jit(solution)/shard_map/all_to_all | solution.py:568
  118.2 2.1 fusion.9
  120.4 4.1 collective-permute-done.5
  124.5 2.4 pad_maximum_fusion.1
  130.0 4.7 all-to-all-start.2
  134.7 2.1 constant_dynamic-update-slice_fusion.63
  138.1 5.1 fusion.18.refs_2_
  144.7 1.8 fusion.90
  147.9 7.6 %all-to-all-done.2 = bf16[2,256,1664]{2,1,0:T(8,128)(2,1)} async-done(((bf16[2,256,1664]{2,1,0:T(8,128)(2,1)}), bf16[2,256,1664]{2,1,0:T(8,128)(2,1)}, u32[]{:S(2)}, u32[]{:S(2)}) %all-to-all-start.2) | async-done | bytes 1703968 | tf_op jit(solution)/shard_map/all_to_all | solution.py:581
  155.5 3.1 convolution_convert_fusion.2
  159.7 3.0 collective-permute-done.8
  165.2 18.7 %collective-permute-done.9 = bf16[256,1536]{1,0:T(8,128)(2,1)} collective-permute-done((bf16[256,1536]{1,0:T(8,128)(2,1)S(1)}, bf16[256,1536]{1,0:T(8,128)(2,1)}, u32[]{:S(2)}, u32[]{:S(2)}) %collective-permute-start.9) | collective-permute-done | bytes 786464 | tf_op jit(solution)/shard_map/ppermute | solution.py:32
  183.8 2.0 multiply_reduce_fusion.1
  187.4 3.6 reverse_select_fusion
  192.4 12.8 %collective-permute-done.10 = bf16[256,1536]{1,0:T(8,128)(2,1)} collective-permute-done((bf16[256,1536]{1,0:T(8,128)(2,1)S(1)}, bf16[256,1536]{1,0:T(8,128)(2,1)}, u32[]{:S(2)}, u32[]{:S(2)}) %collective-permute-start.10) | collective-permute-done | bytes 786464 | tf_op jit(solution)/shard_map/ppermute | solution.py:32
  206.5 2.4 collective-permute-start.11
  212.0 12.3 %all-gather.5.cloned.1.call-done.refs_4_ = bf16[1536,3840]{1,0:T(8,128)(2,1)} async-done(((bf16[96,3840]{1,0:T(8,128)(2,1)}), bf16[1536,3840]{1,0:T(8,128)(2,1)}) %all-gather.5.cloned.1.call-update) | async-done | bytes 11796496 | tf_op jit(solution)/shard_map/all_gather | solution.py:93
  224.4 34.8 %experts.1 = (bf16[1024,1536]{1,0:T(8,128)(2,1)}, bf16[1024,1536]{1,0:T(8,128)(2,1)}, bf16[1024,2560]{1,0:T(8,128)(2,1)}, bf16[1024,1280]{1,0:T(8,128)(2,1)}, bf...) custom-call(bf16[512,1536]{1,0:T(8,128)(2,1)} %copy-done.26, ...), custom_call_target="tpu_custom_call" | custom-call | flops 24159191040 | bytes 44826624 | tf_op jit(solution)/shard_map/experts/pallas_call | solution.py:218
  261.7 3.0 collective-permute-done.13
  268.4 11.5 %convolution_convert_fusion = bf16[1536,2560]{1,0:T(8,128)(2,1)S(1)} fusion(bf16[1024,1536]{1,0:T(8,128)(2,1)S(1)} %copy-done.22, bf16[1024,2560]{1,0:T(8,128)(2,1)} %get-tuple-element.75), kind=kOutput, calls=%fused_computation.1 | convolution fusion | flops 8056995840 | bytes 16252928 | tf_op jit(solution)/shard_map/dot_general | solution.py:25
  279.9 4.6 convolution_convert_fusion.1
  284.6 5.1 pad_maximum_fusion
  292.9 4.8 norm_backward.1
  301.0 2.2 collective-permute-done.16
  305.1 14.3 %collective-permute-done.15 = bf16[256,1536]{1,0:T(8,128)(2,1)S(1)} collective-permute-done((bf16[256,1536]{1,0:T(8,128)(2,1)S(1)}, bf16[256,1536]{1,0:T(8,128)(2,1)S(1)}, u32[]{:S(2)}, u32[]{:S(2)}) %collective-permute-start.15) | collective-permute-done | bytes 786464 | tf_op jit(solution)/shard_map/ppermute | solution.py:32
  321.4 5.1 all-to-all-start.3
  329.6 18.1 %attention_backward.1 = (bf16[1024,1536]{1,0:T(8,128)(2,1)S(1)}, bf16[1024,640]{1,0:T(8,128)(2,1)S(1)}, bf16[1024,1536]{1,0:T(8,128)(2,1)}, f32[1,1536]{1,0:T(1,128)S(1)}) custom-call(bf16[512,1536]{1,0:T(8,128)(2,1)S(1)} %copy-done.9, bf16[512,1536]{1,0:T(8,128)(2,1)} %collective-permute-done.17.refs_1_, bf16[1024,640]{1,0:T(8,128)(2,1)S(1)} %copy-done.7, ...), custom_call_target="tpu_custom_call" | custom-call | flops 19327352832 | bytes 21495808 | tf_op jit(solution)/shard_map/attention_backward/pallas_call | solution.py:310
  349.3 2.7 slice.515
  352.7 1.9 convert_reduce_fusion.1
  354.6 3.1 fusion.10
  360.5 10.1 %all-to-all-start.4 = ((bf16[128,24,128]{2,1,0:T(8,128)(2,1)}), bf16[128,24,128]{2,1,0:T(8,128)(2,1)S(1)}, u32[]{:S(2)}, u32[]{:S(2)}) async-start(bf16[128,24,128]{2,1,0:T(8,128)(2,1)} %copy.522), calls=%async_computation.4 | async-start | bytes 1572864 | tf_op jit(solution)/shard_map/all_to_all | solution.py:636
  370.6 1.9 copy-done.3
  372.5 1.9 copy-done.5
  374.4 5.6 %attention_gradients.1 = bf16[16,112,1024]{2,1,0:T(8,128)(2,1)S(1)} custom-call(bf16[1024,1536]{1,0:T(8,128)(2,1)S(1)} %copy-done.3, bf16[1024,1536]{1,0:T(8,128)(2,1)S(1)} %copy-done.5, bf16[1024,640]{1,0:T(8,128)(2,1)S(1)} %get-tuple-element.89.dqkv_ref, bf16[1024,384]{1,0:T(8,128)(2,1)S(1)} %copy.520.mixed_ref, bf16[16,1024]{1,0:T(8,128)(2,1)S(1)} %fusion.54.lines_ref), custom_call_target="tpu_custom_call" | custom-call | flops 3221225472 | bytes 12058624 | tf_op jit(solution)/shard_map/attention_gradients/pallas_call | solution.py:354
  380.0 3.0 convert_add_fusion
  386.1 8.4 %all-to-all-done.4 = bf16[128,24,128]{2,1,0:T(8,128)(2,1)S(1)} async-done(((bf16[128,24,128]{2,1,0:T(8,128)(2,1)}), bf16[128,24,128]{2,1,0:T(8,128)(2,1)S(1)}, u32[]{:S(2)}, u32[]{:S(2)}) %all-to-all-start.4) | async-done | bytes 786464 | tf_op jit(solution)/shard_map/all_to_all | solution.py:636
  394.5 4.7 all-to-all-start.5
  401.0 4.1 collective-permute-done.19
  405.1 3.2 convert_add_fusion.4
  410.2 4.9 collective-permute-start.21
  416.0 2.0 multiply_reduce_fusion
  418.1 3.2 collective-permute-done.21
  421.3 7.4 %collective-permute-done.22 = bf16[24,3840]{1,0:T(8,128)(2,1)S(1)} collective-permute-done((bf16[24,3840]{1,0:T(8,128)(2,1)S(1)}, bf16[24,3840]{1,0:T(8,128)(2,1)S(1)}, u32[]{:S(2)}, u32[]{:S(2)}) %collective-permute-start.22) | collective-permute-done | bytes 184352 | tf_op jit(solution)/shard_map/ppermute | solution.py:88
  428.6 7.6 %collective-permute-done.23 = bf16[24,3840]{1,0:T(8,128)(2,1)S(1)} collective-permute-done((bf16[24,3840]{1,0:T(8,128)(2,1)S(1)}, bf16[24,3840]{1,0:T(8,128)(2,1)S(1)}, u32[]{:S(2)}, u32[]{:S(2)}) %collective-permute-start.23) | collective-permute-done | bytes 184352 | tf_op jit(solution)/shard_map/ppermute | solution.py:88
  437.4 2.4 fusion.11
  440.2 5.1 all-to-all-done.5
  445.3 2.7 convert_reduce_fusion
  449.6 4.8 collective-permute-start.26
  454.4 2.9 collective-permute-start.27
  457.3 1.7 collective-permute-start.28
  460.2 18.7 %all-to-all-start.6 = ((bf16[128,24,128]{2,1,0:T(8,128)(2,1)}), bf16[128,24,128]{2,1,0:T(8,128)(2,1)S(1)}, u32[]{:S(2)}, u32[]{:S(2)}) async-start(bf16[128,24,128]{2,1,0:T(8,128)(2,1)} %copy.526), calls=%async_computation.7 | async-start | bytes 1572864 | tf_op jit(solution)/shard_map/all_to_all | solution.py:653
  489.0 4.7 collective-permute-done.30
  495.0 10.5 %all-to-all-done.6 = bf16[128,24,128]{2,1,0:T(8,128)(2,1)S(1)} async-done(((bf16[128,24,128]{2,1,0:T(8,128)(2,1)}), bf16[128,24,128]{2,1,0:T(8,128)(2,1)S(1)}, u32[]{:S(2)}, u32[]{:S(2)}) %all-to-all-start.6) | async-done | bytes 786464 | tf_op jit(solution)/shard_map/all_to_all | solution.py:653
  (379 shorter events, 88.3 us)
Async XLA Ops:
  7.2 34.0 %copy-start = (bf16[2,128,1,1536]{3,1,2,0:T(8,128)(2,1)S(1)}, bf16[2,128,1,1536]{3,1,2,0:T(8,128)(2,1)}, u32[]{:S(2)}) copy-start(bf16[2,128,1,1536]{3,1,2,0:T(8,128)(2,1)} %param.19) | copy-start | bytes 2359300
  11.0 30.1 %copy-start.47 = (s32[2,1,128]{2,1,0:T(1,128)}, s32[2,1,128]{2,1,0:T(1,128)S(1)}, u32[]{:S(2)}) copy-start(s32[2,1,128]{2,1,0:T(1,128)S(1)} %constant_dynamic-slice_fusion.1) | copy-start | bytes 3076
  11.4 16.1 %copy-start.41 = (bf16[12,768]{1,0:T(8,128)(2,1)S(1)}, bf16[12,768]{1,0:T(8,128)(2,1)}, u32[]{:S(2)}) copy-start(bf16[12,768]{1,0:T(8,128)(2,1)} %param.25) | copy-start | bytes 55300
  11.4 16.1 %copy-start.33 = (bf16[8,12,256]{2,0,1:T(8,128)(2,1)S(1)}, bf16[8,12,256]{2,0,1:T(8,128)(2,1)}, u32[]{:S(2)}) copy-start(bf16[8,12,256]{2,0,1:T(8,128)(2,1)} %param.30) | copy-start | bytes 147460
  11.4 16.2 %copy-start.34 = (bf16[8,12,256]{2,0,1:T(8,128)(2,1)S(1)}, bf16[8,12,256]{2,0,1:T(8,128)(2,1)}, u32[]{:S(2)}) copy-start(bf16[8,12,256]{2,0,1:T(8,128)(2,1)} %param.31) | copy-start | bytes 147460
  13.4 14.4 %copy-start.54 = (bf16[12,256]{1,0:T(8,128)(2,1)S(1)}, bf16[12,256]{1,0:T(8,128)(2,1)}, u32[]{:S(2)}) copy-start(bf16[12,256]{1,0:T(8,128)(2,1)} %param.27) | copy-start | bytes 18436
  13.4 14.4 %copy-start.42 = (bf16[768,12]{0,1:T(8,128)(2,1)S(1)}, bf16[768,12]{0,1:T(8,128)(2,1)}, u32[]{:S(2)}) copy-start(bf16[768,12]{0,1:T(8,128)(2,1)} %param.28) | copy-start | bytes 55300
  13.4 14.6 %copy-start.44 = (bf16[12,512]{1,0:T(8,128)(2,1)S(1)}, bf16[12,512]{1,0:T(8,128)(2,1)}, u32[]{:S(2)}) copy-start(bf16[12,512]{1,0:T(8,128)(2,1)} %param.33) | copy-start | bytes 36868
  13.4 14.8 %copy-start.45 = (bf16[12,512]{1,0:T(8,128)(2,1)S(1)}, bf16[12,512]{1,0:T(8,128)(2,1)}, u32[]{:S(2)}) copy-start(bf16[12,512]{1,0:T(8,128)(2,1)} %param.34) | copy-start | bytes 36868
  13.5 14.9 %copy-start.46 = (bf16[512,12]{0,1:T(8,128)(2,1)S(1)}, bf16[512,12]{0,1:T(8,128)(2,1)}, u32[]{:S(2)}) copy-start(bf16[512,12]{0,1:T(8,128)(2,1)} %param.35) | copy-start | bytes 36868
  13.5 60.4 %all-to-all-start = ((bf16[128,26,128]{2,1,0:T(8,128)(2,1)}), bf16[128,26,128]{2,1,0:T(8,128)(2,1)S(1)}, u32[]{:S(2)}, u32[]{:S(2)}) async-start(bf16[128,26,128]{2,1,0:T(8,128)(2,1)} %copy.499), calls=%async_computation | async-start | bytes 2097152 | tf_op jit(solution)/shard_map/all_to_all | solution.py:521
  27.5 110.7 %all-gather.3.cloned.1.call-start = ((), (), s32[]{:S(2)}) async-start(), calls=%async_computation.8 | async-start | bytes 3342336 | tf_op jit(solution)/shard_map/all_gather | solution.py:93
  28.4 2.0 collective-permute-start
  31.3 10.7 %collective-permute-start.1 = (bf16[24,4864]{1,0:T(8,128)(2,1)}, bf16[24,4864]{1,0:T(8,128)(2,1)}, u32[]{:S(2)}, u32[]{:S(2)}) collective-permute-start(bf16[24,4864]{1,0:T(8,128)(2,1)} %maximum_select_fusion.1), channel_id=1, source_target_pairs={{0,0},{1,16},{16,1},{17,17},{32,32},{33,48},{48,33},{49,49},{2,2},... | collective-permute-start | bytes 700424 | tf_op jit(solution)/shard_map/ppermute | solution.py:78
  34.7 23.6 %collective-permute-start.2 = (bf16[24,4864]{1,0:T(8,128)(2,1)}, bf16[24,4864]{1,0:T(8,128)(2,1)}, u32[]{:S(2)}, u32[]{:S(2)}) collective-permute-start(bf16[24,4864]{1,0:T(8,128)(2,1)} %maximum_select_fusion.1), channel_id=1, source_target_pairs={{0,1},{1,17},{16,0},{17,16},{32,33},{33,49},{48,32},{49,48},{2,3},... | collective-permute-start | bytes 700424 | tf_op jit(solution)/shard_map/ppermute | solution.py:78
  38.3 34.1 %collective-permute-start.3 = (bf16[24,4864]{1,0:T(8,128)(2,1)}, bf16[24,4864]{1,0:T(8,128)(2,1)}, u32[]{:S(2)}, u32[]{:S(2)}) collective-permute-start(bf16[24,4864]{1,0:T(8,128)(2,1)} %maximum_select_fusion.1), channel_id=1, source_target_pairs={{0,32},{1,48},{16,33},{17,49},{32,0},{33,16},{48,1},{49,17},{2,34}... | collective-permute-start | bytes 700424 | tf_op jit(solution)/shard_map/ppermute | solution.py:78
  40.4 32.0 %collective-permute-start.4 = (bf16[24,4864]{1,0:T(8,128)(2,1)}, bf16[24,4864]{1,0:T(8,128)(2,1)}, u32[]{:S(2)}, u32[]{:S(2)}) collective-permute-start(bf16[24,4864]{1,0:T(8,128)(2,1)} %maximum_select_fusion.1), channel_id=1, source_target_pairs={{0,33},{1,49},{16,32},{17,48},{32,1},{33,17},{48,0},{49,16},{2,35}... | collective-permute-start | bytes 700424 | tf_op jit(solution)/shard_map/ppermute | solution.py:78
  74.6 149.8 %all-gather.5.cloned.1.call-start = ((), (), s32[]{:S(2)}) async-start(), calls=%async_computation.9 | async-start | bytes 12533760 | tf_op jit(solution)/shard_map/all_gather | solution.py:93
  77.3 40.9 %copy-start.55 = (s32[1536]{0:T(1024)}, s32[1536]{0:T(1024)S(1)}, u32[]{:S(2)}) copy-start(s32[1536]{0:T(1024)S(1)} %fusion.67) | copy-start | bytes 18436
  83.7 33.6 %all-to-all-start.1 = ((bf16[128,24,128]{2,1,0:T(8,128)(2,1)}), bf16[128,24,128]{2,1,0:T(8,128)(2,1)S(1)}, u32[]{:S(2)}, u32[]{:S(2)}) async-start(bf16[128,24,128]{2,1,0:T(8,128)(2,1)} %copy.505), calls=%async_computation.1 | async-start | bytes 1572864 | tf_op jit(solution)/shard_map/all_to_all | solution.py:568
  93.4 17.3 %collective-permute-start.6 = (f32[2,8]{1,0:T(2,128)S(1)}, f32[2,8]{1,0:T(2,128)S(1)}, u32[]{:S(2)}, u32[]{:S(2)}) collective-permute-start(f32[2,8]{1,0:T(2,128)S(1)} %convert_reduce_fusion.2), channel_id=1, source_target_pairs={{0,1},{1,0},{2,3},{3,2},{4,5},{5,4},{6,7},{7,6},{8,9},{9,8},{10,11... | collective-permute-start | bytes 200 | tf_op jit(solution)/shard_map/ppermute | solution.py:32
  98.5 26.0 %collective-permute-start.5 = (bf16[256,1536]{1,0:T(8,128)(2,1)S(1)}, bf16[256,1536]{1,0:T(8,128)(2,1)}, u32[]{:S(2)}, u32[]{:S(2)}) collective-permute-start(bf16[256,1536]{1,0:T(8,128)(2,1)S(1)} %multiply_convert_fusion.2), channel_id=1, source_target_pairs={{0,16},{16,0},{1,17},{17,1},{2,18},{18,2},{3,19},{19,3},{4,20},{20... | collective-permute-start | bytes 2359304 | tf_op jit(solution)/shard_map/ppermute | solution.py:32
  126.9 9.9 %collective-permute-start.7 = (bf16[512,1536]{1,0:T(8,128)(2,1)}, bf16[512,1536]{1,0:T(8,128)(2,1)S(1)}, u32[]{:S(2)}, u32[]{:S(2)}) collective-permute-start(bf16[512,1536]{1,0:T(8,128)(2,1)} %pad_maximum_fusion.1), channel_id=1, source_target_pairs={{0,2},{2,0},{1,3},{3,1},{4,6},{6,4},{5,7},{7,5},{8,10},{10,8},{9,1... | collective-permute-start | bytes 4718600 | tf_op jit(solution)/shard_map/ppermute | solution.py:32
  130.0 25.5 %all-to-all-start.2 = ((bf16[2,256,1664]{2,1,0:T(8,128)(2,1)}), bf16[2,256,1664]{2,1,0:T(8,128)(2,1)}, u32[]{:S(2)}, u32[]{:S(2)}) async-start(bf16[2,256,1664]{2,1,0:T(8,128)(2,1)} %broadcast_in_dim.30), calls=%async_computation.2 | async-start | bytes 3407872 | tf_op jit(solution)/shard_map/all_to_all | solution.py:581
  134.7 273.6 %reduce-scatter.2.cloned.1.call-start = ((), (), s32[]{:S(2)}) async-start(), calls=%async_computation.10 | async-start | bytes 12533760 | tf_op jit(solution)/shard_map/reduce_scatter | solution.py:97
  158.8 3.9 collective-permute-start.8
  164.8 19.0 %copy-start.12 = (f32[256,1536]{1,0:T(8,128)S(1)}, f32[256,1536]{1,0:T(8,128)}, u32[]{:S(2)}) copy-start(f32[256,1536]{1,0:T(8,128)} %copy-done.11) | copy-start | bytes 4718596
  164.9 18.9 %collective-permute-start.9 = (bf16[256,1536]{1,0:T(8,128)(2,1)S(1)}, bf16[256,1536]{1,0:T(8,128)(2,1)}, u32[]{:S(2)}, u32[]{:S(2)}) collective-permute-start(bf16[256,1536]{1,0:T(8,128)(2,1)S(1)} %slice.707), channel_id=1, source_target_pairs={{0,16},{16,0},{1,17},{17,1},{2,18},{18,2},{3,19},{19,3},{4,20},{20... | collective-permute-start | bytes 2359304 | tf_op jit(solution)/shard_map/ppermute | solution.py:32
  187.2 18.0 %collective-permute-start.10 = (bf16[256,1536]{1,0:T(8,128)(2,1)S(1)}, bf16[256,1536]{1,0:T(8,128)(2,1)}, u32[]{:S(2)}, u32[]{:S(2)}) collective-permute-start(bf16[256,1536]{1,0:T(8,128)(2,1)S(1)} %multiply_convert_fusion.1), channel_id=1, source_target_pairs={{0,16},{16,0},{1,17},{17,1},{2,18},{18,2},{3,19},{19,3},{4,20},{20... | collective-permute-start | bytes 2359304 | tf_op jit(solution)/shard_map/ppermute | solution.py:32
  191.0 20.0 %collective-permute-start.12 = (bf16[512,1664]{1,0:T(8,128)(2,1)}, bf16[512,1664]{1,0:T(8,128)(2,1)}, u32[]{:S(2)}, u32[]{:S(2)}) collective-permute-start(bf16[512,1664]{1,0:T(8,128)(2,1)} %bitcast.80.refs_2_), channel_id=1, source_target_pairs={{0,2},{2,0},{1,3},{3,1},{4,6},{6,4},{5,7},{7,5},{8,10},{10,8},{9,1... | collective-permute-start | bytes 5111816 | tf_op jit(solution)/shard_map/ppermute | solution.py:32
  206.5 17.9 %copy-start.26 = (bf16[512,1536]{1,0:T(8,128)(2,1)}, bf16[512,1536]{1,0:T(8,128)(2,1)S(1)}, u32[]{:S(2)}) copy-start(bf16[512,1536]{1,0:T(8,128)(2,1)S(1)} %pad_maximum_fusion.2.refs_0_) | copy-start | bytes 4718596
  206.5 5.5 %collective-permute-start.11 = (bf16[512,1536]{1,0:T(8,128)(2,1)S(1)}, bf16[512,1536]{1,0:T(8,128)(2,1)}, u32[]{:S(2)}, u32[]{:S(2)}) collective-permute-start(bf16[512,1536]{1,0:T(8,128)(2,1)S(1)} %pad_maximum_fusion.2.refs_0_), channel_id=1, source_target_pairs={{0,2},{2,0},{1,3},{3,1},{4,6},{6,4},{5,7},{7,5},{8,10},{10,8},{9,1... | collective-permute-start | bytes 4718600 | tf_op jit(solution)/shard_map/ppermute | solution.py:32
  260.9 3.8 collective-permute-start.13
  266.8 22.8 %collective-permute-start.14 = (bf16[256,1536]{1,0:T(8,128)(2,1)S(1)}, bf16[256,1536]{1,0:T(8,128)(2,1)S(1)}, u32[]{:S(2)}, u32[]{:S(2)}) collective-permute-start(bf16[256,1536]{1,0:T(8,128)(2,1)S(1)} %slice.706), channel_id=1, source_target_pairs={{0,16},{16,0},{1,17},{17,1},{2,18},{18,2},{3,19},{19,3},{4,20},{20... | collective-permute-start | bytes 2359304 | tf_op jit(solution)/shard_map/ppermute | solution.py:32
  299.4 3.8 collective-permute-start.16
  300.7 18.7 %collective-permute-start.15 = (bf16[256,1536]{1,0:T(8,128)(2,1)S(1)}, bf16[256,1536]{1,0:T(8,128)(2,1)S(1)}, u32[]{:S(2)}, u32[]{:S(2)}) collective-permute-start(bf16[256,1536]{1,0:T(8,128)(2,1)S(1)} %copy-done.29), channel_id=1, source_target_pairs={{0,16},{16,0},{1,17},{17,1},{2,18},{18,2},{3,19},{19,3},{4,20},{20... | collective-permute-start | bytes 2359304 | tf_op jit(solution)/shard_map/ppermute | solution.py:32
  303.6 17.3 %copy-start.31 = (f32[1,4,4,2,2,24]{5,4,3,2,1,0:T(2,128)S(1)}, f32[1,4,4,2,2,24]{5,4,3,2,1,0:T(2,128)}, u32[]{:S(2)}) copy-start(f32[1,4,4,2,2,24]{5,4,3,2,1,0:T(2,128)} %copy-done.30) | copy-start | bytes 18436
  303.6 17.4 %copy-start.20 = (bf16[48,8,8,128]{3,1,2,0:T(8,128)(2,1)S(1)}, bf16[48,8,8,128]{3,1,2,0:T(8,128)(2,1)}, u32[]{:S(2)}) copy-start(bf16[48,8,8,128]{3,1,2,0:T(8,128)(2,1)} %copy-done.19) | copy-start | bytes 2359300
  305.0 16.3 %copy-start.39 = (f32[1,1536]{1,0:T(1,128)S(1)}, f32[1,1536]{1,0:T(1,128)}, u32[]{:S(2)}) copy-start(f32[1,1536]{1,0:T(1,128)} %slice.509.gain_ref) | copy-start | bytes 18436
  305.1 16.4 %copy-start.57 = (f32[1,1536]{1,0:T(1,128)S(1)}, f32[1,1536]{1,0:T(1,128)}, u32[]{:S(2)}) copy-start(f32[1,1536]{1,0:T(1,128)} %get-tuple-element.91) | copy-start | bytes 18436
  319.5 7.1 %collective-permute-start.17 = (bf16[512,1536]{1,0:T(8,128)(2,1)S(1)}, bf16[512,1536]{1,0:T(8,128)(2,1)}, u32[]{:S(2)}, u32[]{:S(2)}) collective-permute-start(bf16[512,1536]{1,0:T(8,128)(2,1)S(1)} %constant_dynamic-update-slice_fusion.65.refs_0_), channel_id=1, source_target_pairs={{0,2},{2,0},{1,3},{3,1},{4,6},{6,4},{5,7},{7,5},{8,10},{10,8},{9,1... | collective-permute-start | bytes 4718600 | tf_op jit(solution)/shard_map/ppermute | solution.py:32
  321.4 31.2 %all-to-all-start.3 = ((bf16[2,256,1536]{2,1,0:T(8,128)(2,1)}), bf16[2,256,1536]{2,1,0:T(8,128)(2,1)}, u32[]{:S(2)}, u32[]{:S(2)}) async-start(bf16[2,256,1536]{2,1,0:T(8,128)(2,1)} %reverse_select_fusion.1), calls=%async_computation.3 | async-start | bytes 3145728 | tf_op jit(solution)/shard_map/all_to_all | solution.py:632
  352.0 28.0 %collective-permute-start.18 = (bf16[512,1536]{1,0:T(8,128)(2,1)}, bf16[512,1536]{1,0:T(8,128)(2,1)}, u32[]{:S(2)}, u32[]{:S(2)}) collective-permute-start(bf16[512,1536]{1,0:T(8,128)(2,1)} %slice.515), channel_id=1, source_target_pairs={{0,2},{2,0},{1,3},{3,1},{4,6},{6,4},{5,7},{7,5},{8,10},{10,8},{9,1... | collective-permute-start | bytes 4718600 | tf_op jit(solution)/shard_map/ppermute | solution.py:32
  360.5 34.0 %all-to-all-start.4 = ((bf16[128,24,128]{2,1,0:T(8,128)(2,1)}), bf16[128,24,128]{2,1,0:T(8,128)(2,1)S(1)}, u32[]{:S(2)}, u32[]{:S(2)}) async-start(bf16[128,24,128]{2,1,0:T(8,128)(2,1)} %copy.522), calls=%async_computation.4 | async-start | bytes 1572864 | tf_op jit(solution)/shard_map/all_to_all | solution.py:636
  384.7 15.0 %copy-start.48 = (s32[2,1,128]{2,1,0:T(1,128)S(1)}, s32[2,1,128]{2,1,0:T(1,128)}, u32[]{:S(2)}) copy-start(s32[2,1,128]{2,1,0:T(1,128)} %copy-done.47) | copy-start | bytes 3076
  384.7 20.4 %collective-permute-start.19 = (bf16[256,1536]{1,0:T(8,128)(2,1)S(1)}, bf16[256,1536]{1,0:T(8,128)(2,1)}, u32[]{:S(2)}, u32[]{:S(2)}) collective-permute-start(bf16[256,1536]{1,0:T(8,128)(2,1)S(1)} %slice.705), channel_id=1, source_target_pairs={{0,16},{16,0},{1,17},{17,1},{2,18},{18,2},{3,19},{19,3},{4,20},{20... | collective-permute-start | bytes 2359304 | tf_op jit(solution)/shard_map/ppermute | solution.py:32
  394.5 50.8 %all-to-all-start.5 = ((bf16[16,112,1024]{2,1,0:T(8,128)(2,1)}), bf16[16,112,1024]{2,1,0:T(8,128)(2,1)}, u32[]{:S(2)}, u32[]{:S(2)}) async-start(bf16[16,112,1024]{2,1,0:T(8,128)(2,1)} %copy-done.2), calls=%async_computation.5 | async-start | bytes 7340032 | tf_op jit(solution)/shard_map/all_to_all | solution.py:648
  401.0 15.0 %copy-start.38 = (f32[1536]{0:T(1024)S(1)}, f32[1536]{0:T(1024)}, u32[]{:S(2)}) copy-start(f32[1536]{0:T(1024)} %copy-done.37) | copy-start | bytes 18436
  401.0 15.0 %copy-start.50 = (f32[256]{0:T(256)S(1)}, f32[256]{0:T(256)}, u32[]{:S(2)}) copy-start(f32[256]{0:T(256)} %copy-done.49) | copy-start | bytes 3076
  409.5 8.5 %collective-permute-start.20 = (bf16[24,3840]{1,0:T(8,128)(2,1)S(1)}, bf16[24,3840]{1,0:T(8,128)(2,1)S(1)}, u32[]{:S(2)}, u32[]{:S(2)}) collective-permute-start(bf16[24,3840]{1,0:T(8,128)(2,1)S(1)} %get-tuple-element.218), channel_id=1, source_target_pairs={{0,0},{16,1},{1,16},{17,17},{32,32},{48,33},{33,48},{49,49},{2,2},... | collective-permute-start | bytes 552968 | tf_op jit(solution)/shard_map/ppermute | solution.py:88
  410.2 11.0 %collective-permute-start.21 = (bf16[24,3840]{1,0:T(8,128)(2,1)S(1)}, bf16[24,3840]{1,0:T(8,128)(2,1)S(1)}, u32[]{:S(2)}, u32[]{:S(2)}) collective-permute-start(bf16[24,3840]{1,0:T(8,128)(2,1)S(1)} %get-tuple-element.221), channel_id=1, source_target_pairs={{1,0},{17,1},{0,16},{16,17},{33,32},{49,33},{32,48},{48,49},{3,2},... | collective-permute-start | bytes 552968 | tf_op jit(solution)/shard_map/ppermute | solution.py:88
  415.2 13.5 %collective-permute-start.22 = (bf16[24,3840]{1,0:T(8,128)(2,1)S(1)}, bf16[24,3840]{1,0:T(8,128)(2,1)S(1)}, u32[]{:S(2)}, u32[]{:S(2)}) collective-permute-start(bf16[24,3840]{1,0:T(8,128)(2,1)S(1)} %get-tuple-element.220), channel_id=1, source_target_pairs={{32,0},{48,1},{33,16},{49,17},{0,32},{16,33},{1,48},{17,49},{34,2}... | collective-permute-start | bytes 552968 | tf_op jit(solution)/shard_map/ppermute | solution.py:88
  415.4 22.0 %copy-start.18 = (f32[256,1536]{1,0:T(8,128)S(1)}, f32[256,1536]{1,0:T(8,128)}, u32[]{:S(2)}) copy-start(f32[256,1536]{1,0:T(8,128)} %convert_add_fusion.4) | copy-start | bytes 4718596
  415.4 22.0 %copy-start.59 = (f32[256,1536]{1,0:T(8,128)S(1)}, f32[256,1536]{1,0:T(8,128)}, u32[]{:S(2)}) copy-start(f32[256,1536]{1,0:T(8,128)} %get-tuple-element.97) | copy-start | bytes 4718596
  415.4 20.8 %collective-permute-start.23 = (bf16[24,3840]{1,0:T(8,128)(2,1)S(1)}, bf16[24,3840]{1,0:T(8,128)(2,1)S(1)}, u32[]{:S(2)}, u32[]{:S(2)}) collective-permute-start(bf16[24,3840]{1,0:T(8,128)(2,1)S(1)} %get-tuple-element.219), channel_id=1, source_target_pairs={{33,0},{49,1},{32,16},{48,17},{1,32},{17,33},{0,48},{16,49},{35,2}... | collective-permute-start | bytes 552968 | tf_op jit(solution)/shard_map/ppermute | solution.py:88
  436.4 3.8 collective-permute-start.24
  449.0 30.0 %collective-permute-start.25 = (bf16[24,1664]{1,0:T(8,128)(2,1)S(1)}, bf16[24,1664]{1,0:T(8,128)(2,1)S(1)}, u32[]{:S(2)}, u32[]{:S(2)}) collective-permute-start(bf16[24,1664]{1,0:T(8,128)(2,1)S(1)} %get-tuple-element.230), channel_id=1, source_target_pairs={{0,0},{16,1},{1,16},{17,17},{32,32},{48,33},{33,48},{49,49},{2,2},... | collective-permute-start | bytes 239624 | tf_op jit(solution)/shard_map/ppermute | solution.py:88
  449.6 29.3 %collective-permute-start.26 = (bf16[24,1664]{1,0:T(8,128)(2,1)S(1)}, bf16[24,1664]{1,0:T(8,128)(2,1)S(1)}, u32[]{:S(2)}, u32[]{:S(2)}) collective-permute-start(bf16[24,1664]{1,0:T(8,128)(2,1)S(1)} %get-tuple-element.231), channel_id=1, source_target_pairs={{1,0},{17,1},{0,16},{16,17},{33,32},{49,33},{32,48},{48,49},{3,2},... | collective-permute-start | bytes 239624 | tf_op jit(solution)/shard_map/ppermute | solution.py:88
  454.4 24.6 %collective-permute-start.27 = (bf16[24,1664]{1,0:T(8,128)(2,1)S(1)}, bf16[24,1664]{1,0:T(8,128)(2,1)S(1)}, u32[]{:S(2)}, u32[]{:S(2)}) collective-permute-start(bf16[24,1664]{1,0:T(8,128)(2,1)S(1)} %get-tuple-element.233), channel_id=1, source_target_pairs={{32,0},{48,1},{33,16},{49,17},{0,32},{16,33},{1,48},{17,49},{34,2}... | collective-permute-start | bytes 239624 | tf_op jit(solution)/shard_map/ppermute | solution.py:88
  457.3 21.7 %collective-permute-start.28 = (bf16[24,1664]{1,0:T(8,128)(2,1)S(1)}, bf16[24,1664]{1,0:T(8,128)(2,1)S(1)}, u32[]{:S(2)}, u32[]{:S(2)}) collective-permute-start(bf16[24,1664]{1,0:T(8,128)(2,1)S(1)} %get-tuple-element.232), channel_id=1, source_target_pairs={{33,0},{49,1},{32,16},{48,17},{1,32},{17,33},{0,48},{16,49},{35,2}... | collective-permute-start | bytes 239624 | tf_op jit(solution)/shard_map/ppermute | solution.py:88
  460.2 45.3 %all-to-all-start.6 = ((bf16[128,24,128]{2,1,0:T(8,128)(2,1)}), bf16[128,24,128]{2,1,0:T(8,128)(2,1)S(1)}, u32[]{:S(2)}, u32[]{:S(2)}) async-start(bf16[128,24,128]{2,1,0:T(8,128)(2,1)} %copy.526), calls=%async_computation.7 | async-start | bytes 1572864 | tf_op jit(solution)/shard_map/all_to_all | solution.py:653
  479.1 5.0 collective-permute-start.31
  484.1 1.2 collective-permute-start.29
  485.3 8.4 %collective-permute-start.30 = (f32[24,640]{1,0:T(8,128)S(1)}, f32[24,640]{1,0:T(8,128)S(1)}, u32[]{:S(2)}, u32[]{:S(2)}) collective-permute-start(f32[24,640]{1,0:T(8,128)S(1)} %slice_add_fusion.1), channel_id=1, source_target_pairs={{0,1},{1,0},{2,3},{3,2},{4,5},{5,4},{6,7},{7,6},{8,9},{9,8},{10,11... | collective-permute-start | bytes 184328 | tf_op jit(solution)/shard_map/ppermute | solution.py:32
  (41 other events, 191.6 us)
Sparse Core Ops, SparseCore 0:
  74.7 55.7 all-gather.2
  133.6 90.7 all-gather.4
  289.8 102.7 reduce-scatter.1
